TPU v7x, 32 devices: a whole 2x2x4 slice. The times are simulated.
32 devices in a mesh: rows: 16 (over z, x, core), items: 2 (over y).
Axes of the slice: x: 2, y: 2, z: 4, core: 2. Of those that a mesh axis runs over, the one named last changes fastest.
Arguments:
- frames: float32 [4, 4, 64, 64, 512], P('items', None, 'rows'), may hold values from -6 to 6
- counts: int32 [4], P('items'), may hold values from 1 to 4
- time_weight: float32 [4, 512], replicated, may hold values from 0.5 to 2
- first_gain: float32 [512], replicated, may hold values from 0.5 to 1.5
- first_shift: float32 [512], replicated, may hold values from -4 to 4
- mixing_weight: float32 [2048, 64], P(('rows', 'items')), may hold values from -0.5 to 0.5
- mixing_bias: float32 [4, 512], replicated, may hold values from -4 to 4
- second_gain: float32 [512], replicated, may hold values from 0.5 to 1.5
- second_shift: float32 [512], replicated, may hold values from -4 to 4
- expand_weight: float32 [512, 2048], P(None, ('rows', 'items')), may hold values from -0.25 to 0.25
- expand_bias: float32 [2048], replicated, may hold values from -4 to 4
- contract_weight: float32 [2048, 512], P(('rows', 'items')), may hold values from -0.125 to 0.125
- contract_bias: float32 [512], replicated, may hold values from -4 to 4
- output_cotangent: float32 [4, 64, 64, 512], P('items', 'rows'), may hold values from -6 to 6
Outputs:
- block_out: float32 [4, 64, 64, 512], P('items', 'rows')
- frames_grad: float32 [4, 4, 64, 64, 512], P('items', None, 'rows')
- time_weight_grad: float32 [4, 512], replicated
- first_gain_grad: float32 [512], replicated
- first_shift_grad: float32 [512], replicated
- mixing_weight_grad: float32 [2048, 64], P(('rows', 'items'))
- mixing_bias_grad: float32 [4, 512], replicated
- second_gain_grad: float32 [512], replicated
- second_shift_grad: float32 [512], replicated
- expand_weight_grad: float32 [512, 2048], P(None, ('rows', 'items'))
- expand_bias_grad: float32 [2048], replicated
- contract_weight_grad: float32 [2048, 512], P(('rows', 'items'))
- contract_bias_grad: float32 [512], replicated
Inputs may be any that keep to these rules, and one draw needn't show every extreme that they name: counts[i] frames of item i count; the later frames are masked out.
All inputs are finite; a program needn't handle non-finite values.
Results may differ from a plain program's by a relative error of at most 0.0035.
Values sent between devices are 32-bit elements; how exact they have to be, the bound alone decides.
No kernel may reach another device: no remote copies, remote signals or barrier semaphores. Data moves between devices by JAX's collectives and lax.ppermute only.
A program may use at most 128 MiB of HBM per device.

v0:
```python
import math

import jax
import jax.numpy as jnp
from jax import lax
from jax.sharding import PartitionSpec as P

BLOCKS = 8
MODES = 32
HG = 64


HIGHEST = lax.Precision.HIGHEST
shrink_level = 0.01
norm_eps = 1e-05


def tables():
    grid_index = jnp.arange(HG, dtype=jnp.int32)
    along_index = jnp.arange(MODES, dtype=jnp.int32)
    across_index = jnp.concatenate(
        [jnp.arange(MODES // 2, dtype=jnp.int32), jnp.arange(HG - MODES // 2, HG, dtype=jnp.int32)]
    )
    step_angle = 2.0 * math.pi / HG
    factor = 1.0 / math.sqrt(HG)
    width_angle = (along_index[:, None] * grid_index[None, :] % HG).astype(jnp.float32) * step_angle
    height_angle = (across_index[:, None] * grid_index[None, :] % HG).astype(
        jnp.float32
    ) * step_angle
    cos_width = jnp.cos(width_angle) * factor
    sin_width = jnp.sin(width_angle) * factor
    cos_height = jnp.cos(height_angle) * factor
    sin_height = jnp.sin(height_angle) * factor
    doubled = jnp.where(along_index == 0, 1.0, 2.0).astype(jnp.float32)[:, None]
    return (cos_width, sin_width, cos_height, sin_height, cos_width * doubled, sin_width * doubled)


def layer_norm(values, norm_gain, norm_shift):
    average = jnp.mean(values, axis=-1, keepdims=True)
    centred = values - average
    spread = jnp.mean(centred * centred, axis=-1, keepdims=True)
    return centred * lax.rsqrt(spread + norm_eps) * norm_gain + norm_shift


def gelu_exact(values):
    return jax.nn.gelu(values, approximate=False)


def shrink(values):
    return values - jnp.clip(values, -shrink_level, shrink_level)


def merge_frames(frames, time_weight, counts):
    frame_total = frames.shape[1]
    live = (jnp.arange(frame_total, dtype=jnp.int32)[None, :] < counts[:, None]).astype(jnp.float32)
    live = live / counts[:, None].astype(jnp.float32)
    factor = live[:, :, None] * time_weight[None, :, :]
    return jnp.sum(frames * factor[:, :, None, None, :], axis=1)


def head(merged, norm_gain, norm_shift, cos_width, sin_width):
    normed = layer_norm(merged, norm_gain, norm_shift)
    part_real = jnp.einsum("kw,ihwc->ihkc", cos_width, normed, precision=HIGHEST)
    part_imag = -jnp.einsum("kw,ihwc->ihkc", sin_width, normed, precision=HIGHEST)
    lead_items, lead_rows, kept_modes, channel_total = part_real.shape
    block_size = channel_total // BLOCKS
    split_shape = (lead_items, lead_rows, kept_modes, BLOCKS, block_size)
    stacked = jnp.stack([part_real.reshape(split_shape), part_imag.reshape(split_shape)], axis=4)
    return stacked.reshape(lead_items, lead_rows, kept_modes * BLOCKS, 2 * block_size)


def column_modes(parts, cos_height, sin_height):
    block_size = parts.shape[3] // 2
    turned = jnp.concatenate([parts[..., block_size:], -parts[..., :block_size]], axis=3)
    return jnp.einsum("qh,ihpc->iqpc", cos_height, parts, precision=HIGHEST) + jnp.einsum(
        "qh,ihpc->iqpc", sin_height, turned, precision=HIGHEST
    )


def mix_modes(stacked, weight_whole, bias_whole, block_pick):
    block_total = block_pick.shape[1]
    block_size = weight_whole.shape[1]
    weight_table = weight_whole.reshape(2, block_total, 2, block_size, block_size)
    bias_table = bias_whole.reshape(2, 2, block_total, block_size)
    current = stacked
    for layer_index in range(2):
        weight_real = weight_table[layer_index, :, 0]
        weight_imag = weight_table[layer_index, :, 1]
        upper = jnp.concatenate([weight_real, weight_imag], axis=2)
        lower = jnp.concatenate([-weight_imag, weight_real], axis=2)
        combined = jnp.concatenate([upper, lower], axis=1)
        chosen = jnp.einsum("pb,bio->pio", block_pick, combined, precision=HIGHEST)
        offset = jnp.concatenate([bias_table[layer_index, 0], bias_table[layer_index, 1]], axis=1)
        chosen_bias = jnp.dot(block_pick, offset, precision=HIGHEST)
        current = (
            jnp.einsum("iqpc,pco->iqpo", current, chosen, precision=HIGHEST)
            + chosen_bias[None, None]
        )
        if layer_index == 0:
            current = gelu_exact(current)
        else:
            current = shrink(current)
    return current


def inverse_columns(mixed, cos_height, sin_height):
    block_size = mixed.shape[3] // 2
    turned = jnp.concatenate([-mixed[..., block_size:], mixed[..., :block_size]], axis=3)
    return jnp.einsum("qh,iqpc->ihpc", cos_height, mixed, precision=HIGHEST) + jnp.einsum(
        "qh,iqpc->ihpc", sin_height, turned, precision=HIGHEST
    )


def to_spatial(parts, cos_wide, sin_wide):
    lead_items, lead_rows, pair_total, doubled_size = parts.shape
    kept_modes = cos_wide.shape[0]
    block_total = pair_total // kept_modes
    block_size = doubled_size // 2
    split_parts = parts.reshape(lead_items, lead_rows, kept_modes, block_total, 2, block_size)
    channel_total = block_total * block_size
    back_real = split_parts[:, :, :, :, 0, :].reshape(
        lead_items, lead_rows, kept_modes, channel_total
    )
    back_imag = split_parts[:, :, :, :, 1, :].reshape(
        lead_items, lead_rows, kept_modes, channel_total
    )
    return jnp.einsum("kw,ihkc->ihwc", cos_wide, back_real, precision=HIGHEST) - jnp.einsum(
        "kw,ihkc->ihwc", sin_wide, back_imag, precision=HIGHEST
    )


def tail(middle, norm_gain, norm_shift, expand_in, expand_bias_in, contract_in, contract_bias_in):
    normed_two = layer_norm(middle, norm_gain, norm_shift)
    hidden = gelu_exact(
        jnp.einsum("ihwc,cf->ihwf", normed_two, expand_in, precision=HIGHEST) + expand_bias_in
    )
    return (
        middle
        + jnp.einsum("ihwf,fc->ihwc", hidden, contract_in, precision=HIGHEST)
        + contract_bias_in
    )


def local(
    frames,
    counts,
    time_weight,
    first_gain,
    first_shift,
    mixing_weight,
    mixing_bias,
    second_gain,
    second_shift,
    expand_weight,
    expand_bias,
    contract_weight,
    contract_bias,
    output_cotangent,
):
    cos_width, sin_width, cos_height, sin_height, cos_wide, sin_wide = tables()
    expand_whole, contract_whole, mixing_whole = (
        lax.all_gather(expand_weight, ("rows", "items"), axis=1, tiled=True),
        lax.all_gather(contract_weight, ("rows", "items"), axis=0, tiled=True),
        lax.all_gather(mixing_weight, ("rows", "items"), axis=0, tiled=True),
    )
    pair_count = MODES * BLOCKS // lax.axis_size("rows")
    pair_index = lax.axis_index("rows") * pair_count + jnp.arange(pair_count, dtype=jnp.int32)
    block_pick = (
        pair_index[:, None] % BLOCKS == jnp.arange(BLOCKS, dtype=jnp.int32)[None, :]
    ).astype(jnp.float32)

    def merge_fn(frames_in, weight_in):
        return merge_frames(frames_in, weight_in, counts)

    def head_fn(merged_in, gain_in, shift_in):
        return head(merged_in, gain_in, shift_in, cos_width, sin_width)

    def columns_fn(parts_in):
        return column_modes(parts_in, cos_height, sin_height)

    def mix_fn(modes_in, weight_in, bias_in):
        return mix_modes(modes_in, weight_in, bias_in, block_pick)

    def inverse_fn(mixed_in):
        return inverse_columns(mixed_in, cos_height, sin_height)

    def spatial_fn(parts_in):
        return to_spatial(parts_in, cos_wide, sin_wide)

    merged, merge_back = jax.vjp(merge_fn, frames, time_weight)
    rows_modes, head_back = jax.vjp(head_fn, merged, first_gain, first_shift)
    column_parts = lax.all_to_all(rows_modes, "rows", split_axis=2, concat_axis=1, tiled=True)
    kept_spectrum, columns_back = jax.vjp(columns_fn, column_parts)
    mixed = mix_fn(kept_spectrum, mixing_whole, mixing_bias)
    column_back, inverse_back = jax.vjp(inverse_fn, mixed)
    row_back = lax.all_to_all(column_back, "rows", split_axis=1, concat_axis=2, tiled=True)
    spatial, spatial_back = jax.vjp(spatial_fn, row_back)
    middle = merged + spatial
    block_out = tail(
        middle, second_gain, second_shift, expand_whole, expand_bias, contract_whole, contract_bias
    )
    expand_again, contract_again = (
        lax.all_gather(expand_weight, ("rows", "items"), axis=1, tiled=True),
        lax.all_gather(contract_weight, ("rows", "items"), axis=0, tiled=True),
    )
    ignored_out, tail_back = jax.vjp(
        tail,
        middle,
        second_gain,
        second_shift,
        expand_again,
        expand_bias,
        contract_again,
        contract_bias,
    )
    (
        grad_middle_tail,
        grad_second_gain,
        grad_second_shift,
        grad_expand,
        grad_expand_bias,
        grad_contract,
        grad_contract_bias,
    ) = tail_back(output_cotangent)
    (grad_row_back,) = spatial_back(grad_middle_tail)
    grad_column_back = lax.all_to_all(
        grad_row_back, "rows", split_axis=2, concat_axis=1, tiled=True
    )
    (grad_mixed,) = inverse_back(grad_column_back)
    again_parts = lax.all_to_all(
        head_fn(merged, first_gain, first_shift), "rows", split_axis=2, concat_axis=1, tiled=True
    )
    spectrum_again = columns_fn(again_parts)
    ignored_mixed, mix_back = jax.vjp(mix_fn, spectrum_again, mixing_whole, mixing_bias)
    grad_spectrum, grad_mixing, grad_mixing_bias = mix_back(grad_mixed)
    (grad_column_parts,) = columns_back(grad_spectrum)
    grad_rows_modes = lax.all_to_all(
        grad_column_parts, "rows", split_axis=1, concat_axis=2, tiled=True
    )
    grad_merged_head, grad_first_gain, grad_first_shift = head_back(grad_rows_modes)
    grad_merged = grad_middle_tail + grad_merged_head
    grad_frames, grad_time = merge_back(grad_merged)
    expand_share, contract_share, mixing_share = (
        lax.psum_scatter(grad_expand, ("rows", "items"), scatter_dimension=1, tiled=True),
        lax.psum_scatter(grad_contract, ("rows", "items"), scatter_dimension=0, tiled=True),
        lax.psum_scatter(grad_mixing, ("rows", "items"), scatter_dimension=0, tiled=True),
    )
    summed = lax.psum(
        (
            grad_time,
            grad_first_gain,
            grad_first_shift,
            grad_mixing_bias,
            grad_second_gain,
            grad_second_shift,
            grad_expand_bias,
            grad_contract_bias,
        ),
        ("rows", "items"),
    )
    return (
        block_out,
        grad_frames,
        summed[0],
        summed[1],
        summed[2],
        mixing_share,
        summed[3],
        summed[4],
        summed[5],
        expand_share,
        summed[6],
        contract_share,
        summed[7],
    )


def solution(mesh):
    return jax.shard_map(
        local,
        mesh=mesh,
        in_specs=(
            P("items", None, "rows", None, None),
            P("items"),
            P(),
            P(),
            P(),
            P(("rows", "items"), None),
            P(),
            P(),
            P(),
            P(None, ("rows", "items")),
            P(),
            P(("rows", "items"), None),
            P(),
            P("items", "rows", None, None),
        ),
        out_specs=(
            P("items", "rows", None, None),
            P("items", None, "rows", None, None),
            P(),
            P(),
            P(),
            P(("rows", "items"), None),
            P(),
            P(),
            P(),
            P(None, ("rows", "items")),
            P(),
            P(("rows", "items"), None),
            P(),
        ),
        check_vma=False,
    )
```

profile of v0, /device:TPU:0, one launch (start us, length us, event | category | flops | bytes accessed | tf_op | source)
XLA Modules:
  0.0 716.6 jit_solution(74583177915918108)
XLA Ops:
  17.4 3.6 pad_maximum_fusion
  25.3 7.4 %all-to-all-start = ((f32[2,4,256,128]{3,1,0,2:T(4,128)}), f32[2,4,256,128]{3,1,0,2:T(4,128)S(1)}, u32[]{:S(2)}, u32[]{:S(2)}) async-start(f32[2,4,256,128]{3,1,0,2:T(4,128)} %copy.71), calls=%async_computation | async-start | bytes 2097152 | tf_op jit(solution)/shard_map/all_to_all | solution.py:192
  34.0 92.6 %all_gather.11 = f32[2048,64]{1,0:T(8,128)S(1)} all-gather(f32[64,64]{1,0:T(8,128)S(1)} %copy-done.24), channel_id=1, replica_groups=mesh['rows'=16,'items'=2] {'rows','items'}, dimensions={0}, use_global_device_ids=true | all-gather | bytes 540672 | tf_op jit(solution)/shard_map/all_gather | solution.py:164
  142.3 4.1 all-to-all-start.1
  146.5 22.8 %all-to-all-done.1 = f32[2,64,16,128]{3,2,0,1:T(8,128)S(1)} async-done(((f32[2,64,16,128]{3,2,0,1:T(8,128)}), f32[2,64,16,128]{3,2,0,1:T(8,128)S(1)}, u32[]{:S(2)}, u32[]{:S(2)}) %all-to-all-start.1) | async-done | bytes 1048608 | tf_op jit(solution)/shard_map/all_to_all | solution.py:196
  171.9 8.1 %slice_reduce_fusion.1 = (f32[2,4,32,8,64]{4,3,2,1,0:T(8,128)S(1)}, f32[2,4,32,8,64]{4,3,2,1,0:T(8,128)S(1)}) fusion(f32[2,4,32,8,2,64]{5,4,3,2,1,0:T(2,128)} %reshape.227), kind=kLoop, calls=%fused_computation.69 | loop fusion | bytes 2097152 | tf_op jit(solution)/shard_map/jvp()/slice | solution.py:124
  185.4 10.1 %fusion.51 = (u8[2,64,2048]{2,1,0:T(8,128)(4,1)S(1)}, u8[2,64,2048]{2,1,0:T(8,128)(4,1)S(1)}, f32[2,4,64,2048]{3,2,1,0:T(8,128)S(1)}) fusion(f32[2048]{0:T(1024)S(1)} %copy-done.21, f32[512,2048]{0,1:T(8,128)} %all-gather.3.cloned.1.call-done, f32[2,4,64,512]{3,2,1,0:T(8,128)S(1)} %get-tuple-element.93, f32[512]{0:T(512)S(1)} %copy-done.23, ...), kind=kOutput, calls=%fused_computation.105 | convolution fusion | flops 6457655296 | bytes 9977856 | tf_op jit(solution)/shard_map/ihwc,cf->ihwf/dot_general | solution.py:135
  197.5 10.3 %fusion = f32[2,4,64,2048]{3,2,1,0:T(8,128)} fusion(f32[2,4,64,2048]{3,2,1,0:T(8,128)S(1)} %get-tuple-element.94, f32[2048]{0:T(1024)S(1)} %copy-done.21, u8[2,64,2048]{2,1,0:T(8,128)(4,1)S(1)} %get-tuple-element.42, u8[2,64,2048]{2,1,0:T(8,128)(4,1)S(1)} %get-tuple-element.41), kind=kLoop, calls=%fused_computation.1 | loop fusion | flops 71303168 | bytes 8921088 | tf_op jit(solution)/shard_map/erfc | solution.py:46
  207.8 11.5 %fusion.331 = (f32[2048]{0:T(1024)S(1)}, f32[2,4,64,2048]{3,2,1,0:T(8,128)S(1)}) fusion(f32[2,4,64,2048]{3,2,1,0:T(8,128)} %fusion, f32[2,4,64,512]{3,2,1,0:T(8,128)S(1)} %copy-done.17, f32[2048,512]{1,0:T(8,128)} %all-gather.5.cloned.1.call-done, f32[2,4,64,2048]{3,2,1,0:T(8,128)} %copy-done, f32[2048]{0:T(1024)S(1)} %copy-done.21), kind=kOutput, calls=%fused_computation.437 | convolution fusion | flops 6458177536 | bytes 17842176 | tf_op jit(solution)/shard_map/transpose(jvp(ihwf,fc->ihwc))/dot_general | solution.py:139
  219.3 7.0 fusion.324
  234.9 5.1 pad_add_fusion
  245.2 31.5 %all_to_all.71 = f32[2,4,256,128]{3,1,0,2:T(4,128)S(1)} all-to-all(f32[2,4,256,128]{3,1,0,2:T(4,128)S(1)} %copy.83), channel_id=1, replica_groups=mesh['rows'=16,'items'=2] {'rows'}, dimensions={2} | all-to-all | bytes 2097152 | tf_op jit(solution)/shard_map/all_to_all | solution.py:226
  283.1 3.9 fusion.60
  291.7 11.0 %convolution_bitcast_fusion = f32[2048,512]{1,0:T(8,128)} fusion(f32[2,4,64,512]{3,2,1,0:T(8,128)} %param.27, f32[2,4,64,2048]{3,2,1,0:T(8,128)} %fusion, f32[2,4,64,2048]{3,2,1,0:T(8,128)} %copy-done, f32[2048]{0:T(1024)S(1)} %copy-done.21), kind=kOutput, calls=%fused_computation.32 | convolution fusion | flops 6445596672 | bytes 13639680 | tf_op jit(solution)/shard_map/transpose(jvp(ihwf,fc->ihwc))/dot_general | solution.py:139
  302.7 10.6 %convolution_bitcast_fusion.1 = f32[512,2048]{0,1:T(8,128)} fusion(f32[2,4,64,2048]{3,2,1,0:T(8,128)} %copy-done.2, f32[2,4,64,512]{3,2,1,0:T(8,128)S(1)} %get-tuple-element.93, f32[512]{0:T(512)S(1)} %copy-done.23, f32[512]{0:T(512)S(1)} %copy-done.20, f32[2,4,64]{2,1,0:T(4,128)S(1)} %fusion.227, f32[2,4,64]{2,1,0:T(4,128)S(1)} %broadcast_multiply_fusion.2), kind=kOutput, calls=%fused_computation.33 | convolution fusion | flops 6443499520 | bytes 9445376 | tf_op jit(solution)/shard_map/transpose(jvp(ihwc,cf->ihwf))/dot_general | solution.py:135
  313.4 3.6 convolution_bitcast_fusion.6
  321.6 5.3 all-to-all-start.3
  326.9 12.6 %fusion.24 = f32[2,4,64,512]{3,2,1,0:T(8,128)} fusion(f32[2,4,64,512]{3,2,1,0:T(8,128)S(1)} %get-tuple-element.93, f32[2048,512]{1,0:T(8,128)} %all-gather.5.cloned.1.call-done, f32[2,4,64,2048]{3,2,1,0:T(8,128)} %fusion, f32[2,4,64,2048]{3,2,1,0:T(8,128)} %copy-done, f32[2048]{0:T(1024)S(1)} %copy-done.21, f32[512]{0:T(512)S(1)} %copy-done.26), kind=kOutput, calls=%fused_computation.52 | convolution fusion | flops 6446120960 | bytes 14690304 | tf_op jit(solution)/shard_map/ihwf,fc->ihwc/dot_general | solution.py:139
  340.3 9.6 %all-to-all-done.3 = f32[2,64,16,128]{3,2,0,1:T(8,128)} async-done(((f32[2,64,16,128]{3,2,0,1:T(8,128)}), f32[2,64,16,128]{3,2,0,1:T(8,128)}, u32[]{:S(2)}, u32[]{:S(2)}) %all-to-all-start.3) | async-done | bytes 1048608 | tf_op jit(solution)/shard_map/all_to_all | solution.py:237
  353.7 9.6 %slice_reduce_fusion = (f32[2,4,32,8,64]{4,3,2,1,0:T(8,128)}, f32[2,4,32,8,64]{4,3,2,1,0:T(8,128)S(1)}) fusion(f32[2,4,32,8,2,64]{5,4,3,2,1,0:T(2,128)} %reshape.231), kind=kLoop, calls=%fused_computation.65 | loop fusion | flops 131072 | bytes 2097152 | tf_op jit(solution)/shard_map/transpose(jvp())/unstack | solution.py:68
  376.6 44.6 %all-reduce.14 = (f32[4,512]{1,0:T(4,128)}, f32[512]{0:T(512)}, f32[512]{0:T(512)}, f32[4,512]{1,0:T(4,128)}, f32[512]{0:T(512)}, /*index=5*/f32[512]{0:T(512)}, f32[2048]{0:T(1024)}, f32[512]{0:T(512)}) all-reduce(f32[4,512]{1,0:T(4,128)S(1)} %multiply_reduce_fusion.8, ...), channel_id=1, replica_groups=mesh['rows'=16,'items'=2] {'rows','items'}, use_global_device_ids=true, to_apply=%region_11.12 | all-reduce | flops 8704 | bytes 69632 | tf_op jit(solution)/shard_map/psum | solution.py:248
  421.2 7.1 reduce-scatter.10.cloned.1.call-done
  428.3 140.3 %reduce-scatter.8.cloned.1.call-done = f32[64,512]{1,0:T(8,128)} async-done(((f32[2048,512]{1,0:T(8,128)}), f32[64,512]{1,0:T(8,128)}) %reduce-scatter.8.cloned.1.call-update) | async-done | bytes 131088 | tf_op jit(solution)/shard_map/reduce_scatter | solution.py:245
  568.6 141.2 %reduce-scatter.6.cloned.1.call-done = f32[512,64]{0,1:T(8,128)} async-done(((f32[512,2048]{0,1:T(8,128)}), f32[512,64]{0,1:T(8,128)}) %reduce-scatter.6.cloned.1.call-update) | async-done | bytes 131088 | tf_op jit(solution)/shard_map/reduce_scatter | solution.py:244
  (166 shorter events, 88.3 us)
Async XLA Ops:
  7.2 6.0 copy-start.22
  7.2 6.0 copy-start.25
  7.2 178.2 %all-gather.3.cloned.1.call-start = ((), (), s32[]{:S(2)}) async-start(), calls=%async_computation.7 | async-start | bytes 4325376 | tf_op jit(solution)/shard_map/all_gather | solution.py:162
  21.0 12.4 %copy-start.27 = (f32[4,512]{1,0:T(4,128)S(1)}, f32[4,512]{1,0:T(4,128)}, u32[]{:S(2)}) copy-start(f32[4,512]{1,0:T(4,128)} %param.20) | copy-start | bytes 24580
  21.0 13.0 %copy-start.24 = (f32[64,64]{1,0:T(8,128)S(1)}, f32[64,64]{1,0:T(8,128)}, u32[]{:S(2)}) copy-start(f32[64,64]{1,0:T(8,128)} %param.19) | copy-start | bytes 49156
  25.3 104.8 %all-to-all-start = ((f32[2,4,256,128]{3,1,0,2:T(4,128)}), f32[2,4,256,128]{3,1,0,2:T(4,128)S(1)}, u32[]{:S(2)}, u32[]{:S(2)}) async-start(f32[2,4,256,128]{3,1,0,2:T(4,128)} %copy.71), calls=%async_computation | async-start | bytes 2097152 | tf_op jit(solution)/shard_map/all_to_all | solution.py:192
  32.7 175.1 %all-gather.5.cloned.1.call-start = ((), (), s32[]{:S(2)}) async-start(), calls=%async_computation.8 | async-start | bytes 4325376 | tf_op jit(solution)/shard_map/all_gather | solution.py:163
  131.4 5.3 copy-start.11
  142.3 27.0 %all-to-all-start.1 = ((f32[2,64,16,128]{3,2,0,1:T(8,128)}), f32[2,64,16,128]{3,2,0,1:T(8,128)S(1)}, u32[]{:S(2)}, u32[]{:S(2)}) async-start(f32[2,64,16,128]{3,2,0,1:T(8,128)} %copy.79), calls=%async_computation.1 | async-start | bytes 2097152 | tf_op jit(solution)/shard_map/all_to_all | solution.py:196
  146.4 281.9 %reduce-scatter.10.cloned.1.call-start = ((), (), s32[]{:S(2)}) async-start(), calls=%async_computation.11 | async-start | bytes 1081344
  197.5 10.3 %copy-start.17 = (f32[2,4,64,512]{3,2,1,0:T(8,128)S(1)}, f32[2,4,64,512]{3,2,1,0:T(8,128)}, u32[]{:S(2)}) copy-start(f32[2,4,64,512]{3,2,1,0:T(8,128)} %param.27) | copy-start | bytes 3145732
  207.7 11.5 %copy-start.10 = (f32[512,2048]{0,1:T(8,128)S(1)}, f32[512,2048]{0,1:T(8,128)}, u32[]{:S(2)}) copy-start(f32[512,2048]{0,1:T(8,128)} %all-gather.3.cloned.1.call-done) | copy-start | bytes 12582916
  219.2 7.1 copy-start.2
  219.2 7.6 %copy-start.18 = (f32[2,4,64,512]{3,2,1,0:T(8,128)S(1)}, f32[2,4,64,512]{3,2,1,0:T(8,128)}, u32[]{:S(2)}) copy-start(f32[2,4,64,512]{3,2,1,0:T(8,128)} %param.27) | copy-start | bytes 3145732
  278.7 4.3 copy-start.12
  278.7 4.3 copy-start.14
  287.0 4.6 copy-start.16
  291.6 277.0 %reduce-scatter.8.cloned.1.call-start = ((), (), s32[]{:S(2)}) async-start(), calls=%async_computation.10 | async-start | bytes 4325376 | tf_op jit(solution)/shard_map/reduce_scatter | solution.py:245
  302.7 407.1 %reduce-scatter.6.cloned.1.call-start = ((), (), s32[]{:S(2)}) async-start(), calls=%async_computation.9 | async-start | bytes 4325376 | tf_op jit(solution)/shard_map/reduce_scatter | solution.py:244
  318.6 8.3 %copy-start.26 = (f32[512]{0:T(512)S(1)}, f32[512]{0:T(512)}, u32[]{:S(2)}) copy-start(f32[512]{0:T(512)} %param.26) | copy-start | bytes 6148
  321.6 28.3 %all-to-all-start.3 = ((f32[2,64,16,128]{3,2,0,1:T(8,128)}), f32[2,64,16,128]{3,2,0,1:T(8,128)}, u32[]{:S(2)}, u32[]{:S(2)}) async-start(f32[2,64,16,128]{3,2,0,1:T(8,128)} %copy.92), calls=%async_computation.3 | async-start | bytes 2097152 | tf_op jit(solution)/shard_map/all_to_all | solution.py:237
  326.9 12.7 %copy-start.13 = (f32[2,32,16,128]{3,1,0,2:T(8,128)S(1)}, f32[2,32,16,128]{3,1,0,2:T(8,128)}, u32[]{:S(2)}) copy-start(f32[2,32,16,128]{3,1,0,2:T(8,128)} %get-tuple-element.73) | copy-start | bytes 1572868
  326.9 12.6 %copy-start.15 = (f32[16,128,64]{1,2,0:S(1)}, f32[16,128,64]{1,2,0}, u32[]{:S(2)}) copy-start(f32[16,128,64]{1,2,0} %get-tuple-element.91) | copy-start | bytes 1572868
  326.9 12.6 %copy-start.19 = (f32[16,2,32,128]{3,2,1,0:T(8,128)S(1)}, f32[16,2,32,128]{3,2,1,0:T(8,128)}, u32[]{:S(2)}) copy-start(f32[16,2,32,128]{3,2,1,0:T(8,128)} %get-tuple-element.97) | copy-start | bytes 1572868
  (12 other events, 40.9 us)
Sparse Core Ops, SparseCore 0:
  10.9 73.6 all-gather.2
  87.5 61.5 all-gather.4
  291.7 136.4 reduce-scatter.9
  431.1 137.4 reduce-scatter.7
  571.4 138.4 reduce-scatter.5
where the time goes:
time: 724 us; the launch traced here: 717 us
  waiting for transfers between devices  323 us (45%)
  blocking collectives  169 us (23%)
  matrix products  107 us (15%)
  local copies, waits for them, and re-layouts  45.3 us (6%)
  other arithmetic  41.6 us (6%)
  starting transfers between devices  16.9 us (2%)
  between operations  14.8 us (2%)
    reduce_scatter x1, waiting for transfers between devices, local(): lax.psum_scatter(grad_expand, ('rows', 'items'), scatter_dimension=1, til...  141 us
    reduce_scatter x1, waiting for transfers between devices, local(): lax.psum_scatter(grad_contract, ('rows', 'items'), scatter_dimension=0, t...  140 us
    all_gather x1, blocking collectives, local(): lax.all_gather(mixing_weight, ('rows', 'items'), axis=0, tiled=True)  92.6 us
    psum x1, blocking collectives, local(): lax.psum((grad_time, grad_first_gain, grad_first_shift, grad_mixing_bias,...  44.6 us
    dot_general x3, matrix products, tail(): jnp.einsum('ihwf,fc->ihwc', hidden, contract_in, precision=HIGHEST)  35.1 us
    all_to_all x1, blocking collectives, local(): lax.all_to_all(grad_row_back, 'rows', split_axis=2, concat_axis=1, tiled=...  31.5 us
    dot_general x3, matrix products, tail(): jnp.einsum('ihwc,cf->ihwf', normed_two, expand_in, precision=HIGHEST)  27.8 us
    all_to_all x1, waiting for transfers between devices, local(): lax.all_to_all(column_back, 'rows', split_axis=1, concat_axis=2, tiled=True)  22.8 us
  transfers between devices with their start and end apart: 8, of which 5 were waited for; matrix products, arithmetic and copies ran while one was open for 19% of the time, Pallas kernels for 0%

commit v1 on v0

v1 whole, which is shorter than its diff:
```python
import math

import jax
import jax.numpy as jnp
import numpy as np
from jax import lax
from jax.experimental import pallas as pl
from jax.experimental.pallas import tpu as pltpu
from jax.sharding import PartitionSpec as P

BLOCKS = 8
MODES = 32
PAIRS = BLOCKS // 2
HIGHEST = lax.Precision.HIGHEST
SHRINK = 0.01
EPS = 1e-05
F32 = jnp.float32
BF16 = jnp.bfloat16
AXES = ("rows", "items")
LIMIT = 56 * 1024 * 1024
HALF_ROOT = math.sqrt(0.5)
DENSITY = 1.0 / math.sqrt(2.0 * math.pi)


def make_tables(grid_size, rows_local, row_parts):
    n = np.arange(grid_size)
    along = np.arange(MODES)
    across = np.concatenate(
        [np.arange(MODES // 2), np.arange(grid_size - MODES // 2, grid_size)]
    )
    step = 2.0 * np.pi / grid_size
    factor = 1.0 / np.sqrt(grid_size)
    wide = (along[:, None] * n[None, :] % grid_size) * step
    high = (across[:, None] * n[None, :] % grid_size) * step
    cos_w, sin_w = np.cos(wide) * factor, np.sin(wide) * factor
    cos_h, sin_h = np.cos(high) * factor, np.sin(high) * factor
    doubled = np.where(along == 0, 1.0, 2.0)[:, None]
    eye = np.eye(rows_local)
    forward = np.einsum("pkw,hg->kphgw", np.stack([cos_w, -sin_w]), eye)
    forward = forward.reshape(MODES * 2 * rows_local, rows_local * grid_size)
    inverse = np.einsum("pkw,hg->gwkph", np.stack([cos_w * doubled, -sin_w * doubled]), eye)
    inverse = inverse.reshape(rows_local * grid_size, MODES * 2 * rows_local)
    column = np.stack([np.stack([cos_h, sin_h]), np.stack([-sin_h, cos_h])])
    column = column.reshape(2, 2, MODES, row_parts, rows_local)
    column = column.transpose(0, 2, 3, 1, 4).reshape(2 * MODES, row_parts * 2 * rows_local)
    as32 = lambda x: np.ascontiguousarray(x, dtype=np.float32)
    return (
        as32(forward),
        as32(forward.T),
        as32(inverse),
        as32(inverse.T),
        as32(column),
        as32(column.T),
    )


def dot_full(a, b):
    return jnp.dot(a, b, precision=HIGHEST, preferred_element_type=F32)


def halves(x):
    high = x.astype(BF16)
    return high, (x - high.astype(F32)).astype(BF16)


def dot_pairs(a, b, dims):
    spec = (dims, ((), ()))
    one = lambda x, y: lax.dot_general(x, y, spec, preferred_element_type=F32)
    return one(a[0], b[0]) + (one(a[0], b[1]) + one(a[1], b[0]))


NN = ((1,), (0,))
NT = ((1,), (1,))
TN = ((0,), (0,))


def cdf(v):
    return 0.5 + 0.5 * lax.erf(v * HALF_ROOT)


def density(v):
    return DENSITY * jnp.exp(-0.5 * v * v)


def normalise(v):
    average = jnp.mean(v, axis=-1, keepdims=True)
    centred = v - average
    spread = jnp.mean(centred * centred, axis=-1, keepdims=True)
    scale = lax.rsqrt(spread + EPS)
    return centred * scale, scale


def normal_back(unit, scale, weighted):
    m0 = jnp.mean(weighted, axis=-1, keepdims=True)
    m1 = jnp.mean(weighted * unit, axis=-1, keepdims=True)
    return scale * (weighted - m0 - unit * m1)


def call(body, grid, in_specs, out_specs, out_shape, flops, moved, name, scratch=()):
    return pl.pallas_call(
        body,
        grid=grid,
        in_specs=in_specs,
        out_specs=out_specs,
        out_shape=out_shape,
        scratch_shapes=list(scratch),
        name=name,
        cost_estimate=pl.CostEstimate(
            flops=int(flops), transcendentals=0, bytes_accessed=int(moved)
        ),
        compiler_params=pltpu.CompilerParams(vmem_limit_bytes=LIMIT),
    )


def whole(shape):
    return pl.BlockSpec(shape, lambda *_: (0,) * len(shape))


def build(row_parts, item_parts):
    row_bits = row_parts.bit_length() - 1
    item_bits = item_parts.bit_length() - 1
    device_total = row_parts * item_parts
    lanes = 128

    def flip(x, bit):
        pairs = [(f, f ^ (1 << bit)) for f in range(device_total)]
        return lax.ppermute(x, AXES, pairs)

    core_bit = item_bits
    depth_bits = [item_bits + row_bits - 1, item_bits + row_bits - 2]
    plane_a = [item_bits + b for b in range(row_bits - 3, 0, -1)] + list(range(item_bits))
    plane_b = plane_a[::-1]
    plane_count = len(plane_a)
    all_bits = [core_bit] + plane_a + depth_bits[::-1]
    low_bits = row_bits - 3 + item_bits
    mixing_bits = list(range(low_bits)) + [item_bits + row_bits - 1]

    def gather_stages(x, bits):
        for bit in bits:
            x = jnp.concatenate([x, flip(x, bit)], axis=0)
        return x

    def scatter_stages(x, bits):
        for bit in bits[::-1]:
            half = x.shape[0] // 2
            x = x[:half] + flip(x[half:], bit)
        return x

    def xor_order(x, index):
        for bit in range(x.shape[0].bit_length() - 1):
            lead = x.reshape((-1, 2, 1 << bit) + x.shape[1:])
            swapped = (index >> bit) % 2 == 1
            x = jnp.where(swapped, lead[:, ::-1], lead).reshape(x.shape)
        return x

    def turn_plane(x):
        lead = x.reshape((2,) * plane_count + (-1, x.shape[-1]))
        order = tuple(range(plane_count))[::-1] + (plane_count, plane_count + 1)
        return lead.transpose(order).reshape(x.shape)

    def total(x):
        for bit in all_bits:
            x = x + flip(x, bit)
        return x

    def local(
        frames,
        counts,
        time_weight,
        first_gain,
        first_shift,
        mixing_weight,
        mixing_bias,
        second_gain,
        second_shift,
        expand_weight,
        expand_bias,
        contract_weight,
        contract_bias,
        output_cotangent,
    ):
        items, frame_total, rows_local, width, channels = frames.shape
        grid_size = rows_local * row_parts
        tokens = rows_local * width
        wave_rows = MODES * 2 * rows_local
        groups = row_parts // PAIRS
        kept = MODES // groups
        part = kept * 2 * rows_local
        stack = 2 * rows_local
        mode_rows = kept * MODES
        shard = contract_weight.shape[0]
        hidden_total = expand_bias.shape[0]
        hidden_local = hidden_total // 2
        aligned = stack % 8 == 0
        tables = make_tables(grid_size, rows_local, row_parts)
        wave_fwd, wave_fwd_t, wave_inv, wave_inv_t, col, col_t = tables

        row_index = lax.axis_index("rows")
        flat = row_index * item_parts + lax.axis_index("items")
        core = row_index % 2
        pair = (row_index // (row_parts // 8)) % PAIRS
        top = row_index // (row_parts // 2)
        mixing_index = top * (1 << low_bits) + flat % (1 << low_bits)
        mixing_count = 2 << low_bits

        both = jnp.concatenate([expand_weight.T, contract_weight], axis=0)
        both = both.reshape(2, shard, channels).transpose(1, 0, 2).reshape(shard, 2 * channels)
        deep = gather_stages(both, depth_bits)
        expand_rows = gather_stages(deep[:, :channels], plane_a)
        contract_rows = turn_plane(gather_stages(deep[:, channels:], plane_b))

        pieces = gather_stages(mixing_weight.reshape(1, -1, lanes), mixing_bits)
        block_size = channels // BLOCKS
        layers = xor_order(pieces, mixing_index).reshape(2, 2, 2, block_size, block_size)

        def blocks_of(w):
            zero = jnp.zeros_like(w[0])
            return jnp.concatenate(
                [jnp.concatenate([w[0], zero], 1), jnp.concatenate([zero, w[1]], 1)], 0
            )

        def big(w):
            real, imag = blocks_of(w[:, 0]), blocks_of(w[:, 1])
            return jnp.concatenate(
                [jnp.concatenate([real, imag], 1), jnp.concatenate([-imag, real], 1)], 0
            )

        mix_weight = jnp.stack([big(layers[0]), big(layers[1])])
        bias_pairs = mixing_bias.reshape(2, 2, PAIRS, lanes)
        mix_bias = lax.dynamic_index_in_dim(bias_pairs, pair, 2, keepdims=False)
        mix_bias = mix_bias.reshape(2, 1, 2 * lanes)

        masks = [0]
        for bit in depth_bits + plane_a:
            masks = masks + [m | (1 << bit) for m in masks]
        owners = flat ^ jnp.array(masks, dtype=jnp.int32)
        pick = (
            owners[:, None] == jnp.arange(device_total, dtype=jnp.int32)[None, :]
        ).astype(F32)
        bias_shards = expand_bias.reshape(device_total, shard)
        bias_local = jnp.dot(pick, bias_shards, precision=HIGHEST).reshape(1, hidden_local)

        counts_f = counts.astype(F32)
        live = jnp.arange(frame_total, dtype=jnp.int32)[None, :] < counts[:, None]
        live = live.astype(F32) / counts_f[:, None]
        factor = live[:, :, None] * time_weight[None]
        live_wide = jnp.broadcast_to(live[:, :, None], factor.shape)
        first_pair = jnp.stack([first_gain, first_shift])
        second_pair = jnp.stack([second_gain, second_shift])

        send_shape = (2, PAIRS, groups // 2, items, part, lanes)

        def put_parts(ref, values):
            if not aligned:
                ref[0] = values
                return
            for g in range(groups):
                for p in range(PAIRS):
                    ref[g // (groups // 2), p, g % (groups // 2), 0] = values[
                        g * part : (g + 1) * part, p * lanes : (p + 1) * lanes
                    ]

        def get_parts(ref):
            if not aligned:
                return ref[0]
            rows = []
            for g in range(groups):
                rows.append(
                    jnp.concatenate(
                        [
                            ref[g // (groups // 2), p, g % (groups // 2), 0]
                            for p in range(PAIRS)
                        ],
                        axis=1,
                    )
                )
            return jnp.concatenate(rows, axis=0)

        natural = (items, wave_rows, channels)
        parts_type = jax.ShapeDtypeStruct(send_shape if aligned else natural, F32)
        if aligned:
            parts_spec = pl.BlockSpec(
                (2, PAIRS, groups // 2, 1, part, lanes), lambda i: (0, 0, 0, i, 0, 0)
            )
        else:
            parts_spec = pl.BlockSpec((1, wave_rows, channels), lambda i: (i, 0, 0))

        def to_send(x):
            if aligned:
                return x
            x = x.reshape(items, 2, groups // 2, part, PAIRS, lanes)
            return x.transpose(1, 4, 2, 0, 3, 5)

        def from_send(x):
            x = x.reshape(send_shape)
            if aligned:
                return x
            return x.transpose(3, 0, 2, 4, 1, 5).reshape(natural)

        def exchange(x):
            return lax.all_to_all(x.reshape(row_parts, -1, lanes), "rows", 0, 0)

        source_shape = (row_parts, items, kept, stack, lanes)
        turned = (items, kept, row_parts * stack, lanes)
        column_type = jax.ShapeDtypeStruct(source_shape if aligned else turned, F32)
        if aligned:
            column_spec = pl.BlockSpec(
                (row_parts, 1, kept, stack, lanes), lambda i: (0, i, 0, 0, 0)
            )
        else:
            column_spec = pl.BlockSpec((1,) + turned[1:], lambda i: (i, 0, 0, 0))

        def to_columns(x):
            x = x.reshape(source_shape)
            if aligned:
                return x
            return x.transpose(1, 2, 0, 3, 4).reshape(turned)

        def from_columns(x):
            if aligned:
                return x
            x = x.reshape(items, kept, row_parts, stack, lanes)
            return x.transpose(2, 0, 1, 3, 4)

        def get_columns(ref):
            if aligned:
                pieces = [ref[:, 0, k].reshape(row_parts * stack, lanes) for k in range(kept)]
            else:
                pieces = [ref[0, k] for k in range(kept)]
            return jnp.concatenate(pieces, axis=1)

        def put_columns(ref, values):
            for k in range(kept):
                piece = values[:, k * lanes : (k + 1) * lanes]
                if aligned:
                    ref[:, 0, k] = piece.reshape(row_parts, stack, lanes)
                else:
                    ref[0, k] = piece

        def modes_rows(m):
            return jnp.concatenate(
                [
                    jnp.concatenate(
                        [
                            m[:MODES, k * lanes : (k + 1) * lanes],
                            m[MODES:, k * lanes : (k + 1) * lanes],
                        ],
                        axis=1,
                    )
                    for k in range(kept)
                ],
                axis=0,
            )

        def rows_modes(z):
            return jnp.concatenate(
                [
                    jnp.concatenate(
                        [
                            z[k * MODES : (k + 1) * MODES, :lanes],
                            z[k * MODES : (k + 1) * MODES, lanes:],
                        ],
                        axis=0,
                    )
                    for k in range(kept)
                ],
                axis=1,
            )

        item_spec = pl.BlockSpec((1, tokens, channels), lambda i: (i, 0, 0))
        item_type = jax.ShapeDtypeStruct((items, tokens, channels), F32)
        frames_spec = pl.BlockSpec(
            (1, frame_total, rows_local, width, channels), lambda i: (i, 0, 0, 0, 0)
        )
        factor_spec = pl.BlockSpec((1, frame_total, channels), lambda i: (i, 0, 0))
        wave_spec = whole((wave_rows, tokens))
        wave_spec_t = whole((tokens, wave_rows))
        pair_spec = whole((2, channels))
        item_bytes = items * tokens * channels * 4
        wave_flops = 2 * 6 * items * wave_rows * tokens * channels

        def head_body(frames_ref, factor_ref, pair_ref, table_ref, merged_ref, parts_ref):
            merged = 0.0
            for f in range(frame_total):
                frame = frames_ref[0, f].reshape(tokens, channels)
                merged = merged + frame * factor_ref[0, f : f + 1, :]
            merged_ref[0] = merged
            unit, _ = normalise(merged)
            normed = unit * pair_ref[0:1, :] + pair_ref[1:2, :]
            put_parts(parts_ref, dot_full(table_ref[...], normed))

        merged, head_parts = call(
            head_body,
            (items,),
            [frames_spec, factor_spec, pair_spec, wave_spec],
            [item_spec, parts_spec],
            [item_type, parts_type],
            wave_flops,
            item_bytes * (frame_total + 2),
            "head",
        )(frames, factor, first_pair, wave_fwd)
        columns = to_columns(exchange(to_send(head_parts)))

        mode_spec = pl.BlockSpec((1, mode_rows, 2 * lanes), lambda i: (i, 0, 0))
        mode_type = jax.ShapeDtypeStruct((items, mode_rows, 2 * lanes), F32)
        weight_spec = whole((2, 2 * lanes, 2 * lanes))
        bias_spec = whole((2, 1, 2 * lanes))
        col_spec = whole(col.shape)
        col_spec_t = whole(col_t.shape)
        mix_flops = 2 * 6 * items * (2 * mode_rows * 4 * lanes * lanes + 2 * 64 * 128 * kept * lanes)

        def mix_body(x_ref, w_ref, b_ref, col_ref, col_t_ref, out_ref, z_ref, u_ref, v_ref):
            z = modes_rows(dot_full(col_ref[...], get_columns(x_ref)))
            z_ref[0] = z
            u = dot_full(z, w_ref[0]) + b_ref[0]
            u_ref[0] = u
            v = dot_full(u * cdf(u), w_ref[1]) + b_ref[1]
            v_ref[0] = v
            mixed = v - jnp.clip(v, -SHRINK, SHRINK)
            put_columns(out_ref, dot_full(col_t_ref[...], rows_modes(mixed)))

        back, modes_in, first_pre, second_pre = call(
            mix_body,
            (items,),
            [column_spec, weight_spec, bias_spec, col_spec, col_spec_t],
            [column_spec, mode_spec, mode_spec, mode_spec],
            [column_type, mode_type, mode_type, mode_type],
            mix_flops,
            item_bytes * 4,
            "mix",
        )(columns, mix_weight, mix_bias, col, col_t)
        row_back = from_send(exchange(from_columns(back)))

        def split_body(a_ref, b_ref, ah, al, bh, bl):
            ah[...], al[...] = halves(a_ref[...])
            bh[...], bl[...] = halves(b_ref[...])

        split_rows = hidden_local // 4
        split_spec = pl.BlockSpec((split_rows, channels), lambda i: (i, 0))
        half_type = jax.ShapeDtypeStruct((hidden_local, channels), BF16)
        up_h, up_l, down_h, down_l = call(
            split_body,
            (4,),
            [split_spec] * 2,
            [split_spec] * 4,
            [half_type] * 4,
            0,
            hidden_local * channels * 16,
            "split_weights",
        )(expand_rows, contract_rows)

        token_total = items * tokens
        cot_own = output_cotangent.reshape(token_total, channels)
        cot_other = flip(cot_own, core_bit)

        block = min(256, token_total)
        token_spec = pl.BlockSpec((block, channels), lambda i: (i, 0))
        wide_spec = pl.BlockSpec((block, hidden_local), lambda i: (i, 0))
        weight_all = whole((hidden_local, channels))
        ff_flops = 2 * 3 * token_total * channels * hidden_local

        def cot_body(g_ref, dh_ref, dl_ref, gh_ref, hi_ref, lo_ref):
            g = halves(g_ref[...])
            hi_ref[...], lo_ref[...] = g
            gh_ref[...] = dot_pairs(g, (dh_ref[...], dl_ref[...]), NT)

        def cot_call(g):
            return call(
                cot_body,
                (token_total // block,),
                [token_spec, weight_all, weight_all],
                [wide_spec, token_spec, token_spec],
                [
                    jax.ShapeDtypeStruct((token_total, hidden_local), F32),
                    jax.ShapeDtypeStruct((token_total, channels), BF16),
                    jax.ShapeDtypeStruct((token_total, channels), BF16),
                ],
                ff_flops,
                token_total * (hidden_local + channels * 2) * 4,
                "cotangent_up",
            )(g, down_h, down_l)

        gh_own, gh_own_h, gh_own_l = cot_call(cot_own)
        gh_other, gh_other_h, gh_other_l = cot_call(cot_other)

        def spatial_body(parts_ref, merged_ref, pair_ref, table_ref, middle_ref, normed_ref):
            middle = merged_ref[0] + dot_full(table_ref[...], get_parts(parts_ref))
            middle_ref[0] = middle
            unit, _ = normalise(middle)
            normed_ref[0] = unit * pair_ref[0:1, :] + pair_ref[1:2, :]

        middle, normed_two = call(
            spatial_body,
            (items,),
            [parts_spec, item_spec, pair_spec, wave_spec_t],
            [item_spec, item_spec],
            [item_type, item_type],
            wave_flops,
            item_bytes * 4,
            "spatial",
        )(row_back, merged, second_pair, wave_inv)

        pieces_total = 4
        chunk = hidden_local // pieces_total

        def feed_body(n_ref, gh_ref, uh_ref, ul_ref, bias_ref, hh, hl, ph, pl_, grad_ref, bg_ref, nh, nl):
            n = halves(n_ref[...])
            nh[...], nl[...] = n
            grad = 0.0

            @pl.when(pl.program_id(0) == 0)
            def _():
                bg_ref[...] = jnp.zeros_like(bg_ref)

            for q in range(pieces_total):
                cut = slice(q * chunk, (q + 1) * chunk)
                w = (uh_ref[cut, :], ul_ref[cut, :])
                pre = dot_pairs(n, w, NT) + bias_ref[:, cut]
                phi = cdf(pre)
                hh[:, cut], hl[:, cut] = halves(pre * phi)
                gp = gh_ref[:, cut] * (phi + pre * density(pre))
                bg_ref[:, cut] += jnp.sum(gp, axis=0, keepdims=True)
                gp = halves(gp)
                ph[:, cut], pl_[:, cut] = gp
                grad = grad + dot_pairs(gp, w, NN)
            grad_ref[...] = grad

        def feed_call(n, gh):
            wide_half = jax.ShapeDtypeStruct((token_total, hidden_local), BF16)
            slim_half = jax.ShapeDtypeStruct((token_total, channels), BF16)
            return call(
                feed_body,
                (token_total // block,),
                [token_spec, wide_spec, weight_all, weight_all, whole((1, hidden_local))],
                [wide_spec] * 4
                + [token_spec, whole((1, hidden_local)), token_spec, token_spec],
                [wide_half] * 4
                + [
                    jax.ShapeDtypeStruct((token_total, channels), F32),
                    jax.ShapeDtypeStruct((1, hidden_local), F32),
                    slim_half,
                    slim_half,
                ],
                2 * ff_flops,
                token_total * (hidden_local * 3 + channels * 3) * 4,
                "feed_forward",
            )(n, gh, up_h, up_l, bias_local)

        normed_own = normed_two.reshape(token_total, channels)
        normed_other = flip(normed_own, core_bit)
        own = feed_call(normed_own, gh_own)
        other = feed_call(normed_other, gh_other)
        grad_own = own[4]
        grad_back = flip(other[4], core_bit)
        bias_grad_local = own[5] + other[5]

        def middle_body(
            mid_ref, g1_ref, g2_ref, cot_ref, pair_ref, table_ref, gm_ref, parts_ref, small_ref
        ):
            unit, scale = normalise(mid_ref[0])
            grad = g1_ref[0] + g2_ref[0]
            cot = cot_ref[0]
            gm = cot + normal_back(unit, scale, grad * pair_ref[0:1, :])
            gm_ref[0] = gm
            put_parts(parts_ref, dot_full(table_ref[...], gm))

            @pl.when(pl.program_id(0) == 0)
            def _():
                small_ref[...] = jnp.zeros_like(small_ref)

            small_ref[0:1, :] += jnp.sum(grad * unit, axis=0, keepdims=True)
            small_ref[1:2, :] += jnp.sum(grad, axis=0, keepdims=True)
            small_ref[2:3, :] += jnp.sum(cot, axis=0, keepdims=True)

        as_items = lambda x: x.reshape(items, tokens, channels)
        small_type = jax.ShapeDtypeStruct((8, channels), F32)
        small_spec = whole((8, channels))
        grad_middle, middle_parts, small_two = call(
            middle_body,
            (items,),
            [item_spec] * 4 + [pair_spec, wave_spec],
            [item_spec, parts_spec, small_spec],
            [item_type, parts_type, small_type],
            wave_flops,
            item_bytes * 6,
            "middle_back",
        )(
            middle,
            as_items(grad_own),
            as_items(grad_back),
            as_items(cot_own),
            second_pair,
            wave_inv_t,
        )
        grad_columns = to_columns(exchange(to_send(middle_parts)))

        def down_body(hh, hl, dh, dl, out_ref):
            out_ref[...] = dot_pairs((hh[...], hl[...]), (dh[...], dl[...]), NN)

        def down_call(h):
            return call(
                down_body,
                (token_total // block,),
                [wide_spec, wide_spec, weight_all, weight_all],
                token_spec,
                jax.ShapeDtypeStruct((token_total, channels), F32),
                ff_flops,
                token_total * (hidden_local + channels) * 4,
                "contract",
            )(h[0], h[1], down_h, down_l)

        update_own = down_call(own)
        update_back = flip(down_call(other), core_bit)
        block_out = (
            middle.reshape(token_total, channels) + update_own + update_back + contract_bias[None]
        )

        piece_spec = pl.BlockSpec((token_total, chunk), lambda q: (0, q))
        slim_spec = whole((token_total, channels))
        grad_spec = pl.BlockSpec((chunk, channels), lambda q: (q, 0))

        def outer_body(a1h, a1l, a2h, a2l, b1h, b1l, b2h, b2l, out_ref):
            out_ref[...] = dot_pairs(
                (a1h[...], a1l[...]), (b1h[...], b1l[...]), TN
            ) + dot_pairs((a2h[...], a2l[...]), (b2h[...], b2l[...]), TN)

        def outer_call(a, b, name):
            return call(
                outer_body,
                (pieces_total,),
                [piece_spec] * 4 + [slim_spec] * 4,
                grad_spec,
                jax.ShapeDtypeStruct((hidden_local, channels), F32),
                2 * ff_flops,
                (token_total * (hidden_local + channels) * 2 + hidden_local * channels) * 4,
                name,
            )(*a, *b)

        contract_grad = outer_call(
            (own[0], own[1], other[0], other[1]),
            (gh_own_h, gh_own_l, gh_other_h, gh_other_l),
            "contract_grad",
        )
        expand_grad = outer_call(
            (own[2], own[3], other[2], other[3]),
            (own[6], own[7], other[6], other[7]),
            "expand_grad",
        )
        expand_part = scatter_stages(expand_grad, plane_a)
        contract_part = scatter_stages(turn_plane(contract_grad), plane_b)
        both_grad = scatter_stages(
            jnp.concatenate([expand_part, contract_part], axis=1), depth_bits
        )
        expand_weight_grad = both_grad[:, :channels].T
        contract_weight_grad = both_grad[:, channels:]

        def mix_back_body(
            x_ref, z_ref, u_ref, v_ref, w_ref, col_ref, col_t_ref, out_ref, wg_ref, bg_ref
        ):
            @pl.when(pl.program_id(0) == 0)
            def _():
                wg_ref[...] = jnp.zeros_like(wg_ref)
                bg_ref[...] = jnp.zeros_like(bg_ref)

            grad = modes_rows(dot_full(col_ref[...], get_columns(x_ref)))
            e1 = jnp.where(jnp.abs(v_ref[0]) > SHRINK, grad, 0.0)
            u = u_ref[0]
            phi = cdf(u)
            spec = lambda dims: (dims, ((), ()))
            full = lambda a, b, dims: lax.dot_general(
                a, b, spec(dims), precision=HIGHEST, preferred_element_type=F32
            )
            e0 = full(e1, w_ref[1], NT) * (phi + u * density(u))
            wg_ref[0] += full(z_ref[0], e0, TN)
            wg_ref[1] += full(u * phi, e1, TN)
            bg_ref[0] += jnp.sum(e0, axis=0, keepdims=True)
            bg_ref[1] += jnp.sum(e1, axis=0, keepdims=True)
            dz = full(e0, w_ref[0], NT)
            put_columns(out_ref, dot_full(col_t_ref[...], rows_modes(dz)))

        grad_back_parts, big_grad, big_bias = call(
            mix_back_body,
            (items,),
            [column_spec, mode_spec, mode_spec, mode_spec, weight_spec, col_spec, col_spec_t],
            [column_spec, weight_spec, bias_spec],
            [
                column_type,
                jax.ShapeDtypeStruct((2, 2 * lanes, 2 * lanes), F32),
                jax.ShapeDtypeStruct((2, 1, 2 * lanes), F32),
            ],
            2 * mix_flops,
            item_bytes * 4,
            "mix_back",
        )(grad_columns, modes_in, first_pre, second_pre, mix_weight, col, col_t)
        last_parts = from_send(exchange(from_columns(grad_back_parts)))

        def unblock(w):
            rr, ri = w[:lanes, :lanes], w[:lanes, lanes:]
            ir, ii = w[lanes:, :lanes], w[lanes:, lanes:]
            real, imag = rr + ii, ri - ir
            cut = lambda m, b: m[
                b * block_size : (b + 1) * block_size, b * block_size : (b + 1) * block_size
            ]
            return jnp.stack([jnp.stack([cut(real, b), cut(imag, b)]) for b in range(2)])

        mix_grad = jnp.stack([unblock(big_grad[0]), unblock(big_grad[1])])
        mix_grad = mix_grad.reshape(mixing_count, -1, lanes)
        mix_grad = xor_order(mix_grad, mixing_index)
        mixing_weight_grad = scatter_stages(mix_grad, mixing_bits).reshape(mixing_weight.shape)

        bias_full = jnp.zeros((2, 2, PAIRS, lanes), F32)
        bias_full = lax.dynamic_update_slice(
            bias_full, big_bias.reshape(2, 2, 1, lanes), (0, 0, pair, 0)
        ).reshape(4, channels)
        hidden_bias = jnp.dot(
            pick.T, bias_grad_local.reshape(-1, shard), precision=HIGHEST
        ).reshape(-1, channels)
        early = total(jnp.concatenate([small_two[:3], bias_full, hidden_bias], axis=0))

        def final_body(
            parts_ref,
            merged_ref,
            gm_ref,
            frames_ref,
            factor_ref,
            live_ref,
            pair_ref,
            table_ref,
            out_ref,
            small_ref,
        ):
            grad = dot_full(table_ref[...], get_parts(parts_ref))
            unit, scale = normalise(merged_ref[0])
            gm = gm_ref[0] + normal_back(unit, scale, grad * pair_ref[0:1, :])

            @pl.when(pl.program_id(0) == 0)
            def _():
                small_ref[...] = jnp.zeros_like(small_ref)

            small_ref[frame_total : frame_total + 1, :] += jnp.sum(
                grad * unit, axis=0, keepdims=True
            )
            small_ref[frame_total + 1 : frame_total + 2, :] += jnp.sum(
                grad, axis=0, keepdims=True
            )
            for f in range(frame_total):
                frame = frames_ref[0, f].reshape(tokens, channels)
                small_ref[f : f + 1, :] += live_ref[0, f : f + 1, :] * jnp.sum(
                    frame * gm, axis=0, keepdims=True
                )
                out_ref[0, f] = (gm * factor_ref[0, f : f + 1, :]).reshape(
                    rows_local, width, channels
                )

        frames_grad, small_one = call(
            final_body,
            (items,),
            [parts_spec, item_spec, item_spec, frames_spec, factor_spec, factor_spec]
            + [pair_spec, wave_spec_t],
            [frames_spec, small_spec],
            [jax.ShapeDtypeStruct(frames.shape, F32), small_type],
            wave_flops,
            item_bytes * (3 + 2 * frame_total),
            "final",
        )(last_parts, merged, grad_middle, frames, factor, live_wide, first_pair, wave_fwd_t)
        late = total(small_one[: frame_total + 2])

        return (
            block_out.reshape(output_cotangent.shape),
            frames_grad,
            late[:frame_total],
            late[frame_total],
            late[frame_total + 1],
            mixing_weight_grad,
            early[3:7],
            early[0],
            early[1],
            expand_weight_grad,
            early[7:].reshape(hidden_total),
            contract_weight_grad,
            early[2],
        )

    return local


def solution(mesh):
    return jax.shard_map(
        build(mesh.shape["rows"], mesh.shape["items"]),
        mesh=mesh,
        in_specs=(
            P("items", None, "rows", None, None),
            P("items"),
            P(),
            P(),
            P(),
            P(("rows", "items"), None),
            P(),
            P(),
            P(),
            P(None, ("rows", "items")),
            P(),
            P(("rows", "items"), None),
            P(),
            P("items", "rows", None, None),
        ),
        out_specs=(
            P("items", "rows", None, None),
            P("items", None, "rows", None, None),
            P(),
            P(),
            P(),
            P(("rows", "items"), None),
            P(),
            P(),
            P(),
            P(None, ("rows", "items")),
            P(),
            P(("rows", "items"), None),
            P(),
        ),
        check_vma=False,
    )
```

time: 724 us -> 338 us (0.47)
  blocking collectives: 169 us -> 0 us
  waiting for transfers between devices: 323 us -> 159 us
  matrix products: 107 us -> 0.45 us
  Pallas kernels: 0 us -> 87.5 us
  starting transfers between devices: 16.9 us -> 52.7 us
  local copies, waits for them, and re-layouts: 45.3 us -> 18.5 us
  other arithmetic: 41.6 us -> 17.3 us
  between operations: 14.8 us -> 1.33 us
    reduce_scatter x2 -> x0, waiting for transfers between devices: 282 us -> none  [the longest x1 141 us: local(): lax.psum_scatter(grad_expand, ('rows', 'items'), scatter_dimension=1, til...]
    ppermute x0 -> x32, waiting for transfers between devices: none -> 150 us  [flip(): return lax.ppermute(x, AXES, pairs)]
    dot_general x34 -> x2, matrix products: 102 us -> 0.45 us  [the longest x1 0.26 us: local(): jnp.dot(pick.T, bias_grad_local.reshape(-1, shard), precision=HIGHEST)]
    all_gather x1 -> x0, blocking collectives: 92.6 us -> none  [local(): lax.all_gather(mixing_weight, ('rows', 'items'), axis=0, tiled=True)]
    pallas_call x0 -> x15, Pallas kernels: none -> 87.5 us  [the longest x2 17.4 us: feed_call(): call(feed_body, (token_total // block,), [token_spec, wide_spec, weight_a...]
    psum x1 -> x0, blocking collectives: 44.6 us -> none  [local(): lax.psum((grad_time, grad_first_gain, grad_first_shift, grad_mixing_bias,...]
    ppermute x0 -> x32, starting transfers between devices: none -> 32.6 us  [flip(): return lax.ppermute(x, AXES, pairs)]
    all_to_all x1 -> x0, blocking collectives: 31.5 us -> none  [local(): lax.all_to_all(grad_row_back, 'rows', split_axis=2, concat_axis=1, tiled=...]
  transfers between devices with their start and end apart: 8 -> 36, of which waited for: 5 -> 18; matrix products, arithmetic and copies ran while one was open for 19% -> 9% of each run, Pallas kernels for 0% -> 19%
where the time goes in v1:
time: 338 us; the launch traced here: 337 us
  waiting for transfers between devices  159 us (47%)
  Pallas kernels  87.5 us (26%)
  starting transfers between devices  52.7 us (16%)
  local copies, waits for them, and re-layouts  18.5 us (5%)
  other arithmetic  17.3 us (5%)
    ppermute x32, waiting for transfers between devices, flip(): return lax.ppermute(x, AXES, pairs)  150 us
    ppermute x32, starting transfers between devices, flip(): return lax.ppermute(x, AXES, pairs)  32.6 us
    all_to_all x4, starting transfers between devices, exchange(): return lax.all_to_all(x.reshape(row_parts, -1, lanes), 'rows', 0, 0)  20.2 us
    pallas_call x2, Pallas kernels, feed_call(): call(feed_body, (token_total // block,), [token_spec, wide_spec, weight_a...  17.4 us
    pallas_call x2, Pallas kernels, outer_call(): call(outer_body, (pieces_total,), [piece_spec] * 4 + [slim_spec] * 4, gra...  14.6 us
    pallas_call x2, Pallas kernels, cot_call(): call(cot_body, (token_total // block,), [token_spec, weight_all, weight_a...  9.53 us
    pallas_call x2, Pallas kernels, down_call(): call(down_body, (token_total // block,), [wide_spec, wide_spec, weight_al...  9.28 us
    all_to_all x4, waiting for transfers between devices, exchange(): return lax.all_to_all(x.reshape(row_parts, -1, lanes), 'rows', 0, 0)  9.07 us
  transfers between devices with their start and end apart: 36, of which 18 were waited for; matrix products, arithmetic and copies ran while one was open for 9% of the time, Pallas kernels for 19%

profile of v1, /device:TPU:0, one launch (start us, length us, event | category | flops | bytes accessed | tf_op | source)
XLA Modules:
  0.0 337.0 jit_solution(16427859584270546453)
XLA Ops:
  12.8 6.1 %all-to-all-start = ((f32[16,128,128]{2,1,0:T(8,128)}), f32[16,128,128]{2,1,0:T(8,128)S(1)}, u32[]{:S(2)}, u32[]{:S(2)}) async-start(f32[16,128,128]{2,1,0:T(8,128)} %bitcast.145), calls=%async_computation | async-start | bytes 2097152 | tf_op jit(solution)/shard_map/all_to_all | solution.py:301
  23.6 35.9 %collective-permute-done.2 = f32[4,32,128]{2,1,0:T(8,128)S(1)} collective-permute-done((f32[4,32,128]{2,1,0:T(8,128)S(1)}, f32[4,32,128]{2,1,0:T(8,128)S(1)}, u32[]{:S(2)}, u32[]{:S(2)}) %collective-permute-start.2) | collective-permute-done | bytes 65568 | tf_op jit(solution)/shard_map/ppermute | solution.py:127
  62.1 6.1 %mix.1 = (f32[16,2,8,8,128]{4,3,2,1,0:T(8,128)}, f32[2,256,256]{2,1,0:T(8,128)}, f32[2,256,256]{2,1,0:T(8,128)}, f32[2,256,256]{2,1,0:T(8,128)}) custom-call(f32[16,2,8,8,128]{4,3,2,1,0:T(8,128)} %bitcast.144, f32[2,256,256]{2,1,0:T(8,128)} %pad_maximum_fusion.5.w_ref, f32[2,1,256]{2,1,0:T(1,128)} %bitcast.164, f32[64,128]{1,0:T(8,128)} %constant.95.clone.col_ref, ...), custom_call_target="tpu_custom_call" | custom-call | flops 1207959552 | bytes 4194304 | tf_op jit(solution)/shard_map/mix/pallas_call | solution.py:422
  76.0 11.0 %collective-permute-done.7 = f32[256,512]{1,0:T(8,128)S(1)} collective-permute-done((f32[256,512]{1,0:T(8,128)S(1)}, f32[256,512]{1,0:T(8,128)S(1)}, u32[]{:S(2)}, u32[]{:S(2)}) %collective-permute-start.7) | collective-permute-done | bytes 524320 | tf_op jit(solution)/shard_map/ppermute | solution.py:127
  89.8 8.8 %collective-permute-done.5 = f32[256,512]{1,0:T(8,128)S(1)} collective-permute-done((f32[256,512]{1,0:T(8,128)S(1)}, f32[256,512]{1,0:T(8,128)S(1)}, u32[]{:S(2)}, u32[]{:S(2)}) %collective-permute-start.5) | collective-permute-done | bytes 524320 | tf_op jit(solution)/shard_map/ppermute | solution.py:127
  106.0 14.7 %collective-permute-done.8 = f32[512,512]{1,0:T(8,128)} collective-permute-done((f32[512,512]{1,0:T(8,128)}, f32[512,512]{1,0:T(8,128)}, u32[]{:S(2)}, u32[]{:S(2)}) %collective-permute-start.8) | collective-permute-done | bytes 1048608 | tf_op jit(solution)/shard_map/ppermute | solution.py:127
  131.6 4.8 %cotangent_up.2 = (f32[512,1024]{1,0:T(8,128)}, bf16[512,512]{1,0:T(8,128)(2,1)}, bf16[512,512]{1,0:T(8,128)(2,1)}) custom-call(f32[512,512]{1,0:T(8,128)} %bitcast.139, bf16[1024,512]{1,0:T(8,128)(2,1)} %get-tuple-element.60.dh_ref.dh, bf16[1024,512]{1,0:T(8,128)(2,1)} %get-tuple-element.61.dl_ref.dl), custom_call_target="tpu_custom_call" | custom-call | flops 1610612736 | bytes 4194304 | tf_op jit(solution)/shard_map/cotangent_up/pallas_call | solution.py:468
  136.4 4.8 %cotangent_up.3 = (f32[512,1024]{1,0:T(8,128)}, bf16[512,512]{1,0:T(8,128)(2,1)}, bf16[512,512]{1,0:T(8,128)(2,1)}) custom-call(f32[512,512]{1,0:T(8,128)} %collective-permute-done.10.g_ref, bf16[1024,512]{1,0:T(8,128)(2,1)} %get-tuple-element.60.dh_ref.dh, bf16[1024,512]{1,0:T(8,128)(2,1)} %get-tuple-element.61.dl_ref.dl), custom_call_target="tpu_custom_call" | custom-call | flops 1610612736 | bytes 4194304 | tf_op jit(solution)/shard_map/cotangent_up/pallas_call | solution.py:468
  141.2 8.7 %feed_forward.2 = (bf16[512,1024]{1,0:T(8,128)(2,1)}, bf16[512,1024]{1,0:T(8,128)(2,1)}, bf16[512,1024]{1,0:T(8,128)(2,1)}, bf16[512,1024]{1,0:T(8,128)(2,1)}, f...) custom-call(f32[512,512]{1,0:T(8,128)} %bitcast.175, ...), custom_call_target="tpu_custom_call" | custom-call | flops 3221225472 | bytes 9437184 | tf_op jit(solution)/shard_map/feed_forward/pallas_call | solution.py:531
  149.9 8.7 %feed_forward.3 = (bf16[512,1024]{1,0:T(8,128)(2,1)}, bf16[512,1024]{1,0:T(8,128)(2,1)}, bf16[512,1024]{1,0:T(8,128)(2,1)}, bf16[512,1024]{1,0:T(8,128)(2,1)}, f...) custom-call(f32[512,512]{1,0:T(8,128)} %collective-permute-done.9.n_ref, ...), custom_call_target="tpu_custom_call" | custom-call | flops 3221225472 | bytes 9437184 | tf_op jit(solution)/shard_map/feed_forward/pallas_call | solution.py:531
  158.6 7.3 %expand_grad.1 = f32[1024,512]{1,0:T(8,128)} custom-call(bf16[512,1024]{1,0:T(8,128)(2,1)} %get-tuple-element.85.a1h, bf16[512,1024]{1,0:T(8,128)(2,1)} %get-tuple-element.86.a1l, bf16[512,1024]{1,0:T(8,128)(2,1)} %get-tuple-element.87.a2h, bf16[512,1024]{1,0:T(8,128)(2,1)} %get-tuple-element.88.a2l, bf16[512,512]{1,0:T(8,128)(2,1)} %get-tuple-element.89.b1h, ...), custom_call_target="tpu_custom_call" | custom-call | flops 3221225472 | bytes 8388608 | tf_op jit(solution)/shard_map/expand_grad/pallas_call | solution.py:628
  167.8 7.3 %contract_grad.1 = f32[1024,512]{1,0:T(8,128)} custom-call(bf16[512,1024]{1,0:T(8,128)(2,1)} %get-tuple-element.65.hh.a1h, bf16[512,1024]{1,0:T(8,128)(2,1)} %get-tuple-element.66.hl.a1l, bf16[512,1024]{1,0:T(8,128)(2,1)} %get-tuple-element.68.hh.a2h, bf16[512,1024]{1,0:T(8,128)(2,1)} %get-tuple-element.69.hl.a2l, bf16[512,512]{1,0:T(8,128)(2,1)} %get-tuple-element.93.b1h, ...), custom_call_target="tpu_custom_call" | custom-call | flops 3221225472 | bytes 8388608 | tf_op jit(solution)/shard_map/contract_grad/pallas_call | solution.py:628
  177.1 14.4 %collective-permute-done.26 = f32[512,512]{1,0:T(8,128)S(1)} collective-permute-done((f32[512,512]{1,0:T(8,128)S(1)}, f32[512,512]{1,0:T(8,128)S(1)}, u32[]{:S(2)}, u32[]{:S(2)}) %collective-permute-start.26) | collective-permute-done | bytes 1048608 | tf_op jit(solution)/shard_map/ppermute | solution.py:127
  192.0 11.2 %collective-permute-done.28 = f32[512,512]{1,0:T(8,128)S(1)} collective-permute-done((f32[512,512]{1,0:T(8,128)S(1)}, f32[512,512]{1,0:T(8,128)S(1)}, u32[]{:S(2)}, u32[]{:S(2)}) %collective-permute-start.28) | collective-permute-done | bytes 1048608 | tf_op jit(solution)/shard_map/ppermute | solution.py:127
  211.4 4.9 %middle_back.1 = (f32[2,256,512]{2,1,0:T(8,128)}, f32[2,4,2,2,64,128]{5,4,3,2,1,0:T(8,128)}, f32[8,512]{1,0:T(8,128)}) custom-call(f32[2,256,512]{2,1,0:T(8,128)} %get-tuple-element.58.mid_ref, f32[2,256,512]{2,1,0:T(8,128)} %bitcast.142, f32[2,256,512]{2,1,0:T(8,128)} %bitcast.143, f32[2,256,512]{2,1,0:T(8,128)} %bitcast.140, ...), custom_call_target="tpu_custom_call" | custom-call | flops 805306368 | bytes 6291456 | tf_op jit(solution)/shard_map/middle_back/pallas_call | solution.py:578
  216.3 4.8 %all-to-all-start.2 = ((f32[16,128,128]{2,1,0:T(8,128)}), f32[16,128,128]{2,1,0:T(8,128)}, u32[]{:S(2)}, u32[]{:S(2)}) async-start(f32[16,128,128]{2,1,0:T(8,128)} %bitcast.146), calls=%async_computation.2 | async-start | bytes 2097152 | tf_op jit(solution)/shard_map/all_to_all | solution.py:301
  229.5 22.8 %collective-permute-done.30 = f32[128,1024]{1,0:T(8,128)S(1)} collective-permute-done((f32[128,1024]{1,0:T(8,128)S(1)}, f32[128,1024]{1,0:T(8,128)S(1)}, u32[]{:S(2)}, u32[]{:S(2)}) %collective-permute-start.30) | collective-permute-done | bytes 524320 | tf_op jit(solution)/shard_map/ppermute | solution.py:127
  257.4 9.4 %collective-permute-done.31 = f32[64,1024]{1,0:T(8,128)S(1)} collective-permute-done((f32[64,1024]{1,0:T(8,128)S(1)}, f32[64,1024]{1,0:T(8,128)S(1)}, u32[]{:S(2)}, u32[]{:S(2)}) %collective-permute-start.31) | collective-permute-done | bytes 262176 | tf_op jit(solution)/shard_map/ppermute | solution.py:127
  267.6 7.1 %mix_back.1 = (f32[16,2,8,8,128]{4,3,2,1,0:T(8,128)}, f32[2,256,256]{2,1,0:T(8,128)}, f32[2,1,256]{2,1,0:T(1,128)}) custom-call(f32[16,2,8,8,128]{4,3,2,1,0:T(8,128)} %bitcast.37.x_ref, f32[2,256,256]{2,1,0:T(8,128)} %get-tuple-element.73.z_ref, f32[2,256,256]{2,1,0:T(8,128)} %get-tuple-element.74.u_ref, f32[2,256,256]{2,1,0:T(8,128)} %get-tuple-element.75.v_ref, ...), custom_call_target="tpu_custom_call" | custom-call | flops 2415919104 | bytes 4194304 | tf_op jit(solution)/shard_map/mix_back/pallas_call | solution.py:681
  276.9 4.7 %all-to-all-start.3 = ((f32[16,128,128]{2,1,0:T(8,128)}), f32[16,128,128]{2,1,0:T(8,128)S(1)}, u32[]{:S(2)}, u32[]{:S(2)}) async-start(f32[16,128,128]{2,1,0:T(8,128)} %bitcast.38), calls=%async_computation.3 | async-start | bytes 2097152 | tf_op jit(solution)/shard_map/all_to_all | solution.py:301
  284.0 6.8 %collective-permute-done.22 = f32[11,512]{1,0:T(8,128)S(1)} collective-permute-done((f32[11,512]{1,0:T(8,128)S(1)}, f32[11,512]{1,0:T(8,128)S(1)}, u32[]{:S(2)}, u32[]{:S(2)}) %collective-permute-start.22) | collective-permute-done | bytes 22560 | tf_op jit(solution)/shard_map/ppermute | solution.py:127
  296.0 9.1 %all-to-all-done.3 = f32[16,128,128]{2,1,0:T(8,128)S(1)} async-done(((f32[16,128,128]{2,1,0:T(8,128)}), f32[16,128,128]{2,1,0:T(8,128)S(1)}, u32[]{:S(2)}, u32[]{:S(2)}) %all-to-all-start.3) | async-done | bytes 1048608 | tf_op jit(solution)/shard_map/all_to_all | solution.py:301
  306.0 5.9 %final.1 = (f32[2,4,4,64,512]{4,3,2,1,0:T(8,128)}, f32[8,512]{1,0:T(8,128)}) custom-call(f32[2,4,2,2,64,128]{5,4,3,2,1,0:T(8,128)} %bitcast.134, f32[2,256,512]{2,1,0:T(8,128)} %get-tuple-element.57.merged_ref, f32[2,256,512]{2,1,0:T(8,128)} %get-tuple-element.77.gm_ref, f32[2,4,4,64,512]{4,3,2,1,0:T(8,128)} %frames_ref.3, ...), custom_call_target="tpu_custom_call" | custom-call | flops 805306368 | bytes 11534336 | tf_op jit(solution)/shard_map/final/pallas_call | solution.py:755
  313.7 5.5 %collective-permute-start.25 = (f32[11,512]{1,0:T(8,128)S(1)}, f32[11,512]{1,0:T(8,128)S(1)}, u32[]{:S(2)}, u32[]{:S(2)}) collective-permute-start(f32[11,512]{1,0:T(8,128)S(1)} %add.154), channel_id=1, source_target_pairs={{0,16},{1,17},{2,18},{3,19},{4,20},{5,21},{6,22},{7,23},{8,24},{9,... | collective-permute-start | bytes 67592 | tf_op jit(solution)/shard_map/ppermute | solution.py:127
  (212 shorter events, 104.9 us)
Async XLA Ops:
  1.5 17.4 %collective-permute-start = (f32[1,32,128]{2,1,0:T(8,128)S(1)}, f32[1,32,128]{2,1,0:T(8,128)S(1)}, u32[]{:S(2)}, u32[]{:S(2)}) collective-permute-start(f32[1,32,128]{2,1,0:T(8,128)S(1)} %reshape.189), channel_id=1, source_target_pairs={{0,1},{1,0},{2,3},{3,2},{4,5},{5,4},{6,7},{7,6},{8,9},{9,8},{10,11... | collective-permute-start | bytes 49160 | tf_op jit(solution)/shard_map/ppermute | solution.py:127
  12.8 48.4 %all-to-all-start = ((f32[16,128,128]{2,1,0:T(8,128)}), f32[16,128,128]{2,1,0:T(8,128)S(1)}, u32[]{:S(2)}, u32[]{:S(2)}) async-start(f32[16,128,128]{2,1,0:T(8,128)} %bitcast.145), calls=%async_computation | async-start | bytes 2097152 | tf_op jit(solution)/shard_map/all_to_all | solution.py:301
  19.6 40.5 %collective-permute-start.3 = (f32[64,1024]{1,0:T(8,128)S(1)}, f32[64,1024]{1,0:T(8,128)S(1)}, u32[]{:S(2)}, u32[]{:S(2)}) collective-permute-start(f32[64,1024]{1,0:T(8,128)S(1)} %bitcast.135), channel_id=1, source_target_pairs={{0,16},{1,17},{2,18},{3,19},{4,20},{5,21},{6,22},{7,23},{8,24},{9,... | collective-permute-start | bytes 786440 | tf_op jit(solution)/shard_map/ppermute | solution.py:127
  22.3 37.1 %collective-permute-start.2 = (f32[4,32,128]{2,1,0:T(8,128)S(1)}, f32[4,32,128]{2,1,0:T(8,128)S(1)}, u32[]{:S(2)}, u32[]{:S(2)}) collective-permute-start(f32[4,32,128]{2,1,0:T(8,128)S(1)} %pad_maximum_fusion.10), channel_id=1, source_target_pairs={{0,16},{1,17},{2,18},{3,19},{4,20},{5,21},{6,22},{7,23},{8,24},{9,... | collective-permute-start | bytes 196616 | tf_op jit(solution)/shard_map/ppermute | solution.py:127
  60.2 13.5 %collective-permute-start.4 = (f32[128,1024]{1,0:T(8,128)S(1)}, f32[128,1024]{1,0:T(8,128)S(1)}, u32[]{:S(2)}, u32[]{:S(2)}) collective-permute-start(f32[128,1024]{1,0:T(8,128)S(1)} %pad_maximum_fusion.6), channel_id=1, source_target_pairs={{0,8},{1,9},{2,10},{3,11},{4,12},{5,13},{6,14},{7,15},{8,0},{9,1},... | collective-permute-start | bytes 1572872 | tf_op jit(solution)/shard_map/ppermute | solution.py:127
  68.2 32.6 %all-to-all-start.1 = ((f32[16,128,128]{2,1,0:T(8,128)}), f32[16,128,128]{2,1,0:T(8,128)}, u32[]{:S(2)}, u32[]{:S(2)}) async-start(f32[16,128,128]{2,1,0:T(8,128)} %bitcast.147), calls=%async_computation.1 | async-start | bytes 2097152 | tf_op jit(solution)/shard_map/all_to_all | solution.py:301
  73.9 13.1 %collective-permute-start.7 = (f32[256,512]{1,0:T(8,128)S(1)}, f32[256,512]{1,0:T(8,128)S(1)}, u32[]{:S(2)}, u32[]{:S(2)}) collective-permute-start(f32[256,512]{1,0:T(8,128)S(1)} %get-tuple-element.99), channel_id=1, source_target_pairs={{0,1},{1,0},{2,3},{3,2},{4,5},{5,4},{6,7},{7,6},{8,9},{9,8},{10,11... | collective-permute-start | bytes 1572872 | tf_op jit(solution)/shard_map/ppermute | solution.py:127
  74.5 24.1 %collective-permute-start.5 = (f32[256,512]{1,0:T(8,128)S(1)}, f32[256,512]{1,0:T(8,128)S(1)}, u32[]{:S(2)}, u32[]{:S(2)}) collective-permute-start(f32[256,512]{1,0:T(8,128)S(1)} %get-tuple-element.100), channel_id=1, source_target_pairs={{0,4},{1,5},{2,6},{3,7},{4,0},{5,1},{6,2},{7,3},{8,12},{9,13},{10,... | collective-permute-start | bytes 1572872 | tf_op jit(solution)/shard_map/ppermute | solution.py:127
  88.1 32.6 %collective-permute-start.8 = (f32[512,512]{1,0:T(8,128)}, f32[512,512]{1,0:T(8,128)}, u32[]{:S(2)}, u32[]{:S(2)}) collective-permute-start(f32[512,512]{1,0:T(8,128)} %pad_maximum_fusion.3), channel_id=1, source_target_pairs={{0,4},{1,5},{2,6},{3,7},{4,0},{5,1},{6,2},{7,3},{8,12},{9,13},{10,... | collective-permute-start | bytes 3145736 | tf_op jit(solution)/shard_map/ppermute | solution.py:127
  99.6 24.5 %collective-permute-start.6 = (f32[512,512]{1,0:T(8,128)}, f32[512,512]{1,0:T(8,128)}, u32[]{:S(2)}, u32[]{:S(2)}) collective-permute-start(f32[512,512]{1,0:T(8,128)} %pad_maximum_fusion.2), channel_id=1, source_target_pairs={{0,1},{1,0},{2,3},{3,2},{4,5},{5,4},{6,7},{7,6},{8,9},{9,8},{10,11... | collective-permute-start | bytes 3145736 | tf_op jit(solution)/shard_map/ppermute | solution.py:127
  100.1 36.3 %collective-permute-start.10 = (f32[512,512]{1,0:T(8,128)S(1)}, f32[512,512]{1,0:T(8,128)}, u32[]{:S(2)}, u32[]{:S(2)}) collective-permute-start(f32[512,512]{1,0:T(8,128)S(1)} %bitcast.141), channel_id=1, source_target_pairs={{0,2},{1,3},{2,0},{3,1},{4,6},{5,7},{6,4},{7,5},{8,10},{9,11},{10,... | collective-permute-start | bytes 3145736 | tf_op jit(solution)/shard_map/ppermute | solution.py:127
  104.6 45.3 %collective-permute-start.9 = (f32[512,512]{1,0:T(8,128)}, f32[512,512]{1,0:T(8,128)}, u32[]{:S(2)}, u32[]{:S(2)}) collective-permute-start(f32[512,512]{1,0:T(8,128)} %bitcast.174), channel_id=1, source_target_pairs={{0,2},{1,3},{2,0},{3,1},{4,6},{5,7},{6,4},{7,5},{8,10},{9,11},{10,... | collective-permute-start | bytes 3145736 | tf_op jit(solution)/shard_map/ppermute | solution.py:127
  167.2 24.3 %collective-permute-start.26 = (f32[512,512]{1,0:T(8,128)S(1)}, f32[512,512]{1,0:T(8,128)S(1)}, u32[]{:S(2)}, u32[]{:S(2)}) collective-permute-start(f32[512,512]{1,0:T(8,128)S(1)} %slice.319), channel_id=1, source_target_pairs={{0,1},{1,0},{2,3},{3,2},{4,5},{5,4},{6,7},{7,6},{8,9},{9,8},{10,11... | collective-permute-start | bytes 3145736 | tf_op jit(solution)/shard_map/ppermute | solution.py:127
  177.0 26.2 %collective-permute-start.28 = (f32[512,512]{1,0:T(8,128)S(1)}, f32[512,512]{1,0:T(8,128)S(1)}, u32[]{:S(2)}, u32[]{:S(2)}) collective-permute-start(f32[512,512]{1,0:T(8,128)S(1)} %bitcast.151), channel_id=1, source_target_pairs={{0,4},{1,5},{2,6},{3,7},{4,0},{5,1},{6,2},{7,3},{8,12},{9,13},{10,... | collective-permute-start | bytes 3145736 | tf_op jit(solution)/shard_map/ppermute | solution.py:127
  177.1 33.4 %collective-permute-start.12 = (f32[512,512]{1,0:T(8,128)}, f32[512,512]{1,0:T(8,128)S(1)}, u32[]{:S(2)}, u32[]{:S(2)}) collective-permute-start(f32[512,512]{1,0:T(8,128)} %get-tuple-element.71), channel_id=1, source_target_pairs={{0,2},{1,3},{2,0},{3,1},{4,6},{5,7},{6,4},{7,5},{8,10},{9,11},{10,... | collective-permute-start | bytes 3145736 | tf_op jit(solution)/shard_map/ppermute | solution.py:127
  191.8 29.4 %collective-permute-start.27 = (f32[256,512]{1,0:T(8,128)S(1)}, f32[256,512]{1,0:T(8,128)S(1)}, u32[]{:S(2)}, u32[]{:S(2)}) collective-permute-start(f32[256,512]{1,0:T(8,128)S(1)} %slice.321), channel_id=1, source_target_pairs={{0,4},{1,5},{2,6},{3,7},{4,0},{5,1},{6,2},{7,3},{8,12},{9,13},{10,... | collective-permute-start | bytes 1572872 | tf_op jit(solution)/shard_map/ppermute | solution.py:127
  204.3 17.0 %collective-permute-start.29 = (f32[256,512]{1,0:T(8,128)}, f32[256,512]{1,0:T(8,128)}, u32[]{:S(2)}, u32[]{:S(2)}) collective-permute-start(f32[256,512]{1,0:T(8,128)} %slice.325), channel_id=1, source_target_pairs={{0,1},{1,0},{2,3},{3,2},{4,5},{5,4},{6,7},{7,6},{8,9},{9,8},{10,11... | collective-permute-start | bytes 1572872 | tf_op jit(solution)/shard_map/ppermute | solution.py:127
  210.4 44.5 %collective-permute-start.11 = (f32[512,512]{1,0:T(8,128)}, f32[512,512]{1,0:T(8,128)}, u32[]{:S(2)}, u32[]{:S(2)}) collective-permute-start(f32[512,512]{1,0:T(8,128)} %contract.3), channel_id=1, source_target_pairs={{0,2},{1,3},{2,0},{3,1},{4,6},{5,7},{6,4},{7,5},{8,10},{9,11},{10,... | collective-permute-start | bytes 3145736 | tf_op jit(solution)/shard_map/ppermute | solution.py:127
  216.3 51.3 %all-to-all-start.2 = ((f32[16,128,128]{2,1,0:T(8,128)}), f32[16,128,128]{2,1,0:T(8,128)}, u32[]{:S(2)}, u32[]{:S(2)}) async-start(f32[16,128,128]{2,1,0:T(8,128)} %bitcast.146), calls=%async_computation.2 | async-start | bytes 2097152 | tf_op jit(solution)/shard_map/all_to_all | solution.py:301
  222.5 29.8 %collective-permute-start.30 = (f32[128,1024]{1,0:T(8,128)S(1)}, f32[128,1024]{1,0:T(8,128)S(1)}, u32[]{:S(2)}, u32[]{:S(2)}) collective-permute-start(f32[128,1024]{1,0:T(8,128)S(1)} %pad_maximum_fusion.4), channel_id=1, source_target_pairs={{0,8},{1,9},{2,10},{3,11},{4,12},{5,13},{6,14},{7,15},{8,0},{9,1},... | collective-permute-start | bytes 1572872 | tf_op jit(solution)/shard_map/ppermute | solution.py:127
  252.4 14.4 %collective-permute-start.31 = (f32[64,1024]{1,0:T(8,128)S(1)}, f32[64,1024]{1,0:T(8,128)S(1)}, u32[]{:S(2)}, u32[]{:S(2)}) collective-permute-start(f32[64,1024]{1,0:T(8,128)S(1)} %slice.329), channel_id=1, source_target_pairs={{0,16},{1,17},{2,18},{3,19},{4,20},{5,21},{6,22},{7,23},{8,24},{9,... | collective-permute-start | bytes 786440 | tf_op jit(solution)/shard_map/ppermute | solution.py:127
  276.9 28.2 %all-to-all-start.3 = ((f32[16,128,128]{2,1,0:T(8,128)}), f32[16,128,128]{2,1,0:T(8,128)S(1)}, u32[]{:S(2)}, u32[]{:S(2)}) async-start(f32[16,128,128]{2,1,0:T(8,128)} %bitcast.38), calls=%async_computation.3 | async-start | bytes 2097152 | tf_op jit(solution)/shard_map/all_to_all | solution.py:301
  291.4 22.2 %collective-permute-start.18 = (f32[4,32,128]{2,1,0:T(8,128)S(1)}, f32[4,32,128]{2,1,0:T(8,128)S(1)}, u32[]{:S(2)}, u32[]{:S(2)}) collective-permute-start(f32[4,32,128]{2,1,0:T(8,128)S(1)} %slice_bitcast_fusion.3), channel_id=1, source_target_pairs={{0,16},{1,17},{2,18},{3,19},{4,20},{5,21},{6,22},{7,23},{8,24},{9,... | collective-permute-start | bytes 196616 | tf_op jit(solution)/shard_map/ppermute | solution.py:127
  294.8 18.9 %collective-permute-start.24 = (f32[11,512]{1,0:T(8,128)S(1)}, f32[11,512]{1,0:T(8,128)S(1)}, u32[]{:S(2)}, u32[]{:S(2)}) collective-permute-start(f32[11,512]{1,0:T(8,128)S(1)} %add.153), channel_id=1, source_target_pairs={{0,8},{1,9},{2,10},{3,11},{4,12},{5,13},{6,14},{7,15},{8,0},{9,1},... | collective-permute-start | bytes 67592 | tf_op jit(solution)/shard_map/ppermute | solution.py:127
  (31 other events, 385.2 us)

commit v2 on v1

v2 whole, which is shorter than its diff:
```python
import math

import jax
import jax.numpy as jnp
import numpy as np
from jax import lax
from jax.experimental import pallas as pl
from jax.experimental.pallas import tpu as pltpu
from jax.sharding import PartitionSpec as P

BLOCKS = 8
MODES = 32
PAIRS = BLOCKS // 2
HIGHEST = lax.Precision.HIGHEST
SHRINK = 0.01
EPS = 1e-05
F32 = jnp.float32
BF16 = jnp.bfloat16
PLANNED = 0.001
AXES = ("rows", "items")
LIMIT = 56 * 1024 * 1024
HALF_ROOT = math.sqrt(0.5)
DENSITY = 1.0 / math.sqrt(2.0 * math.pi)


def after(x, *others):
    return lax.optimization_barrier((x,) + others)[0]


def make_tables(grid_size, rows_local, row_parts):
    n = np.arange(grid_size)
    along = np.arange(MODES)
    across = np.concatenate(
        [np.arange(MODES // 2), np.arange(grid_size - MODES // 2, grid_size)]
    )
    step = 2.0 * np.pi / grid_size
    factor = 1.0 / np.sqrt(grid_size)
    wide = (along[:, None] * n[None, :] % grid_size) * step
    high = (across[:, None] * n[None, :] % grid_size) * step
    cos_w, sin_w = np.cos(wide) * factor, np.sin(wide) * factor
    cos_h, sin_h = np.cos(high) * factor, np.sin(high) * factor
    doubled = np.where(along == 0, 1.0, 2.0)[:, None]
    eye = np.eye(rows_local)
    forward = np.einsum("pkw,hg->kphgw", np.stack([cos_w, -sin_w]), eye)
    forward = forward.reshape(MODES * 2 * rows_local, rows_local * grid_size)
    inverse = np.einsum("pkw,hg->gwkph", np.stack([cos_w * doubled, -sin_w * doubled]), eye)
    inverse = inverse.reshape(rows_local * grid_size, MODES * 2 * rows_local)
    column = np.stack([np.stack([cos_h, sin_h]), np.stack([-sin_h, cos_h])])
    column = column.reshape(2, 2, MODES, row_parts, rows_local)
    column = column.transpose(0, 2, 3, 1, 4).reshape(2 * MODES, row_parts * 2 * rows_local)
    as32 = lambda x: np.ascontiguousarray(x, dtype=np.float32)
    return (
        as32(forward),
        as32(forward.T),
        as32(inverse),
        as32(inverse.T),
        as32(column),
        as32(column.T),
    )


def dot_full(a, b):
    return jnp.dot(a, b, precision=HIGHEST, preferred_element_type=F32)


def halves(x):
    high = x.astype(BF16)
    return high, (x - high.astype(F32)).astype(BF16)


def dot_pairs(a, b, dims):
    spec = (dims, ((), ()))
    one = lambda x, y: lax.dot_general(x, y, spec, preferred_element_type=F32)
    return one(a[0], b[0]) + (one(a[0], b[1]) + one(a[1], b[0]))


def dot_split(table, x):
    return dot_pairs((table[0], table[1]), halves(x), NN)


def split_table(x):
    high = x.astype(jnp.bfloat16)
    low = (x - high.astype(np.float32)).astype(jnp.bfloat16)
    return np.stack([high, low])


NN = ((1,), (0,))
NT = ((1,), (1,))
TN = ((0,), (0,))


def cdf(v):
    return 0.5 + 0.5 * lax.erf(v * HALF_ROOT)


def density(v):
    return DENSITY * jnp.exp(-0.5 * v * v)


def normalise(v):
    average = jnp.mean(v, axis=-1, keepdims=True)
    centred = v - average
    spread = jnp.mean(centred * centred, axis=-1, keepdims=True)
    scale = lax.rsqrt(spread + EPS)
    return centred * scale, scale


def normal_back(unit, scale, weighted):
    m0 = jnp.mean(weighted, axis=-1, keepdims=True)
    m1 = jnp.mean(weighted * unit, axis=-1, keepdims=True)
    return scale * (weighted - m0 - unit * m1)


def call(body, grid, in_specs, out_specs, out_shape, flops, moved, name, scratch=()):
    many = isinstance(out_shape, (list, tuple))
    shapes = list(out_shape) if many else [out_shape]
    run = pl.pallas_call(
        body,
        grid=grid,
        in_specs=in_specs,
        out_specs=out_specs,
        out_shape=shapes if many else shapes[0],
        scratch_shapes=list(scratch),
        name=name,
        cost_estimate=pl.CostEstimate(
            flops=int(flops * PLANNED),
            transcendentals=0,
            bytes_accessed=int(moved * PLANNED),
        ),
        compiler_params=pltpu.CompilerParams(vmem_limit_bytes=LIMIT),
    )

    return run


def whole(shape):
    return pl.BlockSpec(shape, lambda *_: (0,) * len(shape))


def build(row_parts, item_parts):
    row_bits = row_parts.bit_length() - 1
    item_bits = item_parts.bit_length() - 1
    device_total = row_parts * item_parts
    lanes = 128

    def flip(x, bit):
        pairs = [(f, f ^ (1 << bit)) for f in range(device_total)]
        return lax.ppermute(x, AXES, pairs)

    def flip_mask(x, mask):
        pairs = [(f, f ^ mask) for f in range(device_total)]
        return lax.ppermute(x, AXES, pairs)

    core_bit = item_bits
    depth_bits = [item_bits + row_bits - 1, item_bits + row_bits - 2]
    plane_a = [item_bits + b for b in range(row_bits - 3, 0, -1)] + list(range(item_bits))
    plane_b = plane_a[::-1]
    low_bits = row_bits - 3 + item_bits
    mixing_low = list(range(low_bits))[::-1]
    masks_a, masks_b = [0], [0]
    for bit_a, bit_b in zip(plane_a, plane_b):
        masks_a = masks_a + [m | (1 << bit_a) for m in masks_a]
        masks_b = masks_b + [m | (1 << bit_b) for m in masks_b]
    place_a = [masks_a.index(m) for m in masks_b]

    def gather_stages(x, bits):
        for bit in bits:
            x = jnp.concatenate([x, flip(x, bit)], axis=0)
        return x

    def scatter_stages(x, bits, axis=0):
        for bit in bits[::-1]:
            stay, leave = jnp.split(x, 2, axis=axis)
            x = stay + flip(leave, bit)
        return x

    def mixing_order(x, index):
        for bit in range(x.shape[0].bit_length() - 1):
            lead = x.reshape((-1, 2, 1 << bit) + x.shape[1:])
            swapped = (index >> bit) % 2 == 1
            x = jnp.where(swapped, lead[:, ::-1], lead).reshape(x.shape)
        return x

    def total(x):
        for bits in ([core_bit], plane_a, depth_bits):
            masks = [0]
            for bit in bits:
                masks = masks + [m | (1 << bit) for m in masks]
            parts = [x] + [flip_mask(x, m) for m in masks[1:]]
            while len(parts) > 1:
                parts = [a + b for a, b in zip(parts[::2], parts[1::2])]
            x = parts[0]
        return x

    def local(
        frames,
        counts,
        time_weight,
        first_gain,
        first_shift,
        mixing_weight,
        mixing_bias,
        second_gain,
        second_shift,
        expand_weight,
        expand_bias,
        contract_weight,
        contract_bias,
        output_cotangent,
    ):
        items, frame_total, rows_local, width, channels = frames.shape
        grid_size = rows_local * row_parts
        tokens = rows_local * width
        wave_rows = MODES * 2 * rows_local
        groups = row_parts // PAIRS
        kept = MODES // groups
        part = kept * 2 * rows_local
        stack = 2 * rows_local
        mode_rows = kept * MODES
        shard = contract_weight.shape[0]
        hidden_total = expand_bias.shape[0]
        hidden_local = hidden_total // 2
        piece_total = len(masks_a)
        half = hidden_local // 2
        unit = half // piece_total
        quarter = half // 2
        block_size = channels // BLOCKS
        aligned = stack % 8 == 0
        tables = make_tables(grid_size, rows_local, row_parts)
        wave_fwd, wave_fwd_t, wave_inv, wave_inv_t, col, col_t = tables
        wave_fwd_t, wave_inv, wave_inv_t = map(split_table, (wave_fwd_t, wave_inv, wave_inv_t))
        col_half, col_t_half = split_table(col), split_table(col_t)

        row_index = lax.axis_index("rows")
        flat = row_index * item_parts + lax.axis_index("items")
        pair = (row_index // (row_parts // 8)) % PAIRS
        top = row_index // (row_parts // 2)
        mixing_index = top * (1 << low_bits) + flat % (1 << low_bits)
        mixing_count = 2 << low_bits

        state = []

        def seq(x):
            return after(x, *state) if state else x

        def done(x):
            state[:] = [x]

        both = jnp.concatenate([expand_weight.T, contract_weight], axis=1)
        carried = jnp.concatenate([both, mixing_weight.reshape(-1, 2 * channels)], axis=0)
        arrived = flip(carried, depth_bits[0])
        both_near = jnp.concatenate([both, flip(both, depth_bits[1])], axis=0)
        pieces = jnp.stack(
            [mixing_weight.reshape(-1, lanes), arrived[shard:].reshape(-1, lanes)]
        )
        pieces = gather_stages(pieces, mixing_low)
        axes_total = low_bits + 1

        def turn_axes(x):
            lead = x.reshape((2,) * axes_total + x.shape[1:])
            order = tuple(range(axes_total))[::-1]
            return lead.transpose(order + (axes_total, axes_total + 1)).reshape(x.shape)

        layers = mixing_order(turn_axes(pieces), mixing_index)
        layers = layers.reshape(2, 2, 2, block_size, block_size)

        def blocks_of(w):
            zero = jnp.zeros_like(w[0])
            return jnp.concatenate(
                [jnp.concatenate([w[0], zero], 1), jnp.concatenate([zero, w[1]], 1)], 0
            )

        def big(w):
            real, imag = blocks_of(w[:, 0]), blocks_of(w[:, 1])
            return jnp.concatenate(
                [jnp.concatenate([real, imag], 1), jnp.concatenate([-imag, real], 1)], 0
            )

        mix_weight = [big(layers[0]), big(layers[1])]
        bias_pairs = mixing_bias.reshape(2, 2, PAIRS, lanes)
        mix_bias = lax.dynamic_index_in_dim(bias_pairs, pair, 2, keepdims=False)
        mix_bias = mix_bias.reshape(2, 1, 2 * lanes)

        first_bit, second_bit = (1 << b for b in depth_bits)
        masks = [
            far | p | near for far in (0, first_bit) for p in masks_a for near in (0, second_bit)
        ]
        owners = flat ^ jnp.array(masks, dtype=jnp.int32)
        pick = (
            owners[:, None] == jnp.arange(device_total, dtype=jnp.int32)[None, :]
        ).astype(F32)
        bias_shards = expand_bias.reshape(device_total, shard)
        bias_local = jnp.dot(pick, bias_shards, precision=HIGHEST).reshape(1, hidden_local)

        as_row = lambda x: x.reshape(1, channels)
        gain_one, shift_one = as_row(first_gain), as_row(first_shift)
        gain_two, shift_two = as_row(second_gain), as_row(second_shift)

        def put_parts(ref, values):
            if not aligned:
                ref[0] = values
                return
            for g in range(groups):
                for p in range(PAIRS):
                    ref[g // (groups // 2), p, g % (groups // 2), 0] = values[
                        g * part : (g + 1) * part, p * lanes : (p + 1) * lanes
                    ]

        def get_parts(ref):
            if not aligned:
                return ref[0]
            rows = []
            for g in range(groups):
                rows.append(
                    jnp.concatenate(
                        [
                            ref[g // (groups // 2), p, g % (groups // 2), 0]
                            for p in range(PAIRS)
                        ],
                        axis=1,
                    )
                )
            return jnp.concatenate(rows, axis=0)

        def parts_type(count):
            shape = (2, PAIRS, groups // 2, count, part, lanes)
            if not aligned:
                shape = (count, wave_rows, channels)
            return jax.ShapeDtypeStruct(shape, F32)

        if aligned:
            parts_spec = pl.BlockSpec(
                (2, PAIRS, groups // 2, 1, part, lanes), lambda i: (0, 0, 0, i, 0, 0)
            )
        else:
            parts_spec = pl.BlockSpec((1, wave_rows, channels), lambda i: (i, 0, 0))

        def to_send(x, count):
            if aligned:
                return x
            x = x.reshape(count, 2, groups // 2, part, PAIRS, lanes)
            return x.transpose(1, 4, 2, 0, 3, 5)

        def from_send(x, count):
            x = x.reshape(2, PAIRS, groups // 2, count, part, lanes)
            if aligned:
                return x
            return x.transpose(3, 0, 2, 4, 1, 5).reshape(count, wave_rows, channels)

        def exchange(x):
            return lax.all_to_all(x.reshape(row_parts, -1, lanes), "rows", 0, 0)

        def column_type(count):
            shape = (row_parts, count, kept, stack, lanes)
            if not aligned:
                shape = (count, kept, row_parts * stack, lanes)
            return jax.ShapeDtypeStruct(shape, F32)

        if aligned:
            column_spec = pl.BlockSpec(
                (row_parts, 1, kept, stack, lanes), lambda i: (0, i, 0, 0, 0)
            )
        else:
            column_spec = pl.BlockSpec(
                (1, kept, row_parts * stack, lanes), lambda i: (i, 0, 0, 0)
            )

        def to_columns(x, count):
            x = x.reshape(row_parts, count, kept, stack, lanes)
            if aligned:
                return x
            return x.transpose(1, 2, 0, 3, 4).reshape(column_type(count).shape)

        def from_columns(x, count):
            if aligned:
                return x
            x = x.reshape(count, kept, row_parts, stack, lanes)
            return x.transpose(2, 0, 1, 3, 4)

        def get_columns(ref):
            if aligned:
                pieces = [ref[:, 0, k].reshape(row_parts * stack, lanes) for k in range(kept)]
            else:
                pieces = [ref[0, k] for k in range(kept)]
            return jnp.concatenate(pieces, axis=1)

        def put_columns(ref, values):
            for k in range(kept):
                piece = values[:, k * lanes : (k + 1) * lanes]
                if aligned:
                    ref[:, 0, k] = piece.reshape(row_parts, stack, lanes)
                else:
                    ref[0, k] = piece

        def modes_rows(m):
            cut = lambda p, k: m[p * MODES : (p + 1) * MODES, k * lanes : (k + 1) * lanes]
            return jnp.concatenate(
                [jnp.concatenate([cut(0, k), cut(1, k)], axis=1) for k in range(kept)], axis=0
            )

        def rows_modes(z):
            cut = lambda p, k: z[k * MODES : (k + 1) * MODES, p * lanes : (p + 1) * lanes]
            return jnp.concatenate(
                [jnp.concatenate([cut(0, k), cut(1, k)], axis=0) for k in range(kept)], axis=1
            )

        def live_row(counts_ref, item, f):
            seen = jnp.full((1, channels), counts_ref[item], jnp.int32)
            return jnp.where(seen > f, 1.0 / seen.astype(F32), 0.0)

        item_spec = pl.BlockSpec((1, tokens, channels), lambda i: (i, 0, 0))
        item_type = jax.ShapeDtypeStruct((items, tokens, channels), F32)
        frames_spec = pl.BlockSpec(
            (1, frame_total, rows_local, width, channels), lambda i: (i, 0, 0, 0, 0)
        )
        time_spec = whole((frame_total, channels))
        counts_spec = pl.BlockSpec(memory_space=pltpu.SMEM)
        row_spec = whole((1, channels))
        slab_bytes = tokens * channels * 4
        wave_flops = 2 * wave_rows * tokens * channels

        def head_body(counts_ref, frames_ref, time_ref, gain_ref, shift_ref, table_ref, merged_ref, parts_ref):
            item = pl.program_id(0)
            merged = 0.0
            for f in range(frame_total):
                frame = frames_ref[0, f].reshape(tokens, channels)
                merged = merged + frame * (live_row(counts_ref, item, f) * time_ref[f : f + 1, :])
            merged_ref[0] = merged
            unit, _ = normalise(merged)
            normed = unit * gain_ref[...] + shift_ref[...]
            put_parts(parts_ref, dot_full(table_ref[...], normed))

        merged, head_parts = call(
            head_body,
            (items,),
            [counts_spec, frames_spec, time_spec, row_spec, row_spec, whole(wave_fwd.shape)],
            [item_spec, parts_spec],
            [item_type, parts_type(items)],
            6 * items * wave_flops,
            items * slab_bytes * (frame_total + 2),
            "head",
        )(counts, frames, time_weight, gain_one, shift_one, wave_fwd)
        done(merged)
        columns = to_columns(exchange(to_send(head_parts, items)), items)

        far = arrived[:shard]
        batches = [seq(both_near), jnp.concatenate([far, flip(seq(far), depth_bits[1])], axis=0)]

        def gather_plane(x):
            got = {0: x}
            for bit in plane_a:
                for m in list(got):
                    got[m | (1 << bit)] = flip(got[m], bit)
            return [got[m] for m in masks_a]

        shards = [gather_plane(batches[0])]

        cot_own = output_cotangent.reshape(items * tokens, channels)
        cot_other = flip(cot_own, core_bit)
        token_total = items * tokens
        block = tokens
        token_spec = pl.BlockSpec((block, channels), lambda i: (i, 0))
        half_flops = 2 * 3 * token_total * channels * half
        count = piece_total // 2
        up_spec = pl.BlockSpec((unit, channels), lambda *_: (0, 0))
        down_spec = pl.BlockSpec((unit, channels), lambda *_: (0, 1))
        scratch_one = [pltpu.VMEM((half, channels), BF16)] * 2
        scratch_two = [pltpu.VMEM((hidden_local, channels), BF16)] * 2

        def split_into(refs, high_ref, low_ref):
            @pl.when(pl.program_id(0) == 0)
            def _():
                for n, r in enumerate(refs):
                    cut = slice(n * unit, (n + 1) * unit)
                    high_ref[cut, :], low_ref[cut, :] = halves(r[...])

        def cot_body(g1_ref, g2_ref, *refs):
            w_refs, outs, (wh, wl) = refs[:piece_total], refs[piece_total:-2], refs[-2:]
            split_into(w_refs, wh, wl)
            w = (wh[...], wl[...])
            g1, g2 = halves(g1_ref[...]), halves(g2_ref[...])
            outs[0][...] = dot_pairs(g1, w, NT)
            outs[1][...] = dot_pairs(g2, w, NT)
            if len(outs) > 2:
                outs[2][...], outs[3][...] = g1
                outs[4][...], outs[5][...] = g2

        def cot_call(w, extra):
            spec = pl.BlockSpec((block, half), lambda i: (i, 0))
            kind = jax.ShapeDtypeStruct((token_total, half), F32)
            slim_kind = jax.ShapeDtypeStruct((token_total, channels), BF16)
            out = call(
                cot_body,
                (items,),
                [token_spec, token_spec] + [down_spec] * piece_total,
                [spec, spec] + [token_spec] * extra,
                [kind, kind] + [slim_kind] * extra,
                2 * half_flops,
                token_total * (half + channels) * 8,
                "cotangent_up",
                scratch_one,
            )(cot_own, cot_other, seq(w[0]), *w[1:])
            done(out[0])
            return out

        mode_spec = pl.BlockSpec((mode_rows, 2 * lanes), lambda i: (i, 0))
        mode_type = jax.ShapeDtypeStruct((items * mode_rows, 2 * lanes), F32)
        square = (2 * lanes, 2 * lanes)
        weight_spec = whole(square)
        bias_spec = whole((2, 1, 2 * lanes))
        mix_flops = 2 * items * (2 * mode_rows * 4 * lanes * lanes + 2 * col.size * kept * lanes)

        def mix_body(x_ref, w0_ref, w1_ref, b_ref, col_ref, col_t_ref, out_ref, z_ref, u_ref, v_ref):
            z = modes_rows(dot_full(col_ref[...], get_columns(x_ref)))
            z_ref[...] = z
            u = dot_full(z, w0_ref[...]) + b_ref[0]
            u_ref[...] = u
            v = dot_full(u * cdf(u), w1_ref[...]) + b_ref[1]
            v_ref[...] = v
            mixed = v - jnp.clip(v, -SHRINK, SHRINK)
            put_columns(out_ref, dot_split(col_t_ref[...], rows_modes(mixed)))

        first_gates = [batches[1]] if 1 else []
        if 2 == 1:
            first_gates += shards[0][1:]
        if 2 == 2:
            first_gates += [s for m, s in zip(masks_a, shards[0]) if m in [1 << b for b in plane_a]]
        if 0 == 0:
            shards.append(gather_plane(batches[1]))
        mixed = call(
            mix_body,
            (items,),
            [column_spec, weight_spec, weight_spec, bias_spec]
            + [whole(col.shape), whole(col_t_half.shape)],
            [column_spec, mode_spec, mode_spec, mode_spec],
            [column_type(items), mode_type, mode_type, mode_type],
            6 * mix_flops,
            items * slab_bytes * 4,
            "mix",
        )(after(seq(columns), *first_gates), *mix_weight, mix_bias, col, col_t_half)
        done(mixed[1])
        single = [1 << b for b in plane_a]
        near = [s for m, s in zip(masks_a, shards[1]) if m in single]
        rest = [s for m, s in zip(masks_a, shards[0]) if m and m not in single]
        a1 = {0: [], 1: near + rest, 2: near, 3: near[:1], 4: near[:1] + rest}[4]
        row_back = from_send(exchange(after(from_columns(mixed[0], items), *a1)), items)

        def spatial_body(parts_ref, merged_ref, gain_ref, shift_ref, table_ref, middle_ref, normed_ref):
            middle = merged_ref[0] + dot_split(table_ref[...], get_parts(parts_ref))
            middle_ref[0] = middle
            unit, _ = normalise(middle)
            normed_ref[0] = unit * gain_ref[...] + shift_ref[...]

        def spatial_call(parts, *gates):
            out = call(
                spatial_body,
                (items,),
                [parts_spec, item_spec, row_spec, row_spec, whole(wave_inv.shape)],
                [item_spec, item_spec],
                [item_type, item_type],
                3 * items * wave_flops,
                items * slab_bytes * 4,
                "spatial",
            )(after(seq(parts), *gates), merged, gain_two, shift_two, wave_inv)
            done(out[0])
            return out

        wide = (token_total, hidden_local)
        wide_half = jax.ShapeDtypeStruct(wide, BF16)
        slim_half = jax.ShapeDtypeStruct((token_total, channels), BF16)
        wide_spec = pl.BlockSpec((tokens, hidden_local), lambda i: (i, 0))

        def feed_body(n_ref, bias_ref, ga_ref, gb_ref, *refs):
            w_refs = refs[: 2 * piece_total]
            hh, hl, ph, pl_, grad_ref, bg_ref, nh, nl, wh_ref, wl_ref = refs[2 * piece_total :]
            split_into(w_refs, wh_ref, wl_ref)

            @pl.when(pl.program_id(0) == 0)
            def _():
                bg_ref[...] = jnp.zeros_like(bg_ref)

            n = halves(n_ref[0])
            nh[...], nl[...] = n
            grad = 0.0
            for q in range(4):
                cut = slice(q * quarter, (q + 1) * quarter)
                w = (wh_ref[cut, :], wl_ref[cut, :])
                g_cut = slice(q % 2 * quarter, (q % 2 + 1) * quarter)
                raised = (ga_ref, gb_ref)[q // 2][:, g_cut]
                pre = dot_pairs(n, w, NT) + bias_ref[:, cut]
                phi = cdf(pre)
                hh[:, cut], hl[:, cut] = halves(pre * phi)
                gp = raised * (phi + pre * density(pre))
                bg_ref[:, cut] += jnp.sum(gp, axis=0, keepdims=True)
                gp = halves(gp)
                ph[:, cut], pl_[:, cut] = gp
                grad = grad + dot_pairs(gp, w, NN)
            grad_ref[0] = grad

        def feed_call(side, n):
            out = call(
                feed_body,
                (items,),
                [item_spec, whole((1, hidden_local))]
                + [pl.BlockSpec((tokens, half), lambda i: (i, 0))] * 2
                + [up_spec] * (2 * piece_total),
                [wide_spec] * 4
                + [item_spec, whole((1, hidden_local))]
                + [token_spec] * 2,
                [wide_half] * 4
                + [item_type, jax.ShapeDtypeStruct((1, hidden_local), F32)]
                + [slim_half] * 2,
                2 * 2 * 3 * token_total * channels * hidden_local,
                token_total * (hidden_local * 3 + channels * 3) * 4,
                f"feed_forward{side}",
                scratch_two,
            )(seq(n), bias_local, raised[0][side], raised[1][side], *shards[0], *shards[1])
            done(out[4])
            return out

        def middle_body(
            mid_ref, g1_ref, g2_ref, cot_ref, gain_ref, table_ref, gm_ref, parts_ref, small_ref
        ):
            unit, scale = normalise(mid_ref[0])
            grad = g1_ref[0] + g2_ref[0]
            cot = cot_ref[...]
            gm = cot + normal_back(unit, scale, grad * gain_ref[...])
            gm_ref[0] = gm
            put_parts(parts_ref, dot_split(table_ref[...], gm))

            @pl.when(pl.program_id(0) == 0)
            def _():
                small_ref[...] = jnp.zeros_like(small_ref)

            small_ref[0:1, :] += jnp.sum(grad * unit, axis=0, keepdims=True)
            small_ref[1:2, :] += jnp.sum(grad, axis=0, keepdims=True)
            small_ref[2:3, :] += jnp.sum(cot, axis=0, keepdims=True)

        small_type = jax.ShapeDtypeStruct((8, channels), F32)
        small_spec = whole((8, channels))

        if 0 == 1:
            shards.append(gather_plane(after(batches[1], mixed[1])))
        raised = [cot_call(shards[0], 4), cot_call(shards[1], 0)]
        middle, normed_own = spatial_call(row_back)
        normed_other = flip(normed_own, core_bit)
        fed = [feed_call(0, normed_own), feed_call(1, normed_other)]
        grad_middle, middle_parts, small_two = call(
            middle_body,
            (items,),
            [item_spec] * 3 + [token_spec, row_spec, whole(wave_inv_t.shape)],
            [item_spec, parts_spec, small_spec],
            [item_type, parts_type(items), small_type],
            3 * items * wave_flops,
            items * slab_bytes * 6,
            "middle_back",
        )(middle, fed[0][4], seq(flip(fed[1][4], core_bit)), cot_own, gain_two, wave_inv_t)
        done(small_two)
        grad_columns = to_columns(exchange(to_send(middle_parts, items)), items)

        lane_block = unit % lanes == 0
        wide_count = count if lane_block else 1

        def outer_body(*refs):
            out_c, out_e = refs[-2:]
            contract_out, expand_out = 0.0, 0.0
            per_side = 2 * wide_count + 6
            for s in range(2):
                mine = refs[per_side * s : per_side * (s + 1)]
                h = tuple(
                    jnp.concatenate(
                        [r[...] for r in mine[n * wide_count : (n + 1) * wide_count]], axis=1
                    )
                    for n in range(2)
                )
                ph, pl_, gh, gl, nh, nl = [r[...] for r in mine[2 * wide_count :]]
                contract_out += dot_pairs(h, (gh, gl), TN)
                expand_out += dot_pairs((ph, pl_), (nh, nl), TN)
            there = refs[2 * per_side : -2]
            if there:
                contract_out += there[0][...]
                expand_out += there[1][...]
            out_c[...], out_e[...] = contract_out, expand_out

        def outer_call(side, there=()):
            picks = place_a[side * count : (side + 1) * count]

            def unit_spec(p):
                return pl.BlockSpec((token_total, unit), lambda b: (0, b * piece_total + p))

            def gathered(x):
                return jnp.concatenate(
                    [
                        x[:, b * half + p * unit : b * half + (p + 1) * unit]
                        for b in range(2)
                        for p in picks
                    ],
                    axis=1,
                )

            def half_of(x):
                return jnp.concatenate(
                    [x[:, b * half + side * quarter :][:, :quarter] for b in range(2)], axis=1
                )

            specs, operands = [], []
            slim_spec = whole((token_total, channels))
            for s in range(2):
                values = fed[s]
                if lane_block:
                    specs += [unit_spec(p) for p in picks] * 2
                    specs += [
                        pl.BlockSpec((token_total, quarter), lambda b: (0, b * 2 + side))
                    ] * 2
                    operands += [values[0]] * count + [values[1]] * count + list(values[2:4])
                else:
                    specs += [whole((token_total, half))] * 4
                    operands += [gathered(v) for v in values[:2]]
                    operands += [half_of(v) for v in values[2:4]]
                specs += [slim_spec] * 4
                operands += list(raised[0][2 + 2 * s : 4 + 2 * s]) + list(values[6:8])
            operands[0] = seq(operands[0])
            rows = quarter if lane_block else half
            row_block = pl.BlockSpec((rows, channels), lambda b: (b, 0))
            kind = jax.ShapeDtypeStruct((half, channels), F32)
            out = call(
                outer_body,
                (half // rows,),
                specs + [row_block] * len(there),
                [row_block] * 2,
                [kind, kind],
                4 * half_flops,
                token_total * (half + channels) * 16,
                f"weight_grads{side}",
            )(*operands, *there)
            done(out[0])
            return out

        leaving = outer_call(1)
        contract_there = flip(leaving[0], plane_b[-1])
        expand_there = flip(leaving[1], plane_a[-1])

        def contract_calls():
            def down_body(hh, hl, *refs):
                extra = refs[: -3 - 2 * piece_total]
                w_refs, (out_ref, wh_ref, wl_ref) = refs[-3 - 2 * piece_total : -3], refs[-3:]
                split_into(w_refs, wh_ref, wl_ref)
                out = dot_pairs((hh[...], hl[...]), (wh_ref[...], wl_ref[...]), NN)
                if extra:
                    out = out + extra[0][0] + extra[1][0] + extra[2][...]
                out_ref[0] = out

            def down_call(side, extra, specs):
                out = call(
                    down_body,
                    (items,),
                    [wide_spec] * 2 + specs + [down_spec] * (2 * piece_total),
                    item_spec,
                    item_type,
                    2 * 3 * token_total * channels * hidden_local,
                    token_total * (hidden_local + channels) * 4,
                    f"contract{side}",
                    scratch_two,
                )(seq(fed[side][0]), fed[side][1], *extra, *shards[0], *shards[1])
                done(out)
                return out

            return down_call

        down_call = contract_calls()

        def finish_output(there):
            extra = [middle, there, as_row(contract_bias)]
            return down_call(0, extra, [item_spec, item_spec, row_spec])

        if 2:
            there = flip(down_call(1, [], []), core_bit)
        if 2 == 1:
            block_out = finish_output(there)

        def mix_back_body(
            x_ref, z_ref, u_ref, v_ref, w0_ref, w1_ref, col_ref, col_t_ref, out_ref, wg_ref, bg_ref, sum_ref
        ):
            step = pl.program_id(0)
            grad = modes_rows(dot_split(col_ref[...], get_columns(x_ref)))
            e1 = jnp.where(jnp.abs(v_ref[...]) > SHRINK, grad, 0.0)
            u = u_ref[...]
            phi = cdf(u)
            e1_half = halves(e1)
            e0 = dot_pairs(e1_half, halves(w1_ref[...]), NT) * (phi + u * density(u))
            e0_half = halves(e0)
            dz = dot_pairs(e0_half, halves(w0_ref[...]), NT)
            put_columns(out_ref, dot_split(col_t_ref[...], rows_modes(dz)))

            @pl.when(step == 0)
            def _():
                sum_ref[...] = jnp.zeros_like(sum_ref)
                bg_ref[...] = jnp.zeros_like(bg_ref)

            sum_ref[0] += dot_pairs(halves(z_ref[...]), e0_half, TN)
            sum_ref[1] += dot_pairs(halves(u * phi), e1_half, TN)
            bg_ref[0] += jnp.sum(e0, axis=0, keepdims=True)
            bg_ref[1] += jnp.sum(e1, axis=0, keepdims=True)

            @pl.when(step == items - 1)
            def _():
                for layer in range(2):
                    w = sum_ref[layer]
                    real = w[:lanes, :lanes] + w[lanes:, lanes:]
                    imag = w[:lanes, lanes:] - w[lanes:, :lanes]
                    for b in range(2):
                        cut = slice(b * block_size, (b + 1) * block_size)
                        wg_ref[layer, b, 0] = real[cut, cut]
                        wg_ref[layer, b, 1] = imag[cut, cut]

        grad_shape = (2, 2, 2, block_size, block_size)
        back_parts, mix_grad, big_bias = call(
            mix_back_body,
            (items,),
            [column_spec, mode_spec, mode_spec, mode_spec, weight_spec, weight_spec]
            + [whole(col_half.shape), whole(col_t_half.shape)],
            [column_spec, whole(grad_shape), bias_spec],
            [
                column_type(items),
                jax.ShapeDtypeStruct(grad_shape, F32),
                jax.ShapeDtypeStruct((2, 1, 2 * lanes), F32),
            ],
            3 * 2 * mix_flops,
            items * slab_bytes * 4,
            "mix_back",
            [pltpu.VMEM((2,) + square, F32)],
        )(seq(grad_columns), *mixed[1:], *mix_weight, col_half, col_t_half)
        done(big_bias)
        last_parts = from_send(exchange(from_columns(back_parts, items)), items)
        if 2 == 2:
            block_out = finish_output(there)
        staying = outer_call(0, (contract_there, expand_there))
        if 2 == 3:
            block_out = finish_output(there)
        if 2 == 0:
            block_out = finish_output(flip(down_call(1, [], []), core_bit))
        by_batch = lambda x: x.reshape(2, quarter, channels)
        contract_part = scatter_stages(by_batch(staying[0]), plane_b[:-1], 1)
        expand_part = scatter_stages(by_batch(staying[1]), plane_a[:-1], 1)

        mix_grad = mix_grad.reshape(mixing_count, -1, lanes)
        mix_grad = turn_axes(mixing_order(mix_grad, mixing_index))
        mix_grad = scatter_stages(mix_grad, mixing_low)
        joined = jnp.concatenate([expand_part, contract_part], axis=2)
        both_grad = scatter_stages(joined, depth_bits[1:], 1).reshape(2 * shard, 2 * channels)
        leaving_last = jnp.concatenate(
            [both_grad[shard:], mix_grad[1].reshape(-1, 2 * channels)], axis=0
        )
        arrived_last = flip(after(leaving_last, last_parts), depth_bits[0])
        both_grad = both_grad[:shard] + arrived_last[:shard]
        mixing_weight_grad = mix_grad[0].reshape(mixing_weight.shape) + arrived_last[
            shard:
        ].reshape(mixing_weight.shape)
        expand_weight_grad = both_grad[:, :channels].T
        contract_weight_grad = both_grad[:, channels:]

        def final_body(
            counts_ref,
            parts_ref,
            merged_ref,
            *refs,
        ):
            gm_ref, frames_ref, gain_ref, table_ref, total_ref, small_ref = refs
            item = pl.program_id(0)
            grad = dot_split(table_ref[...], get_parts(parts_ref))
            unit, scale = normalise(merged_ref[0])
            gm = gm_ref[0] + normal_back(unit, scale, grad * gain_ref[...])
            total_ref[0] = gm

            @pl.when(item == 0)
            def _():
                small_ref[...] = jnp.zeros_like(small_ref)

            small_ref[frame_total : frame_total + 1, :] += jnp.sum(
                grad * unit, axis=0, keepdims=True
            )
            small_ref[frame_total + 1 : frame_total + 2, :] += jnp.sum(
                grad, axis=0, keepdims=True
            )
            for f in range(frame_total):
                live = live_row(counts_ref, item, f)
                frame = frames_ref[0, f].reshape(tokens, channels)
                small_ref[f : f + 1, :] += live * jnp.sum(frame * gm, axis=0, keepdims=True)

        grad_merged, small_one = call(
            final_body,
            (items,),
            [counts_spec, parts_spec, item_spec, item_spec]
            + [frames_spec, row_spec, whole(wave_fwd_t.shape)],
            [item_spec, small_spec],
            [item_type, small_type],
            3 * items * wave_flops,
            items * slab_bytes * (4 + frame_total),
            "final",
        )(
            counts,
            seq(last_parts),
            merged,
            grad_middle,
            frames,
            gain_one,
            wave_fwd_t,
        )
        done(small_one)

        def frames_body(counts_ref, gm_ref, time_ref, out_ref):
            item = pl.program_id(0)
            gm = gm_ref[0]
            for f in range(frame_total):
                factor = live_row(counts_ref, item, f) * time_ref[f : f + 1, :]
                out_ref[0, f] = (gm * factor).reshape(rows_local, width, channels)

        frames_grad = call(
            frames_body,
            (items,),
            [counts_spec, item_spec, time_spec],
            frames_spec,
            jax.ShapeDtypeStruct(frames.shape, F32),
            0,
            items * slab_bytes * (1 + frame_total),
            "frames_grad",
        )(counts, seq(grad_merged), time_weight)

        bias_grad_local = fed[0][5] + fed[1][5]
        bias_full = jnp.zeros((2, 2, PAIRS, lanes), F32)
        bias_full = lax.dynamic_update_slice(
            bias_full, big_bias.reshape(2, 2, 1, lanes), (0, 0, pair, 0)
        ).reshape(4, channels)
        hidden_bias = jnp.dot(
            pick.T, bias_grad_local.reshape(-1, shard), precision=HIGHEST
        ).reshape(-1, channels)
        late = total(
            jnp.concatenate(
                [small_one[: frame_total + 2], small_two[:3], bias_full, hidden_bias], axis=0
            )
        )
        at = frame_total

        return (
            block_out.reshape(output_cotangent.shape),
            frames_grad,
            late[:at],
            late[at],
            late[at + 1],
            mixing_weight_grad,
            late[at + 5 : at + 9],
            late[at + 2],
            late[at + 3],
            expand_weight_grad,
            late[at + 9 :].reshape(hidden_total),
            contract_weight_grad,
            late[at + 4],
        )

    return local


def solution(mesh):
    return jax.shard_map(
        build(mesh.shape["rows"], mesh.shape["items"]),
        mesh=mesh,
        in_specs=(
            P("items", None, "rows", None, None),
            P("items"),
            P(),
            P(),
            P(),
            P(("rows", "items"), None),
            P(),
            P(),
            P(),
            P(None, ("rows", "items")),
            P(),
            P(("rows", "items"), None),
            P(),
            P("items", "rows", None, None),
        ),
        out_specs=(
            P("items", "rows", None, None),
            P("items", None, "rows", None, None),
            P(),
            P(),
            P(),
            P(("rows", "items"), None),
            P(),
            P(),
            P(),
            P(None, ("rows", "items")),
            P(),
            P(("rows", "items"), None),
            P(),
        ),
        check_vma=False,
    )
```

time: 338 us -> 245 us (0.72)
  waiting for transfers between devices: 159 us -> 80.6 us
  other arithmetic: 17.3 us -> 7.62 us
    ppermute x32 -> x23, waiting for transfers between devices: 150 us -> 66.9 us  [flip(): return lax.ppermute(x, AXES, pairs)]
    ppermute x0 -> x7, starting transfers between devices: none -> 8.08 us  [flip_mask(): return lax.ppermute(x, AXES, pairs)]
    ppermute x32 -> x23, starting transfers between devices: 32.6 us -> 24.8 us  [flip(): return lax.ppermute(x, AXES, pairs)]
    ppermute x0 -> x7, waiting for transfers between devices: none -> 6.85 us  [flip_mask(): return lax.ppermute(x, AXES, pairs)]
    concatenate x8 -> x2, other arithmetic: 6.53 us -> 0.01 us  [gather_stages(): x = jnp.concatenate([x, flip(x, bit)], axis=0)]
    slice x13 -> x7, local copies, waits for them, and re-layouts: 6.01 us -> 0.66 us  [the longest x1 0.6 us: local(): late[at + 4]]
    concatenate x3 -> x8, other arithmetic: 0.07 us -> 3.68 us  [the longest x1 0.99 us: local(): jnp.concatenate([both, mixing_weight.reshape(-1, 2 * channels)], axis=0)]
    unnamed x44 -> x55, local copies, waits for them, and re-layouts: 3.53 us -> 6.99 us
  transfers between devices with their start and end apart: 36 -> 34, of which waited for: 18 -> 19; matrix products, arithmetic and copies ran while one was open for 9% -> 6% of each run, Pallas kernels for 19% -> 28%
where the time goes in v2:
time: 245 us; the launch traced here: 244 us
  Pallas kernels  84.4 us (34%)
  waiting for transfers between devices  80.6 us (33%)
  starting transfers between devices  54.4 us (22%)
  local copies, waits for them, and re-layouts  15.7 us (6%)
  other arithmetic  7.62 us (3%)
    ppermute x23, waiting for transfers between devices, flip(): return lax.ppermute(x, AXES, pairs)  66.9 us
    ppermute x23, starting transfers between devices, flip(): return lax.ppermute(x, AXES, pairs)  24.8 us
    all_to_all x4, starting transfers between devices, exchange(): return lax.all_to_all(x.reshape(row_parts, -1, lanes), 'rows', 0, 0)  21.5 us
    pallas_call x2, Pallas kernels, feed_call(): call(feed_body, (items,), [item_spec, whole((1, hidden_local))] + [pl.Blo...  17.9 us
    pallas_call x2, Pallas kernels, outer_call(): call(outer_body, (half // rows,), specs + [row_block] * len(there), [row_...  15.3 us
    pallas_call x2, Pallas kernels, down_call(): call(down_body, (items,), [wide_spec] * 2 + specs + [down_spec] * (2 * pi...  10.4 us
    pallas_call x2, Pallas kernels, cot_call(): call(cot_body, (items,), [token_spec, token_spec] + [down_spec] * piece_t...  9.2 us
    ppermute x7, starting transfers between devices, flip_mask(): return lax.ppermute(x, AXES, pairs)  8.08 us
  transfers between devices with their start and end apart: 34, of which 19 were waited for; matrix products, arithmetic and copies ran while one was open for 6% of the time, Pallas kernels for 28%

profile of v2, /device:TPU:0, one launch (start us, length us, event | category | flops | bytes accessed | tf_op | source)
XLA Modules:
  0.0 244.5 jit_solution(14782372042804400222)
XLA Ops:
  9.3 4.3 %head.1 = (f32[2,256,512]{2,1,0:T(8,128)}, f32[2,4,2,2,64,128]{5,4,3,2,1,0:T(8,128)}) custom-call(s32[2]{0:T(128)} %counts_ref.5, f32[2,4,4,64,512]{4,3,2,1,0:T(8,128)} %refs_1_.1, f32[4,512]{1,0:T(4,128)} %time_ref.3, f32[1,512]{1,0:T(1,128)} %bitcast.117, f32[1,512]{1,0:T(1,128)} %bitcast.121, f32[256,256]{1,0:T(8,128)} %constant.96.clone.table_ref), custom_call_target="tpu_custom_call" | custom-call | flops 805306 | bytes 6291 | tf_op jit(solution)/shard_map/head/pallas_call | solution.py:433
  13.6 4.4 %all-to-all-start = ((f32[16,128,128]{2,1,0:T(8,128)}), f32[16,128,128]{2,1,0:T(8,128)}, u32[]{:S(2)}, u32[]{:S(2)}) async-start(f32[16,128,128]{2,1,0:T(8,128)} %bitcast.98), calls=%async_computation | async-start | bytes 2097152 | tf_op jit(solution)/shard_map/all_to_all | solution.py:351
  26.4 17.1 %collective-permute-done.1 = f32[64,1024]{1,0:T(8,128)S(1)} collective-permute-done((f32[64,1024]{1,0:T(8,128)S(1)}, f32[64,1024]{1,0:T(8,128)S(1)}, u32[]{:S(2)}, u32[]{:S(2)}) %collective-permute-start.1) | collective-permute-done | bytes 262176 | tf_op jit(solution)/shard_map/ppermute | solution.py:148
  47.7 5.9 %mix.1 = (f32[16,2,8,8,128]{4,3,2,1,0:T(8,128)}, f32[512,256]{1,0:T(8,128)}, f32[512,256]{1,0:T(8,128)}, f32[512,256]{1,0:T(8,128)}) custom-call(f32[16,2,8,8,128]{4,3,2,1,0:T(8,128)} %bitcast.3.x_ref, f32[256,256]{1,0:T(8,128)} %get-tuple-element.162.w0_ref, f32[256,256]{1,0:T(8,128)} %get-tuple-element.163.w1_ref, f32[2,1,256]{2,1,0:T(1,128)} %bitcast.119, ...), custom_call_target="tpu_custom_call" | custom-call | flops 1207959 | bytes 4194 | tf_op jit(solution)/shard_map/mix/pallas_call | solution.py:530
  58.3 4.5 %all-to-all-start.1 = ((f32[16,128,128]{2,1,0:T(8,128)}), f32[16,128,128]{2,1,0:T(8,128)}, u32[]{:S(2)}, u32[]{:S(2)}) async-start(f32[16,128,128]{2,1,0:T(8,128)} %bitcast.100), calls=%async_computation.1 | async-start | bytes 2097152 | tf_op jit(solution)/shard_map/all_to_all | solution.py:351
  66.7 4.7 %cotangent_up.2 = (f32[512,512]{1,0:T(8,128)}, f32[512,512]{1,0:T(8,128)}, bf16[512,512]{1,0:T(8,128)(2,1)}, bf16[512,512]{1,0:T(8,128)(2,1)}, bf16[512,512]{1,0:T(8,128)(2,1)}, /*index=5*/bf16[512,512]{1,0:T(8,128)(2,1)}) custom-call(f32[512,512]{1,0:T(8,128)} %bitcast.85, f32[512,512]{1,0:T(8,128)} %copy-done.12, f32[128,1024]{1,0:T(8,128)} %copy-done.2, ...), custom_call_target="tpu_custom_call" | custom-call | flops 1610612 | bytes 4194 | tf_op jit(solution)/shard_map/cotangent_up/pallas_call | solution.py:492
  71.4 6.2 %collective-permute-done.10.refs_2_.refs_6_.refs_9_ = f32[128,1024]{1,0:T(8,128)S(1)} collective-permute-done((f32[128,1024]{1,0:T(8,128)S(1)}, f32[128,1024]{1,0:T(8,128)S(1)}, u32[]{:S(2)}, u32[]{:S(2)}) %collective-permute-start.10) | collective-permute-done | bytes 524320 | tf_op jit(solution)/shard_map/ppermute | solution.py:148
  77.7 10.8 %collective-permute-done.11.refs_3_.refs_7_.refs_10_ = f32[128,1024]{1,0:T(8,128)S(1)} collective-permute-done((f32[128,1024]{1,0:T(8,128)S(1)}, f32[128,1024]{1,0:T(8,128)S(1)}, u32[]{:S(2)}, u32[]{:S(2)}) %collective-permute-start.11) | collective-permute-done | bytes 524320 | tf_op jit(solution)/shard_map/ppermute | solution.py:148
  89.3 4.5 %cotangent_up.3 = (f32[512,512]{1,0:T(8,128)}, f32[512,512]{1,0:T(8,128)}) custom-call(f32[512,512]{1,0:T(8,128)} %bitcast.86, f32[512,512]{1,0:T(8,128)} %copy-done.12, f32[128,1024]{1,0:T(8,128)} %copy-done.3, f32[128,1024]{1,0:T(8,128)} %copy-done.6, f32[128,1024]{1,0:T(8,128)} %copy-done.8, f32[128,1024]{1,0:T(8,128)} %copy-done.9), custom_call_target="tpu_custom_call" | custom-call | flops 1610612 | bytes 4194 | tf_op jit(solution)/shard_map/cotangent_up/pallas_call | solution.py:492
  98.0 8.9 %feed_forward0.1 = (bf16[512,1024]{1,0:T(8,128)(2,1)}, bf16[512,1024]{1,0:T(8,128)(2,1)}, bf16[512,1024]{1,0:T(8,128)(2,1)}, bf16[512,1024]{1,0:T(8,128)(2,1)}, ...) custom-call(f32[2,256,512]{2,1,0:T(8,128)} %get-tuple-element.92.n_ref, ...), custom_call_target="tpu_custom_call" | custom-call | flops 3221225 | bytes 9437 | tf_op jit(solution)/shard_map/feed_forward0/pallas_call | solution.py:601
  108.0 8.9 %feed_forward1.1 = (bf16[512,1024]{1,0:T(8,128)(2,1)}, bf16[512,1024]{1,0:T(8,128)(2,1)}, bf16[512,1024]{1,0:T(8,128)(2,1)}, bf16[512,1024]{1,0:T(8,128)(2,1)}, ...) custom-call(f32[2,256,512]{2,1,0:T(8,128)} %copy-done.16, ...), custom_call_target="tpu_custom_call" | custom-call | flops 3221225 | bytes 9437 | tf_op jit(solution)/shard_map/feed_forward1/pallas_call | solution.py:601
  121.0 4.4 %middle_back.1 = (f32[2,256,512]{2,1,0:T(8,128)}, f32[2,4,2,2,64,128]{5,4,3,2,1,0:T(8,128)}, f32[8,512]{1,0:T(8,128)}) custom-call(f32[2,256,512]{2,1,0:T(8,128)} %get-tuple-element.91.mid_ref.refs_0_, f32[2,256,512]{2,1,0:T(8,128)} %get-tuple-element.94.g1_ref, f32[2,256,512]{2,1,0:T(8,128)} %copy-done.18, f32[512,512]{1,0:T(8,128)} %bitcast.87, ...), custom_call_target="tpu_custom_call" | custom-call | flops 402653 | bytes 6291 | tf_op jit(solution)/shard_map/middle_back/pallas_call | solution.py:648
  125.3 5.7 %all-to-all-start.2 = ((f32[16,128,128]{2,1,0:T(8,128)}), f32[16,128,128]{2,1,0:T(8,128)S(1)}, u32[]{:S(2)}, u32[]{:S(2)}) async-start(f32[16,128,128]{2,1,0:T(8,128)} %bitcast.101), calls=%async_computation.2 | async-start | bytes 2097152 | tf_op jit(solution)/shard_map/all_to_all | solution.py:351
  131.1 7.5 %weight_grads1.1 = (f32[512,512]{1,0:T(8,128)}, f32[512,512]{1,0:T(8,128)}) custom-call(bf16[512,1024]{1,0:T(8,128)(2,1)} %get-tuple-element.126.refs_0_.refs_1_.hh, bf16[512,1024]{1,0:T(8,128)(2,1)} %get-tuple-element.126.refs_0_.refs_1_.hh, bf16[512,1024]{1,0:T(8,128)(2,1)} %get-tuple-element.104.refs_2_.refs_3_.hl, ...), custom_call_target="tpu_custom_call" | custom-call | flops 3221225 | bytes 8388 | tf_op jit(solution)/shard_map/weight_grads1/pallas_call | solution.py:726
  138.6 5.0 %contract1.1 = f32[2,256,512]{2,1,0:T(8,128)} custom-call(bf16[512,1024]{1,0:T(8,128)(2,1)} %get-tuple-element.119.refs_10_.refs_11_.hh, bf16[512,1024]{1,0:T(8,128)(2,1)} %get-tuple-element.111.refs_12_.refs_13_.hl, f32[128,1024]{1,0:T(8,128)} %copy-done.2, f32[128,1024]{1,0:T(8,128)} %copy-done.5, f32[128,1024]{1,0:T(8,128)} %copy-done.4, ...), custom_call_target="tpu_custom_call" | custom-call | flops 1610612 | bytes 3145 | tf_op jit(solution)/shard_map/contract1/pallas_call | solution.py:754
  147.3 6.8 %all-to-all-done.2 = f32[16,128,128]{2,1,0:T(8,128)S(1)} async-done(((f32[16,128,128]{2,1,0:T(8,128)}), f32[16,128,128]{2,1,0:T(8,128)S(1)}, u32[]{:S(2)}, u32[]{:S(2)}) %all-to-all-start.2) | async-done | bytes 1048608 | tf_op jit(solution)/shard_map/all_to_all | solution.py:351
  155.1 5.7 %mix_back.1 = (f32[16,2,8,8,128]{4,3,2,1,0:T(8,128)}, f32[2,2,2,64,64]{4,3,2,1,0:T(8,128)}, f32[2,1,256]{2,1,0:T(1,128)}) custom-call(f32[16,2,8,8,128]{4,3,2,1,0:T(8,128)} %bitcast.88, f32[512,256]{1,0:T(8,128)} %get-tuple-element.84.z_ref, f32[512,256]{1,0:T(8,128)} %get-tuple-element.121.u_ref, f32[512,256]{1,0:T(8,128)} %get-tuple-element.122.v_ref, ...), custom_call_target="tpu_custom_call" | custom-call | flops 1207959 | bytes 4194 | tf_op jit(solution)/shard_map/mix_back/pallas_call | solution.py:817
  160.8 6.9 %all-to-all-start.3 = ((f32[16,128,128]{2,1,0:T(8,128)}), f32[16,128,128]{2,1,0:T(8,128)S(1)}, u32[]{:S(2)}, u32[]{:S(2)}) async-start(f32[16,128,128]{2,1,0:T(8,128)} %bitcast.99), calls=%async_computation.3 | async-start | bytes 2097152 | tf_op jit(solution)/shard_map/all_to_all | solution.py:351
  168.8 5.5 %contract0.1 = f32[2,256,512]{2,1,0:T(8,128)} custom-call(bf16[512,1024]{1,0:T(8,128)(2,1)} %get-tuple-element.126.refs_0_.refs_1_.hh, bf16[512,1024]{1,0:T(8,128)(2,1)} %get-tuple-element.104.refs_2_.refs_3_.hl, f32[2,256,512]{2,1,0:T(8,128)} %get-tuple-element.91.mid_ref.refs_0_, f32[2,256,512]{2,1,0:T(8,128)} %collective-permute-done.14.refs_1_, ...), custom_call_target="tpu_custom_call" | custom-call | flops 1610612 | bytes 3145 | tf_op jit(solution)/shard_map/contract0/pallas_call | solution.py:754
  177.4 7.8 %weight_grads0.1 = (f32[512,512]{1,0:T(8,128)}, f32[512,512]{1,0:T(8,128)}) custom-call(bf16[512,1024]{1,0:T(8,128)(2,1)} %get-tuple-element.126.refs_0_.refs_1_.hh, bf16[512,1024]{1,0:T(8,128)(2,1)} %get-tuple-element.126.refs_0_.refs_1_.hh, bf16[512,1024]{1,0:T(8,128)(2,1)} %get-tuple-element.104.refs_2_.refs_3_.hl, ...), custom_call_target="tpu_custom_call" | custom-call | flops 3221225 | bytes 8388 | tf_op jit(solution)/shard_map/weight_grads0/pallas_call | solution.py:726
  191.0 10.4 %collective-permute-done.26 = f32[2,128,512]{2,1,0:T(8,128)S(1)} collective-permute-done((f32[2,128,512]{2,1,0:T(8,128)S(1)}, f32[2,128,512]{2,1,0:T(8,128)S(1)}, u32[]{:S(2)}, u32[]{:S(2)}) %collective-permute-start.26) | collective-permute-done | bytes 524320 | tf_op jit(solution)/shard_map/ppermute | solution.py:148
  207.3 4.7 %final.1 = (f32[2,256,512]{2,1,0:T(8,128)}, f32[8,512]{1,0:T(8,128)}) custom-call(s32[2]{0:T(128)} %counts_ref.5, f32[2,4,2,2,64,128]{5,4,3,2,1,0:T(8,128)} %bitcast.89, f32[2,256,512]{2,1,0:T(8,128)} %get-tuple-element.77.merged_ref, f32[2,256,512]{2,1,0:T(8,128)} %get-tuple-element.130.refs_0_, f32[2,4,4,64,512]{4,3,2,1,0:T(8,128)} %refs_1_.1, ...), custom_call_target="tpu_custom_call" | custom-call | flops 402653 | bytes 8388 | tf_op jit(solution)/shard_map/final/pallas_call | solution.py:890
  212.9 4.4 %collective-permute-done.28 = f32[2,64,1024]{2,1,0:T(8,128)S(1)} collective-permute-done((f32[2,64,1024]{2,1,0:T(8,128)S(1)}, f32[2,64,1024]{2,1,0:T(8,128)S(1)}, u32[]{:S(2)}, u32[]{:S(2)}) %collective-permute-start.28) | collective-permute-done | bytes 524320 | tf_op jit(solution)/shard_map/ppermute | solution.py:148
  233.5 4.2 %collective-permute-done.21 = f32[17,512]{1,0:T(8,128)S(1)} collective-permute-done((f32[17,512]{1,0:T(8,128)S(1)}, f32[17,512]{1,0:T(8,128)S(1)}, u32[]{:S(2)}, u32[]{:S(2)}) %collective-permute-start.21) | collective-permute-done | bytes 34848 | tf_op jit(solution)/shard_map/ppermute | solution.py:152
  (189 shorter events, 83.8 us)
Async XLA Ops:
  2.6 17.5 %collective-permute-start = (f32[68,1024]{1,0:T(8,128)S(1)}, f32[68,1024]{1,0:T(8,128)S(1)}, u32[]{:S(2)}, u32[]{:S(2)}) collective-permute-start(f32[68,1024]{1,0:T(8,128)S(1)} %pad_maximum_fusion.3), channel_id=1, source_target_pairs={{0,16},{1,17},{2,18},{3,19},{4,20},{5,21},{6,22},{7,23},{8,24},{9,... | collective-permute-start | bytes 835592 | tf_op jit(solution)/shard_map/ppermute | solution.py:148
  7.7 15.3 %collective-permute-start.2 = (f32[64,1024]{1,0:T(8,128)S(1)}, f32[64,1024]{1,0:T(8,128)S(1)}, u32[]{:S(2)}, u32[]{:S(2)}) collective-permute-start(f32[64,1024]{1,0:T(8,128)S(1)} %pad_maximum_fusion.5), channel_id=1, source_target_pairs={{0,8},{1,9},{2,10},{3,11},{4,12},{5,13},{6,14},{7,15},{8,0},{9,1},... | collective-permute-start | bytes 786440 | tf_op jit(solution)/shard_map/ppermute | solution.py:148
  13.6 34.0 %all-to-all-start = ((f32[16,128,128]{2,1,0:T(8,128)}), f32[16,128,128]{2,1,0:T(8,128)}, u32[]{:S(2)}, u32[]{:S(2)}) async-start(f32[16,128,128]{2,1,0:T(8,128)} %bitcast.98), calls=%async_computation | async-start | bytes 2097152 | tf_op jit(solution)/shard_map/all_to_all | solution.py:351
  23.1 24.6 %collective-permute-start.4 = (f32[128,1024]{1,0:T(8,128)S(1)}, f32[128,1024]{1,0:T(8,128)S(1)}, u32[]{:S(2)}, u32[]{:S(2)}) collective-permute-start(f32[128,1024]{1,0:T(8,128)S(1)} %pad_maximum_fusion.2.refs_0_.refs_3_), channel_id=1, source_target_pairs={{0,1},{1,0},{2,3},{3,2},{4,5},{5,4},{6,7},{7,6},{8,9},{9,8},{10,11... | collective-permute-start | bytes 1572872 | tf_op jit(solution)/shard_map/ppermute | solution.py:148
  23.6 21.5 %collective-permute-start.3 = (f32[128,1024]{1,0:T(8,128)S(1)}, f32[128,1024]{1,0:T(8,128)S(1)}, u32[]{:S(2)}, u32[]{:S(2)}) collective-permute-start(f32[128,1024]{1,0:T(8,128)S(1)} %pad_maximum_fusion.2.refs_0_.refs_3_), channel_id=1, source_target_pairs={{0,4},{1,5},{2,6},{3,7},{4,0},{5,1},{6,2},{7,3},{8,12},{9,13},{10,... | collective-permute-start | bytes 1572872 | tf_op jit(solution)/shard_map/ppermute | solution.py:148
  25.1 18.3 %collective-permute-start.1 = (f32[64,1024]{1,0:T(8,128)S(1)}, f32[64,1024]{1,0:T(8,128)S(1)}, u32[]{:S(2)}, u32[]{:S(2)}) collective-permute-start(f32[64,1024]{1,0:T(8,128)S(1)} %slice.152), channel_id=1, source_target_pairs={{0,8},{1,9},{2,10},{3,11},{4,12},{5,13},{6,14},{7,15},{8,0},{9,1},... | collective-permute-start | bytes 786440 | tf_op jit(solution)/shard_map/ppermute | solution.py:148
  43.5 13.5 %collective-permute-start.7 = (f32[128,1024]{1,0:T(8,128)S(1)}, f32[128,1024]{1,0:T(8,128)S(1)}, u32[]{:S(2)}, u32[]{:S(2)}) collective-permute-start(f32[128,1024]{1,0:T(8,128)S(1)} %pad_maximum_fusion.1.refs_0_.refs_4_.refs_7_), channel_id=1, source_target_pairs={{0,4},{1,5},{2,6},{3,7},{4,0},{5,1},{6,2},{7,3},{8,12},{9,13},{10,... | collective-permute-start | bytes 1572872 | tf_op jit(solution)/shard_map/ppermute | solution.py:148
  45.1 13.2 %collective-permute-start.8 = (f32[128,1024]{1,0:T(8,128)S(1)}, f32[128,1024]{1,0:T(8,128)S(1)}, u32[]{:S(2)}, u32[]{:S(2)}) collective-permute-start(f32[128,1024]{1,0:T(8,128)S(1)} %collective-permute-done.3.refs_1_.refs_4_), channel_id=1, source_target_pairs={{0,1},{1,0},{2,3},{3,2},{4,5},{5,4},{6,7},{7,6},{8,9},{9,8},{10,11... | collective-permute-start | bytes 1572872 | tf_op jit(solution)/shard_map/ppermute | solution.py:148
  58.3 35.5 %all-to-all-start.1 = ((f32[16,128,128]{2,1,0:T(8,128)}), f32[16,128,128]{2,1,0:T(8,128)}, u32[]{:S(2)}, u32[]{:S(2)}) async-start(f32[16,128,128]{2,1,0:T(8,128)} %bitcast.100), calls=%async_computation.1 | async-start | bytes 2097152 | tf_op jit(solution)/shard_map/all_to_all | solution.py:351
  62.9 14.8 %collective-permute-start.10 = (f32[128,1024]{1,0:T(8,128)S(1)}, f32[128,1024]{1,0:T(8,128)S(1)}, u32[]{:S(2)}, u32[]{:S(2)}) collective-permute-start(f32[128,1024]{1,0:T(8,128)S(1)} %pad_maximum_fusion.1.refs_0_.refs_4_.refs_7_), channel_id=1, source_target_pairs={{0,1},{1,0},{2,3},{3,2},{4,5},{5,4},{6,7},{7,6},{8,9},{9,8},{10,11... | collective-permute-start | bytes 1572872 | tf_op jit(solution)/shard_map/ppermute | solution.py:148
  64.5 24.0 %collective-permute-start.11 = (f32[128,1024]{1,0:T(8,128)S(1)}, f32[128,1024]{1,0:T(8,128)S(1)}, u32[]{:S(2)}, u32[]{:S(2)}) collective-permute-start(f32[128,1024]{1,0:T(8,128)S(1)} %collective-permute-done.7.refs_1_.refs_5_.refs_8_), channel_id=1, source_target_pairs={{0,1},{1,0},{2,3},{3,2},{4,5},{5,4},{6,7},{7,6},{8,9},{9,8},{10,11... | collective-permute-start | bytes 1572872 | tf_op jit(solution)/shard_map/ppermute | solution.py:148
  97.1 9.9 %collective-permute-start.12 = (f32[2,256,512]{2,1,0:T(8,128)}, f32[2,256,512]{2,1,0:T(8,128)S(1)}, u32[]{:S(2)}, u32[]{:S(2)}) collective-permute-start(f32[2,256,512]{2,1,0:T(8,128)} %get-tuple-element.92.n_ref), channel_id=1, source_target_pairs={{0,2},{1,3},{2,0},{3,1},{4,6},{5,7},{6,4},{7,5},{8,10},{9,11},{10,... | collective-permute-start | bytes 3145736 | tf_op jit(solution)/shard_map/ppermute | solution.py:148
  125.3 28.7 %all-to-all-start.2 = ((f32[16,128,128]{2,1,0:T(8,128)}), f32[16,128,128]{2,1,0:T(8,128)S(1)}, u32[]{:S(2)}, u32[]{:S(2)}) async-start(f32[16,128,128]{2,1,0:T(8,128)} %bitcast.101), calls=%async_computation.2 | async-start | bytes 2097152 | tf_op jit(solution)/shard_map/all_to_all | solution.py:351
  143.6 25.2 %collective-permute-start.14 = (f32[2,256,512]{2,1,0:T(8,128)}, f32[2,256,512]{2,1,0:T(8,128)}, u32[]{:S(2)}, u32[]{:S(2)}) collective-permute-start(f32[2,256,512]{2,1,0:T(8,128)} %contract1.1), channel_id=1, source_target_pairs={{0,2},{1,3},{2,0},{3,1},{4,6},{5,7},{6,4},{7,5},{8,10},{9,11},{10,... | collective-permute-start | bytes 3145736 | tf_op jit(solution)/shard_map/ppermute | solution.py:148
  144.0 30.4 %collective-permute-start.16 = (f32[512,512]{1,0:T(8,128)}, f32[512,512]{1,0:T(8,128)S(1)}, u32[]{:S(2)}, u32[]{:S(2)}) collective-permute-start(f32[512,512]{1,0:T(8,128)} %get-tuple-element.127), channel_id=1, source_target_pairs={{0,1},{1,0},{2,3},{3,2},{4,5},{5,4},{6,7},{7,6},{8,9},{9,8},{10,11... | collective-permute-start | bytes 3145736 | tf_op jit(solution)/shard_map/ppermute | solution.py:148
  145.5 31.9 %collective-permute-start.15 = (f32[512,512]{1,0:T(8,128)}, f32[512,512]{1,0:T(8,128)}, u32[]{:S(2)}, u32[]{:S(2)}) collective-permute-start(f32[512,512]{1,0:T(8,128)} %get-tuple-element.118), channel_id=1, source_target_pairs={{0,4},{1,5},{2,6},{3,7},{4,0},{5,1},{6,2},{7,3},{8,12},{9,13},{10,... | collective-permute-start | bytes 3145736 | tf_op jit(solution)/shard_map/ppermute | solution.py:148
  160.8 45.6 %all-to-all-start.3 = ((f32[16,128,128]{2,1,0:T(8,128)}), f32[16,128,128]{2,1,0:T(8,128)S(1)}, u32[]{:S(2)}, u32[]{:S(2)}) async-start(f32[16,128,128]{2,1,0:T(8,128)} %bitcast.99), calls=%async_computation.3 | async-start | bytes 2097152 | tf_op jit(solution)/shard_map/all_to_all | solution.py:351
  186.3 15.1 %collective-permute-start.26 = (f32[2,128,512]{2,1,0:T(8,128)S(1)}, f32[2,128,512]{2,1,0:T(8,128)S(1)}, u32[]{:S(2)}, u32[]{:S(2)}) collective-permute-start(f32[2,128,512]{2,1,0:T(8,128)S(1)} %split.51), channel_id=1, source_target_pairs={{0,4},{1,5},{2,6},{3,7},{4,0},{5,1},{6,2},{7,3},{8,12},{9,13},{10,... | collective-permute-start | bytes 1572872 | tf_op jit(solution)/shard_map/ppermute | solution.py:148
  189.8 13.7 %collective-permute-start.27 = (f32[2,128,512]{2,1,0:T(8,128)}, f32[2,128,512]{2,1,0:T(8,128)}, u32[]{:S(2)}, u32[]{:S(2)}) collective-permute-start(f32[2,128,512]{2,1,0:T(8,128)} %split.53), channel_id=1, source_target_pairs={{0,1},{1,0},{2,3},{3,2},{4,5},{5,4},{6,7},{7,6},{8,9},{9,8},{10,11... | collective-permute-start | bytes 1572872 | tf_op jit(solution)/shard_map/ppermute | solution.py:148
  190.9 15.3 %collective-permute-start.25 = (f32[2,32,128]{2,1,0:T(8,128)S(1)}, f32[2,32,128]{2,1,0:T(8,128)S(1)}, u32[]{:S(2)}, u32[]{:S(2)}) collective-permute-start(f32[2,32,128]{2,1,0:T(8,128)S(1)} %split.49), channel_id=1, source_target_pairs={{0,2},{1,3},{2,0},{3,1},{4,6},{5,7},{6,4},{7,5},{8,10},{9,11},{10,... | collective-permute-start | bytes 98312 | tf_op jit(solution)/shard_map/ppermute | solution.py:148
  204.7 12.6 %collective-permute-start.28 = (f32[2,64,1024]{2,1,0:T(8,128)S(1)}, f32[2,64,1024]{2,1,0:T(8,128)S(1)}, u32[]{:S(2)}, u32[]{:S(2)}) collective-permute-start(f32[2,64,1024]{2,1,0:T(8,128)S(1)} %pad_maximum_fusion), channel_id=1, source_target_pairs={{0,8},{1,9},{2,10},{3,11},{4,12},{5,13},{6,14},{7,15},{8,0},{9,1},... | collective-permute-start | bytes 1572872 | tf_op jit(solution)/shard_map/ppermute | solution.py:148
  224.3 9.1 %collective-permute-start.23 = (f32[17,512]{1,0:T(8,128)S(1)}, f32[17,512]{1,0:T(8,128)S(1)}, u32[]{:S(2)}, u32[]{:S(2)}) collective-permute-start(f32[17,512]{1,0:T(8,128)S(1)} %add_add_fusion.1), channel_id=1, source_target_pairs={{0,24},{1,25},{2,26},{3,27},{4,28},{5,29},{6,30},{7,31},{8,16},{9,... | collective-permute-start | bytes 104456 | tf_op jit(solution)/shard_map/ppermute | solution.py:152
  227.2 10.5 %collective-permute-start.21 = (f32[17,512]{1,0:T(8,128)S(1)}, f32[17,512]{1,0:T(8,128)S(1)}, u32[]{:S(2)}, u32[]{:S(2)}) collective-permute-start(f32[17,512]{1,0:T(8,128)S(1)} %add_add_fusion.1), channel_id=1, source_target_pairs={{0,16},{1,17},{2,18},{3,19},{4,20},{5,21},{6,22},{7,23},{8,24},{9,... | collective-permute-start | bytes 104456 | tf_op jit(solution)/shard_map/ppermute | solution.py:152
  228.8 14.2 %collective-permute-start.29 = (f32[68,1024]{1,0:T(8,128)S(1)}, f32[68,1024]{1,0:T(8,128)S(1)}, u32[]{:S(2)}, u32[]{:S(2)}) collective-permute-start(f32[68,1024]{1,0:T(8,128)S(1)} %pad_maximum_fusion.4), channel_id=1, source_target_pairs={{0,16},{1,17},{2,18},{3,19},{4,20},{5,21},{6,22},{7,23},{8,24},{9,... | collective-permute-start | bytes 835592 | tf_op jit(solution)/shard_map/ppermute | solution.py:148
  (36 other events, 429.6 us)

commit v3 on v2

--- a/solution.py
+++ b/solution.py
@@ -16,15 +16,23 @@
 EPS = 1e-05
 F32 = jnp.float32
 BF16 = jnp.bfloat16
-PLANNED = 0.001
 AXES = ("rows", "items")
 LIMIT = 56 * 1024 * 1024
 HALF_ROOT = math.sqrt(0.5)
 DENSITY = 1.0 / math.sqrt(2.0 * math.pi)
 
 
+HELD_NOW = {}
+
+
+def hold(x):
+    HELD_NOW[id(x)] = x
+    return x
+
+
 def after(x, *others):
-    return lax.optimization_barrier((x,) + others)[0]
+    out = lax.optimization_barrier((x,) + others)[0]
+    return hold(out) if id(x) in HELD_NOW else out
 
 
 def make_tables(grid_size, rows_local, row_parts):
@@ -35,8 +43,10 @@
     )
     step = 2.0 * np.pi / grid_size
     factor = 1.0 / np.sqrt(grid_size)
-    wide = (along[:, None] * n[None, :] % grid_size) * step
-    high = (across[:, None] * n[None, :] % grid_size) * step
+    angle = lambda k: (
+        (k[:, None] * n[None, :] % grid_size).astype(np.float32) * np.float32(step)
+    ).astype(np.float64)
+    wide, high = angle(along), angle(across)
     cos_w, sin_w = np.cos(wide) * factor, np.sin(wide) * factor
     cos_h, sin_h = np.cos(high) * factor, np.sin(high) * factor
     doubled = np.where(along == 0, 1.0, 2.0)[:, None]
@@ -114,6 +124,9 @@
 def call(body, grid, in_specs, out_specs, out_shape, flops, moved, name, scratch=()):
     many = isinstance(out_shape, (list, tuple))
     shapes = list(out_shape) if many else [out_shape]
+    vout = VOUT.get(name, ())
+    kinds = [pltpu.VMEM if n in vout else pltpu.HBM for n in range(len(shapes))]
+    shapes = [k(s.shape, s.dtype) for k, s in zip(kinds, shapes)]
     run = pl.pallas_call(
         body,
         grid=grid,
@@ -123,14 +136,32 @@
         scratch_shapes=list(scratch),
         name=name,
         cost_estimate=pl.CostEstimate(
-            flops=int(flops * PLANNED),
+            flops=int(flops),
             transcendentals=0,
-            bytes_accessed=int(moved * PLANNED),
+            bytes_accessed=int(moved),
         ),
         compiler_params=pltpu.CompilerParams(vmem_limit_bytes=LIMIT),
     )
 
-    return run
+    def go(*operands):
+        operands = [
+            o
+            if o.size <= 8192
+            else pltpu.with_memory_space_constraint(
+                o, pltpu.VMEM if id(o) in HELD_NOW else pltpu.HBM
+            )
+            for o in operands
+        ]
+        outs = run(*operands)
+        for n, o in enumerate(outs if many else [outs]):
+            if n in vout:
+                hold(o)
+        return outs
+
+    return go
+
+
+VOUT = {"spatial": (1,), "feed_forward0": (4,), "feed_forward1": (4,)}
 
 
 def whole(shape):
@@ -182,15 +213,21 @@
         return x
 
     def total(x):
-        for bits in ([core_bit], plane_a, depth_bits):
+        orders = {
+            0: ([core_bit], plane_a, depth_bits),
+            1: (depth_bits, [core_bit], plane_a),
+            2: ([core_bit], depth_bits, plane_a),
+        }[1]
+        for bits in orders:
             masks = [0]
             for bit in bits:
                 masks = masks + [m | (1 << bit) for m in masks]
             parts = [x] + [flip_mask(x, m) for m in masks[1:]]
+            if bits is orders[-1]:
+                return parts
             while len(parts) > 1:
                 parts = [a + b for a, b in zip(parts[::2], parts[1::2])]
             x = parts[0]
-        return x
 
     def local(
         frames,
@@ -208,6 +245,7 @@
         contract_bias,
         output_cotangent,
     ):
+        HELD_NOW.clear()
         items, frame_total, rows_local, width, channels = frames.shape
         grid_size = rows_local * row_parts
         tokens = rows_local * width
@@ -246,13 +284,12 @@
         def done(x):
             state[:] = [x]
 
-        both = jnp.concatenate([expand_weight.T, contract_weight], axis=1)
-        carried = jnp.concatenate([both, mixing_weight.reshape(-1, 2 * channels)], axis=0)
+        carried = jnp.concatenate([expand_weight.T, contract_weight, mixing_weight], axis=1)
         arrived = flip(carried, depth_bits[0])
-        both_near = jnp.concatenate([both, flip(both, depth_bits[1])], axis=0)
-        pieces = jnp.stack(
-            [mixing_weight.reshape(-1, lanes), arrived[shard:].reshape(-1, lanes)]
-        )
+        beside = flip(carried, depth_bits[1])
+        both_near = jnp.concatenate([carried[:, : 2 * channels], beside[:, : 2 * channels]], axis=0)
+        pieces = jnp.stack([mixing_weight, arrived[:, 2 * channels :]])
+        pieces = pieces.reshape(2, -1, lanes)
         pieces = gather_stages(pieces, mixing_low)
         axes_total = low_bits + 1
 
@@ -441,9 +478,9 @@
             "head",
         )(counts, frames, time_weight, gain_one, shift_one, wave_fwd)
         done(merged)
-        columns = to_columns(exchange(to_send(head_parts, items)), items)
-
-        far = arrived[:shard]
+        columns = hold(to_columns(exchange(to_send(head_parts, items)), items))
+
+        far = arrived[:, : 2 * channels]
         batches = [seq(both_near), jnp.concatenate([far, flip(seq(far), depth_bits[1])], axis=0)]
 
         def gather_plane(x):
@@ -456,7 +493,7 @@
         shards = [gather_plane(batches[0])]
 
         cot_own = output_cotangent.reshape(items * tokens, channels)
-        cot_other = flip(cot_own, core_bit)
+        cot_other = hold(flip(cot_own, core_bit))
         token_total = items * tokens
         block = tokens
         token_spec = pl.BlockSpec((block, channels), lambda i: (i, 0))
@@ -510,12 +547,24 @@
         bias_spec = whole((2, 1, 2 * lanes))
         mix_flops = 2 * items * (2 * mode_rows * 4 * lanes * lanes + 2 * col.size * kept * lanes)
 
+        def layer(z, w):
+            zr, zi = z[:, :lanes], z[:, lanes:]
+            real = dot_full(zr, w[:lanes, :lanes]) + dot_full(zi, w[lanes:, :lanes])
+            imag = dot_full(zi, w[lanes:, lanes:]) + dot_full(zr, w[:lanes, lanes:])
+            return jnp.concatenate([real, imag], axis=1)
+
+        same = (np.arange(2 * MODES) // MODES)[:, None] == (
+            np.arange(col.shape[1]) // rows_local % 2
+        )[None, :]
+        col_two = np.stack([np.where(same, col, 0), np.where(same, 0, col)]).astype(np.float32)
+
         def mix_body(x_ref, w0_ref, w1_ref, b_ref, col_ref, col_t_ref, out_ref, z_ref, u_ref, v_ref):
-            z = modes_rows(dot_full(col_ref[...], get_columns(x_ref)))
+            x = get_columns(x_ref)
+            z = modes_rows(dot_full(col_ref[0], x) + dot_full(col_ref[1], x))
             z_ref[...] = z
-            u = dot_full(z, w0_ref[...]) + b_ref[0]
+            u = layer(z, w0_ref[...]) + b_ref[0]
             u_ref[...] = u
-            v = dot_full(u * cdf(u), w1_ref[...]) + b_ref[1]
+            v = layer(u * cdf(u), w1_ref[...]) + b_ref[1]
             v_ref[...] = v
             mixed = v - jnp.clip(v, -SHRINK, SHRINK)
             put_columns(out_ref, dot_split(col_t_ref[...], rows_modes(mixed)))
@@ -531,19 +580,19 @@
             mix_body,
             (items,),
             [column_spec, weight_spec, weight_spec, bias_spec]
-            + [whole(col.shape), whole(col_t_half.shape)],
+            + [whole(col_two.shape), whole(col_t_half.shape)],
             [column_spec, mode_spec, mode_spec, mode_spec],
             [column_type(items), mode_type, mode_type, mode_type],
             6 * mix_flops,
             items * slab_bytes * 4,
             "mix",
-        )(after(seq(columns), *first_gates), *mix_weight, mix_bias, col, col_t_half)
+        )(after(seq(columns), *first_gates), *mix_weight, mix_bias, col_two, col_t_half)
         done(mixed[1])
         single = [1 << b for b in plane_a]
         near = [s for m, s in zip(masks_a, shards[1]) if m in single]
         rest = [s for m, s in zip(masks_a, shards[0]) if m and m not in single]
         a1 = {0: [], 1: near + rest, 2: near, 3: near[:1], 4: near[:1] + rest}[4]
-        row_back = from_send(exchange(after(from_columns(mixed[0], items), *a1)), items)
+        row_back = hold(from_send(exchange(after(from_columns(mixed[0], items), *a1)), items))
 
         def spatial_body(parts_ref, merged_ref, gain_ref, shift_ref, table_ref, middle_ref, normed_ref):
             middle = merged_ref[0] + dot_split(table_ref[...], get_parts(parts_ref))
@@ -641,9 +690,13 @@
 
         if 0 == 1:
             shards.append(gather_plane(after(batches[1], mixed[1])))
-        raised = [cot_call(shards[0], 4), cot_call(shards[1], 0)]
+        raised = [cot_call(shards[0], 4)]
+        if not 0:
+            raised.append(cot_call(shards[1], 0))
         middle, normed_own = spatial_call(row_back)
-        normed_other = flip(normed_own, core_bit)
+        normed_other = hold(flip(normed_own, core_bit))
+        if 0:
+            raised.append(cot_call(shards[1], 0))
         fed = [feed_call(0, normed_own), feed_call(1, normed_other)]
         grad_middle, middle_parts, small_two = call(
             middle_body,
@@ -654,15 +707,15 @@
             3 * items * wave_flops,
             items * slab_bytes * 6,
             "middle_back",
-        )(middle, fed[0][4], seq(flip(fed[1][4], core_bit)), cot_own, gain_two, wave_inv_t)
+        )(middle, fed[0][4], seq(hold(flip(fed[1][4], core_bit))), cot_own, gain_two, wave_inv_t)
         done(small_two)
-        grad_columns = to_columns(exchange(to_send(middle_parts, items)), items)
+        grad_columns = hold(to_columns(exchange(to_send(middle_parts, items)), items))
 
         lane_block = unit % lanes == 0
         wide_count = count if lane_block else 1
 
         def outer_body(*refs):
-            out_c, out_e = refs[-2:]
+            outs = refs[-4:] if refs[-1].ndim == 3 else refs[-2:]
             contract_out, expand_out = 0.0, 0.0
             per_side = 2 * wide_count + 6
             for s in range(2):
@@ -676,13 +729,16 @@
                 ph, pl_, gh, gl, nh, nl = [r[...] for r in mine[2 * wide_count :]]
                 contract_out += dot_pairs(h, (gh, gl), TN)
                 expand_out += dot_pairs((ph, pl_), (nh, nl), TN)
-            there = refs[2 * per_side : -2]
-            if there:
-                contract_out += there[0][...]
-                expand_out += there[1][...]
-            out_c[...], out_e[...] = contract_out, expand_out
-
-        def outer_call(side, there=()):
+            if len(outs) == 4:
+                for o, x in ((0, contract_out), (2, expand_out)):
+                    for side in range(2):
+                        for b in range(outs[0].shape[0]):
+                            at = (b * 2 + side) * outs[0].shape[1]
+                            outs[o + side][b] = x[at : at + outs[0].shape[1], :]
+            else:
+                outs[0][...], outs[1][...] = contract_out, expand_out
+
+        def outer_call(side):
             picks = place_a[side * count : (side + 1) * count]
 
             def unit_spec(p):
@@ -722,23 +778,33 @@
             operands[0] = seq(operands[0])
             rows = quarter if lane_block else half
             row_block = pl.BlockSpec((rows, channels), lambda b: (b, 0))
-            kind = jax.ShapeDtypeStruct((half, channels), F32)
+            if side == 0:
+                eighth = quarter // 2
+                outs = [jax.ShapeDtypeStruct((2, eighth, channels), F32)] * 4
+                batches_here = rows // quarter
+                out_specs = [
+                    pl.BlockSpec((batches_here, eighth, channels), lambda b: (b, 0, 0))
+                ] * 4
+            else:
+                outs = [jax.ShapeDtypeStruct((half, channels), F32)] * 2
+                out_specs = [row_block] * 2
             out = call(
                 outer_body,
                 (half // rows,),
-                specs + [row_block] * len(there),
-                [row_block] * 2,
-                [kind, kind],
+                specs,
+                out_specs,
+                outs,
                 4 * half_flops,
                 token_total * (half + channels) * 16,
                 f"weight_grads{side}",
-            )(*operands, *there)
+            )(*operands)
             done(out[0])
             return out
 
         leaving = outer_call(1)
-        contract_there = flip(leaving[0], plane_b[-1])
-        expand_there = flip(leaving[1], plane_a[-1])
+        staying = outer_call(0) if 1 else None
+        contract_there = hold(flip(leaving[0], plane_b[-1]))
+        expand_there = hold(flip(leaving[1], plane_a[-1]))
 
         def contract_calls():
             def down_body(hh, hl, *refs):
@@ -773,9 +839,9 @@
             extra = [middle, there, as_row(contract_bias)]
             return down_call(0, extra, [item_spec, item_spec, row_spec])
 
-        if 2:
-            there = flip(down_call(1, [], []), core_bit)
-        if 2 == 1:
+        if 4 in (1, 2, 3):
+            there = hold(flip(down_call(1, [], []), core_bit))
+        if 4 == 1:
             block_out = finish_output(there)
 
         def mix_back_body(
@@ -831,34 +897,55 @@
             [pltpu.VMEM((2,) + square, F32)],
         )(seq(grad_columns), *mixed[1:], *mix_weight, col_half, col_t_half)
         done(big_bias)
-        last_parts = from_send(exchange(from_columns(back_parts, items)), items)
-        if 2 == 2:
+        last_parts = hold(from_send(exchange(from_columns(back_parts, items)), items))
+        if 4 == 2:
             block_out = finish_output(there)
-        staying = outer_call(0, (contract_there, expand_there))
-        if 2 == 3:
+        if staying is None:
+            staying = outer_call(0)
+        came = [x.reshape(2, quarter, channels) for x in (contract_there, expand_there)]
+        if 4 == 4:
+            there = hold(flip(down_call(1, [], []), core_bit))
+
+        def add_body(a_ref, b_ref, c_ref, d_ref, o1_ref, o2_ref):
+            o1_ref[...] = a_ref[...] + b_ref[...]
+            o2_ref[...] = c_ref[...] + d_ref[...]
+
+        thin = (1, quarter // 2, channels)
+        first_part = pl.BlockSpec(thin, lambda b: (b, 0, 0))
+        second_part = pl.BlockSpec(thin, lambda b: (b, 1, 0))
+        leave_kind = jax.ShapeDtypeStruct((2, quarter // 2, channels), F32)
+        leave_c, leave_e = call(
+            add_body,
+            (2,),
+            [first_part, second_part] * 2,
+            [first_part] * 2,
+            [leave_kind] * 2,
+            0,
+            half * channels * 12,
+            "add_leaving",
+        )(seq(staying[1]), came[0], staying[3], came[1])
+        done(leave_c)
+        if 4 == 3:
             block_out = finish_output(there)
-        if 2 == 0:
-            block_out = finish_output(flip(down_call(1, [], []), core_bit))
-        by_batch = lambda x: x.reshape(2, quarter, channels)
-        contract_part = scatter_stages(by_batch(staying[0]), plane_b[:-1], 1)
-        expand_part = scatter_stages(by_batch(staying[1]), plane_a[:-1], 1)
+        if 4 == 4 and 1:
+            block_out = finish_output(there)
+        travelling = []
+        for stay, leave, got, bits in (
+            (staying[2], leave_e, came[1], plane_a),
+            (staying[0], leave_c, came[0], plane_b),
+        ):
+            stay = stay + got[:, : quarter // 2]
+            for bit in bits[1:-1][::-1]:
+                stay, leave = jnp.split(stay + flip(leave, bit), 2, axis=1)
+            travelling.append((stay, flip(leave, bits[0])))
+        if 4 == 0:
+            block_out = finish_output(hold(flip(down_call(1, [], []), core_bit)))
 
         mix_grad = mix_grad.reshape(mixing_count, -1, lanes)
         mix_grad = turn_axes(mixing_order(mix_grad, mixing_index))
+        if 1:
+            mix_grad = after(mix_grad, block_out)
         mix_grad = scatter_stages(mix_grad, mixing_low)
-        joined = jnp.concatenate([expand_part, contract_part], axis=2)
-        both_grad = scatter_stages(joined, depth_bits[1:], 1).reshape(2 * shard, 2 * channels)
-        leaving_last = jnp.concatenate(
-            [both_grad[shard:], mix_grad[1].reshape(-1, 2 * channels)], axis=0
-        )
-        arrived_last = flip(after(leaving_last, last_parts), depth_bits[0])
-        both_grad = both_grad[:shard] + arrived_last[:shard]
-        mixing_weight_grad = mix_grad[0].reshape(mixing_weight.shape) + arrived_last[
-            shard:
-        ].reshape(mixing_weight.shape)
-        expand_weight_grad = both_grad[:, :channels].T
-        contract_weight_grad = both_grad[:, channels:]
-
         def final_body(
             counts_ref,
             parts_ref,
@@ -926,6 +1013,26 @@
             "frames_grad",
         )(counts, seq(grad_merged), time_weight)
 
+        if 1:
+            gate = small_one if 1 == 1 else block_out
+            travelling = [(s, after(r, gate)) for s, r in travelling]
+        joined = jnp.concatenate([s + r for s, r in travelling], axis=2)
+        stay, leave = jnp.split(joined, 2, axis=1)
+        got = flip(leave, depth_bits[1])
+        if 1:
+            got = after(got, small_one)
+        both_grad = (stay + got).reshape(2 * shard, 2 * channels)
+        leaving_last = jnp.concatenate(
+            [both_grad[shard:], mix_grad[1].reshape(-1, 2 * channels)], axis=0
+        )
+        arrived_last = flip(after(leaving_last, last_parts), depth_bits[0])
+        both_grad = both_grad[:shard] + arrived_last[:shard]
+        mixing_weight_grad = mix_grad[0].reshape(mixing_weight.shape) + arrived_last[
+            shard:
+        ].reshape(mixing_weight.shape)
+        expand_weight_grad = both_grad[:, :channels].T
+        contract_weight_grad = both_grad[:, channels:]
+
         bias_grad_local = fed[0][5] + fed[1][5]
         bias_full = jnp.zeros((2, 2, PAIRS, lanes), F32)
         bias_full = lax.dynamic_update_slice(
@@ -934,27 +1041,49 @@
         hidden_bias = jnp.dot(
             pick.T, bias_grad_local.reshape(-1, shard), precision=HIGHEST
         ).reshape(-1, channels)
-        late = total(
-            jnp.concatenate(
-                [small_one[: frame_total + 2], small_two[:3], bias_full, hidden_bias], axis=0
-            )
+        at = frame_total
+        rows = jnp.concatenate(
+            [small_one[: at + 2], small_two[:3], bias_full, hidden_bias], axis=0
         )
-        at = frame_total
+        parts = total(rows)
+        widths = [at, 1, 1, 1, 1, 1, 4, rows.shape[0] - at - 9]
+
+        def finish_body(*refs):
+            ins, outs = refs[: len(parts)], refs[len(parts) :]
+            sums = [r[...] for r in ins]
+            while len(sums) > 1:
+                sums = [a + b for a, b in zip(sums[::2], sums[1::2])]
+            row = 0
+            for out, count in zip(outs, widths):
+                out[...] = sums[0][row : row + count, :]
+                row += count
+
+        finals = call(
+            finish_body,
+            (1,),
+            [whole(rows.shape)] * len(parts),
+            [whole((w, channels)) for w in widths],
+            [jax.ShapeDtypeStruct((w, channels), F32) for w in widths],
+            0,
+            rows.size * 24,
+            "sums",
+        )(*parts)
+        time_grad, gain_1, shift_1, gain_2, shift_2, bias_c, mix_bias_grad, bias_e = finals
 
         return (
             block_out.reshape(output_cotangent.shape),
             frames_grad,
-            late[:at],
-            late[at],
-            late[at + 1],
+            time_grad,
+            gain_1.reshape(channels),
+            shift_1.reshape(channels),
             mixing_weight_grad,
-            late[at + 5 : at + 9],
-            late[at + 2],
-            late[at + 3],
+            mix_bias_grad,
+            gain_2.reshape(channels),
+            shift_2.reshape(channels),
             expand_weight_grad,
-            late[at + 9 :].reshape(hidden_total),
+            bias_e.reshape(hidden_total),
             contract_weight_grad,
-            late[at + 4],
+            bias_c.reshape(channels),
         )
 
     return local

time: 245 us -> 229 us (0.935)
  waiting for transfers between devices: 80.6 us -> 71.2 us
  local copies, waits for them, and re-layouts: 15.7 us -> 7.69 us
    ppermute x7, waiting for transfers between devices: 6.85 us -> 1.99 us  [flip_mask(): return lax.ppermute(x, AXES, pairs)]
    split x6 -> x2, local copies, waits for them, and re-layouts: 3.08 us -> 0.01 us  [scatter_stages(): stay, leave = jnp.split(x, 2, axis=axis)]
    add x0 -> x3, other arithmetic: none -> 2.64 us  [the longest x2 2.58 us: local(): joined = jnp.concatenate([s + r for s, r in travelling], axis=2)]
    unnamed x55 -> x54, local copies, waits for them, and re-layouts: 6.99 us -> 4.4 us
    all_to_all x4, waiting for transfers between devices: 6.83 us -> 4.35 us  [exchange(): return lax.all_to_all(x.reshape(row_parts, -1, lanes), 'rows', 0, 0)]
    pallas_call x15 -> x17, Pallas kernels: 84.4 us -> 86.3 us  [go(): outs = run(*operands)]
  transfers between devices with their start and end apart: 34 -> 34, of which waited for: 19 -> 16; matrix products, arithmetic and copies ran while one was open for 6% -> 4% of each run, Pallas kernels for 28% -> 31%
where the time goes in v3:
time: 229 us; the launch traced here: 228 us
  Pallas kernels  86.3 us (38%)
  waiting for transfers between devices  71.2 us (31%)
  starting transfers between devices  55.6 us (24%)
  local copies, waits for them, and re-layouts  7.69 us (3%)
  other arithmetic  5.54 us (2%)
    pallas_call x17, Pallas kernels, go(): outs = run(*operands)  86.3 us
    ppermute x23, waiting for transfers between devices, flip(): return lax.ppermute(x, AXES, pairs)  64.8 us
    ppermute x23, starting transfers between devices, flip(): return lax.ppermute(x, AXES, pairs)  27 us
    all_to_all x4, starting transfers between devices, exchange(): return lax.all_to_all(x.reshape(row_parts, -1, lanes), 'rows', 0, 0)  21.3 us
    ppermute x7, starting transfers between devices, flip_mask(): return lax.ppermute(x, AXES, pairs)  7.39 us
  transfers between devices with their start and end apart: 34, of which 16 were waited for; matrix products, arithmetic and copies ran while one was open for 4% of the time, Pallas kernels for 31%

profile of v3, /device:TPU:0, one launch (start us, length us, event | category | flops | bytes accessed | tf_op | source)
XLA Modules:
  0.0 228.1 jit_solution(2335010115254302036)
XLA Ops:
  1.7 4.1 %collective-permute-start = (f32[64,1088]{1,0:T(8,128)S(1)}, f32[64,1088]{1,0:T(8,128)S(1)}, u32[]{:S(2)}, u32[]{:S(2)}) collective-permute-start(f32[64,1088]{1,0:T(8,128)S(1)} %pad_maximum_fusion.3), channel_id=1, source_target_pairs={{0,16},{1,17},{2,18},{3,19},{4,20},{5,21},{6,22},{7,23},{8,24},{9,... | collective-permute-start | bytes 835592 | tf_op jit(solution)/shard_map/ppermute | solution.py:179
  7.4 4.3 %head.1 = (f32[2,256,512]{2,1,0:T(8,128)}, f32[2,4,2,2,64,128]{5,4,3,2,1,0:T(8,128)}) custom-call(s32[2]{0:T(128)} %counts_ref.5, f32[2,4,4,64,512]{4,3,2,1,0:T(8,128)} %refs_1_.1, f32[4,512]{1,0:T(4,128)} %time_ref.3, f32[1,512]{1,0:T(1,128)} %bitcast.114, f32[1,512]{1,0:T(1,128)} %bitcast.118, f32[256,256]{1,0:T(8,128)} %constant.96.clone.table_ref), custom_call_target="tpu_custom_call" | custom-call | flops 805306368 | bytes 6291456 | tf_op jit(solution)/shard_map/head/pallas_call | solution.py:155
  15.5 3.7 %collective-permute-done = f32[64,1088]{1,0:T(8,128)S(1)} collective-permute-done((f32[64,1088]{1,0:T(8,128)S(1)}, f32[64,1088]{1,0:T(8,128)S(1)}, u32[]{:S(2)}, u32[]{:S(2)}) %collective-permute-start) | collective-permute-done | bytes 278560 | tf_op jit(solution)/shard_map/ppermute | solution.py:179
  28.6 13.3 %collective-permute-done.1 = f32[64,1024]{1,0:T(8,128)S(1)} collective-permute-done((f32[64,1024]{1,0:T(8,128)S(1)}, f32[64,1024]{1,0:T(8,128)S(1)}, u32[]{:S(2)}, u32[]{:S(2)}) %collective-permute-start.1) | collective-permute-done | bytes 262176 | tf_op jit(solution)/shard_map/ppermute | solution.py:179
  46.5 6.4 %mix.1 = (f32[16,2,8,8,128]{4,3,2,1,0:T(8,128)}, f32[512,256]{1,0:T(8,128)}, f32[512,256]{1,0:T(8,128)}, f32[512,256]{1,0:T(8,128)}) custom-call(f32[16,2,8,8,128]{4,3,2,1,0:T(8,128)S(1)} %bitcast.83, f32[256,256]{1,0:T(8,128)} %get-tuple-element.186.w0_ref, f32[256,256]{1,0:T(8,128)} %get-tuple-element.187.w1_ref, f32[2,1,256]{2,1,0:T(1,128)} %bitcast.122, ...), custom_call_target="tpu_custom_call" | custom-call | flops 1207959552 | bytes 4194304 | tf_op jit(solution)/shard_map/mix/pallas_call | solution.py:155
  57.6 4.7 %all-to-all-start.1 = ((f32[16,128,128]{2,1,0:T(8,128)}), f32[16,128,128]{2,1,0:T(8,128)S(1)}, u32[]{:S(2)}, u32[]{:S(2)}) async-start(f32[16,128,128]{2,1,0:T(8,128)} %bitcast.90), calls=%async_computation.1 | async-start | bytes 2097152 | tf_op jit(solution)/shard_map/all_to_all | solution.py:388
  65.2 4.6 %cotangent_up.2 = (f32[512,512]{1,0:T(8,128)}, f32[512,512]{1,0:T(8,128)}, bf16[512,512]{1,0:T(8,128)(2,1)}, bf16[512,512]{1,0:T(8,128)(2,1)}, bf16[512,512]{1,0:T(8,128)(2,1)}, /*index=5*/bf16[512,512]{1,0:T(8,128)(2,1)}) custom-call(f32[512,512]{1,0:T(8,128)} %bitcast.93, f32[512,512]{1,0:T(8,128)S(1)} %collective-permute-done.9.g2_ref, ...), custom_call_target="tpu_custom_call" | custom-call | flops 1610612736 | bytes 4194304 | tf_op jit(solution)/shard_map/cotangent_up/pallas_call | solution.py:155
  69.8 7.7 %collective-permute-done.10.refs_2_.refs_6_.refs_9_ = f32[128,1024]{1,0:T(8,128)S(1)} collective-permute-done((f32[128,1024]{1,0:T(8,128)S(1)}, f32[128,1024]{1,0:T(8,128)S(1)}, u32[]{:S(2)}, u32[]{:S(2)}) %collective-permute-start.10) | collective-permute-done | bytes 524320 | tf_op jit(solution)/shard_map/ppermute | solution.py:179
  77.5 10.4 %collective-permute-done.11.refs_3_.refs_7_.refs_10_ = f32[128,1024]{1,0:T(8,128)S(1)} collective-permute-done((f32[128,1024]{1,0:T(8,128)}, f32[128,1024]{1,0:T(8,128)S(1)}, u32[]{:S(2)}, u32[]{:S(2)}) %collective-permute-start.11) | collective-permute-done | bytes 524320 | tf_op jit(solution)/shard_map/ppermute | solution.py:179
  88.7 4.4 %cotangent_up.3 = (f32[512,512]{1,0:T(8,128)}, f32[512,512]{1,0:T(8,128)}) custom-call(f32[512,512]{1,0:T(8,128)} %bitcast.94, f32[512,512]{1,0:T(8,128)S(1)} %collective-permute-done.9.g2_ref, f32[128,1024]{1,0:T(8,128)} %copy-done.3, f32[128,1024]{1,0:T(8,128)} %collective-permute-done.7.refs_1_.refs_5_.refs_8_, f32[128,1024]{1,0:T(8,128)} %copy-done.7, ...), custom_call_target="tpu_custom_call" | custom-call | flops 1610612736 | bytes 4194304 | tf_op jit(solution)/shard_map/cotangent_up/pallas_call | solution.py:155
  97.1 8.4 %feed_forward0.1 = (bf16[512,1024]{1,0:T(8,128)(2,1)}, bf16[512,1024]{1,0:T(8,128)(2,1)}, bf16[512,1024]{1,0:T(8,128)(2,1)}, bf16[512,1024]{1,0:T(8,128)(2,1)}, ...) custom-call(f32[2,256,512]{2,1,0:T(8,128)S(1)} %get-tuple-element.109.n_ref, ...), custom_call_target="tpu_custom_call" | custom-call | flops 3221225472 | bytes 9437184 | tf_op jit(solution)/shard_map/feed_forward0/pallas_call | solution.py:155
  105.5 8.5 %feed_forward1.1 = (bf16[512,1024]{1,0:T(8,128)(2,1)}, bf16[512,1024]{1,0:T(8,128)(2,1)}, bf16[512,1024]{1,0:T(8,128)(2,1)}, bf16[512,1024]{1,0:T(8,128)(2,1)}, ...) custom-call(f32[2,256,512]{2,1,0:T(8,128)S(1)} %collective-permute-done.12., ...), custom_call_target="tpu_custom_call" | custom-call | flops 3221225472 | bytes 9437184 | tf_op jit(solution)/shard_map/feed_forward1/pallas_call | solution.py:155
  116.9 3.9 %middle_back.1 = (f32[2,256,512]{2,1,0:T(8,128)}, f32[2,4,2,2,64,128]{5,4,3,2,1,0:T(8,128)}, f32[8,512]{1,0:T(8,128)}) custom-call(f32[2,256,512]{2,1,0:T(8,128)} %get-tuple-element.108.mid_ref.refs_0_, f32[2,256,512]{2,1,0:T(8,128)S(1)} %get-tuple-element.111.g1_ref, f32[2,256,512]{2,1,0:T(8,128)S(1)} %collective-permute-done.13.g2_ref, ...), custom_call_target="tpu_custom_call" | custom-call | flops 402653184 | bytes 6291456 | tf_op jit(solution)/shard_map/middle_back/pallas_call | solution.py:155
  120.8 6.0 %all-to-all-start.2 = ((f32[16,128,128]{2,1,0:T(8,128)}), f32[16,128,128]{2,1,0:T(8,128)S(1)}, u32[]{:S(2)}, u32[]{:S(2)}) async-start(f32[16,128,128]{2,1,0:T(8,128)} %bitcast.91), calls=%async_computation.2 | async-start | bytes 2097152 | tf_op jit(solution)/shard_map/all_to_all | solution.py:388
  126.8 7.5 %weight_grads1.1 = (f32[512,512]{1,0:T(8,128)}, f32[512,512]{1,0:T(8,128)}) custom-call(bf16[512,1024]{1,0:T(8,128)(2,1)} %get-tuple-element.148.refs_0_.refs_1_.hh, bf16[512,1024]{1,0:T(8,128)(2,1)} %get-tuple-element.148.refs_0_.refs_1_.hh, bf16[512,1024]{1,0:T(8,128)(2,1)} %get-tuple-element.119.refs_2_.refs_3_.hl, ...), custom_call_target="tpu_custom_call" | custom-call | flops 3221225472 | bytes 8388608 | tf_op jit(solution)/shard_map/weight_grads1/pallas_call | solution.py:155
  137.8 7.7 %weight_grads0.1 = (f32[2,128,512]{2,1,0:T(8,128)}, f32[2,128,512]{2,1,0:T(8,128)}, f32[2,128,512]{2,1,0:T(8,128)}, f32[2,128,512]{2,1,0:T(8,128)}) custom-call(bf16[512,1024]{1,0:T(8,128)(2,1)} %get-tuple-element.148.refs_0_.refs_1_.hh, bf16[512,1024]{1,0:T(8,128)(2,1)} %get-tuple-element.148.refs_0_.refs_1_.hh, ...), custom_call_target="tpu_custom_call" | custom-call | flops 3221225472 | bytes 8388608 | tf_op jit(solution)/shard_map/weight_grads0/pallas_call | solution.py:155
  145.4 4.3 %all-to-all-done.2 = f32[16,128,128]{2,1,0:T(8,128)S(1)} async-done(((f32[16,128,128]{2,1,0:T(8,128)}), f32[16,128,128]{2,1,0:T(8,128)S(1)}, u32[]{:S(2)}, u32[]{:S(2)}) %all-to-all-start.2) | async-done | bytes 1048608 | tf_op jit(solution)/shard_map/all_to_all | solution.py:388
  149.8 5.6 %mix_back.1 = (f32[16,2,8,8,128]{4,3,2,1,0:T(8,128)}, f32[2,2,2,64,64]{4,3,2,1,0:T(8,128)}, f32[2,1,256]{2,1,0:T(1,128)}) custom-call(f32[16,2,8,8,128]{4,3,2,1,0:T(8,128)S(1)} %bitcast.84, f32[512,256]{1,0:T(8,128)} %get-tuple-element.101.z_ref, f32[512,256]{1,0:T(8,128)} %get-tuple-element.140.u_ref, f32[512,256]{1,0:T(8,128)} %get-tuple-element.141.v_ref, ...), custom_call_target="tpu_custom_call" | custom-call | flops 1207959552 | bytes 4194304 | tf_op jit(solution)/shard_map/mix_back/pallas_call | solution.py:155
  155.4 6.9 %all-to-all-start.3 = ((f32[16,128,128]{2,1,0:T(8,128)}), f32[16,128,128]{2,1,0:T(8,128)S(1)}, u32[]{:S(2)}, u32[]{:S(2)}) async-start(f32[16,128,128]{2,1,0:T(8,128)} %bitcast.89), calls=%async_computation.3 | async-start | bytes 2097152 | tf_op jit(solution)/shard_map/all_to_all | solution.py:388
  162.4 5.0 %contract1.1 = f32[2,256,512]{2,1,0:T(8,128)} custom-call(bf16[512,1024]{1,0:T(8,128)(2,1)} %get-tuple-element.143.refs_10_.refs_11_.hh, bf16[512,1024]{1,0:T(8,128)(2,1)} %get-tuple-element.127.refs_12_.refs_13_.hl, f32[128,1024]{1,0:T(8,128)} %copy-done.2, f32[128,1024]{1,0:T(8,128)} %collective-permute-done.3.refs_1_.refs_4_, f32[128,1024]{1,0:T(8,128)} %copy-done.6, ...), custom_call_target="tpu_custom_call" | custom-call | flops 1610612736 | bytes 3145728 | tf_op jit(solution)/shard_map/contract1/pallas_call | solution.py:155
  174.7 5.3 %contract0.1 = f32[2,256,512]{2,1,0:T(8,128)} custom-call(bf16[512,1024]{1,0:T(8,128)(2,1)} %get-tuple-element.148.refs_0_.refs_1_.hh, bf16[512,1024]{1,0:T(8,128)(2,1)} %get-tuple-element.119.refs_2_.refs_3_.hl, f32[2,256,512]{2,1,0:T(8,128)} %get-tuple-element.108.mid_ref.refs_0_, f32[2,256,512]{2,1,0:T(8,128)S(1)} %collective-permute-done.16.refs_1_, ...), custom_call_target="tpu_custom_call" | custom-call | flops 1610612736 | bytes 3145728 | tf_op jit(solution)/shard_map/contract0/pallas_call | solution.py:155
  181.1 5.8 %collective-permute-done.24 = f32[4,32,128]{2,1,0:T(8,128)S(1)} collective-permute-done((f32[4,32,128]{2,1,0:T(8,128)S(1)}, f32[4,32,128]{2,1,0:T(8,128)S(1)}, u32[]{:S(2)}, u32[]{:S(2)}) %collective-permute-start.24) | collective-permute-done | bytes 65568 | tf_op jit(solution)/shard_map/ppermute | solution.py:179
  187.0 4.5 %final.1 = (f32[2,256,512]{2,1,0:T(8,128)}, f32[8,512]{1,0:T(8,128)}) custom-call(s32[2]{0:T(128)} %counts_ref.5, f32[2,4,2,2,64,128]{5,4,3,2,1,0:T(8,128)S(1)} %bitcast.82, f32[2,256,512]{2,1,0:T(8,128)} %get-tuple-element.94.merged_ref, f32[2,256,512]{2,1,0:T(8,128)} %get-tuple-element.151.refs_0_, f32[2,4,4,64,512]{4,3,2,1,0:T(8,128)} %refs_1_.1, ...), custom_call_target="tpu_custom_call" | custom-call | flops 402653184 | bytes 8388608 | tf_op jit(solution)/shard_map/final/pallas_call | solution.py:155
  200.1 10.0 %collective-permute-done.28 = f32[2,64,1024]{2,1,0:T(8,128)S(1)} collective-permute-done((f32[2,64,1024]{2,1,0:T(8,128)S(1)}, f32[2,64,1024]{2,1,0:T(8,128)S(1)}, u32[]{:S(2)}, u32[]{:S(2)}) %collective-permute-start.28) | collective-permute-done | bytes 524320 | tf_op jit(solution)/shard_map/ppermute | solution.py:179
  (184 shorter events, 73.7 us)
Async XLA Ops:
  1.7 17.5 %collective-permute-start = (f32[64,1088]{1,0:T(8,128)S(1)}, f32[64,1088]{1,0:T(8,128)S(1)}, u32[]{:S(2)}, u32[]{:S(2)}) collective-permute-start(f32[64,1088]{1,0:T(8,128)S(1)} %pad_maximum_fusion.3), channel_id=1, source_target_pairs={{0,16},{1,17},{2,18},{3,19},{4,20},{5,21},{6,22},{7,23},{8,24},{9,... | collective-permute-start | bytes 835592 | tf_op jit(solution)/shard_map/ppermute | solution.py:179
  5.8 17.3 %collective-permute-start.2 = (f32[64,1088]{1,0:T(8,128)S(1)}, f32[64,1088]{1,0:T(8,128)S(1)}, u32[]{:S(2)}, u32[]{:S(2)}) collective-permute-start(f32[64,1088]{1,0:T(8,128)S(1)} %pad_maximum_fusion.3), channel_id=1, source_target_pairs={{0,8},{1,9},{2,10},{3,11},{4,12},{5,13},{6,14},{7,15},{8,0},{9,1},... | collective-permute-start | bytes 835592 | tf_op jit(solution)/shard_map/ppermute | solution.py:179
  11.8 34.7 %all-to-all-start = ((f32[16,128,128]{2,1,0:T(8,128)}), f32[16,128,128]{2,1,0:T(8,128)S(1)}, u32[]{:S(2)}, u32[]{:S(2)}) async-start(f32[16,128,128]{2,1,0:T(8,128)} %bitcast.88), calls=%async_computation | async-start | bytes 2097152 | tf_op jit(solution)/shard_map/all_to_all | solution.py:388
  25.0 21.5 %collective-permute-start.4 = (f32[128,1024]{1,0:T(8,128)S(1)}, f32[128,1024]{1,0:T(8,128)S(1)}, u32[]{:S(2)}, u32[]{:S(2)}) collective-permute-start(f32[128,1024]{1,0:T(8,128)S(1)} %pad_maximum_fusion.2.refs_0_.refs_3_), channel_id=1, source_target_pairs={{0,1},{1,0},{2,3},{3,2},{4,5},{5,4},{6,7},{7,6},{8,9},{9,8},{10,11... | collective-permute-start | bytes 1572872 | tf_op jit(solution)/shard_map/ppermute | solution.py:179
  25.5 18.2 %collective-permute-start.3 = (f32[128,1024]{1,0:T(8,128)S(1)}, f32[128,1024]{1,0:T(8,128)}, u32[]{:S(2)}, u32[]{:S(2)}) collective-permute-start(f32[128,1024]{1,0:T(8,128)S(1)} %pad_maximum_fusion.2.refs_0_.refs_3_), channel_id=1, source_target_pairs={{0,4},{1,5},{2,6},{3,7},{4,0},{5,1},{6,2},{7,3},{8,12},{9,13},{10,... | collective-permute-start | bytes 1572872 | tf_op jit(solution)/shard_map/ppermute | solution.py:179
  25.7 16.3 %collective-permute-start.1 = (f32[64,1024]{1,0:T(8,128)S(1)}, f32[64,1024]{1,0:T(8,128)S(1)}, u32[]{:S(2)}, u32[]{:S(2)}) collective-permute-start(f32[64,1024]{1,0:T(8,128)S(1)} %slice.132), channel_id=1, source_target_pairs={{0,8},{1,9},{2,10},{3,11},{4,12},{5,13},{6,14},{7,15},{8,0},{9,1},... | collective-permute-start | bytes 786440 | tf_op jit(solution)/shard_map/ppermute | solution.py:179
  42.0 14.1 %collective-permute-start.7 = (f32[128,1024]{1,0:T(8,128)S(1)}, f32[128,1024]{1,0:T(8,128)}, u32[]{:S(2)}, u32[]{:S(2)}) collective-permute-start(f32[128,1024]{1,0:T(8,128)S(1)} %pad_maximum_fusion.1.refs_0_.refs_4_.refs_7_), channel_id=1, source_target_pairs={{0,4},{1,5},{2,6},{3,7},{4,0},{5,1},{6,2},{7,3},{8,12},{9,13},{10,... | collective-permute-start | bytes 1572872 | tf_op jit(solution)/shard_map/ppermute | solution.py:179
  43.7 13.9 %collective-permute-start.8 = (f32[128,1024]{1,0:T(8,128)}, f32[128,1024]{1,0:T(8,128)}, u32[]{:S(2)}, u32[]{:S(2)}) collective-permute-start(f32[128,1024]{1,0:T(8,128)} %collective-permute-done.3.refs_1_.refs_4_), channel_id=1, source_target_pairs={{0,1},{1,0},{2,3},{3,2},{4,5},{5,4},{6,7},{7,6},{8,9},{9,8},{10,11... | collective-permute-start | bytes 1572872 | tf_op jit(solution)/shard_map/ppermute | solution.py:179
  57.6 35.5 %all-to-all-start.1 = ((f32[16,128,128]{2,1,0:T(8,128)}), f32[16,128,128]{2,1,0:T(8,128)S(1)}, u32[]{:S(2)}, u32[]{:S(2)}) async-start(f32[16,128,128]{2,1,0:T(8,128)} %bitcast.90), calls=%async_computation.1 | async-start | bytes 2097152 | tf_op jit(solution)/shard_map/all_to_all | solution.py:388
  62.8 14.8 %collective-permute-start.10 = (f32[128,1024]{1,0:T(8,128)S(1)}, f32[128,1024]{1,0:T(8,128)S(1)}, u32[]{:S(2)}, u32[]{:S(2)}) collective-permute-start(f32[128,1024]{1,0:T(8,128)S(1)} %pad_maximum_fusion.1.refs_0_.refs_4_.refs_7_), channel_id=1, source_target_pairs={{0,1},{1,0},{2,3},{3,2},{4,5},{5,4},{6,7},{7,6},{8,9},{9,8},{10,11... | collective-permute-start | bytes 1572872 | tf_op jit(solution)/shard_map/ppermute | solution.py:179
  64.3 23.7 %collective-permute-start.11 = (f32[128,1024]{1,0:T(8,128)}, f32[128,1024]{1,0:T(8,128)S(1)}, u32[]{:S(2)}, u32[]{:S(2)}) collective-permute-start(f32[128,1024]{1,0:T(8,128)} %collective-permute-done.7.refs_1_.refs_5_.refs_8_), channel_id=1, source_target_pairs={{0,1},{1,0},{2,3},{3,2},{4,5},{5,4},{6,7},{7,6},{8,9},{9,8},{10,11... | collective-permute-start | bytes 1572872 | tf_op jit(solution)/shard_map/ppermute | solution.py:179
  96.1 9.4 %collective-permute-start.12 = (f32[2,256,512]{2,1,0:T(8,128)S(1)}, f32[2,256,512]{2,1,0:T(8,128)S(1)}, u32[]{:S(2)}, u32[]{:S(2)}) collective-permute-start(f32[2,256,512]{2,1,0:T(8,128)S(1)} %get-tuple-element.109.n_ref), channel_id=1, source_target_pairs={{0,2},{1,3},{2,0},{3,1},{4,6},{5,7},{6,4},{7,5},{8,10},{9,11},{10,... | collective-permute-start | bytes 3145736 | tf_op jit(solution)/shard_map/ppermute | solution.py:179
  120.8 29.0 %all-to-all-start.2 = ((f32[16,128,128]{2,1,0:T(8,128)}), f32[16,128,128]{2,1,0:T(8,128)S(1)}, u32[]{:S(2)}, u32[]{:S(2)}) async-start(f32[16,128,128]{2,1,0:T(8,128)} %bitcast.91), calls=%async_computation.2 | async-start | bytes 2097152 | tf_op jit(solution)/shard_map/all_to_all | solution.py:388
  134.3 33.6 %collective-permute-start.14 = (f32[512,512]{1,0:T(8,128)}, f32[512,512]{1,0:T(8,128)S(1)}, u32[]{:S(2)}, u32[]{:S(2)}) collective-permute-start(f32[512,512]{1,0:T(8,128)} %get-tuple-element.134), channel_id=1, source_target_pairs={{0,4},{1,5},{2,6},{3,7},{4,0},{5,1},{6,2},{7,3},{8,12},{9,13},{10,... | collective-permute-start | bytes 3145736 | tf_op jit(solution)/shard_map/ppermute | solution.py:179
  136.2 31.7 %collective-permute-start.15 = (f32[512,512]{1,0:T(8,128)}, f32[512,512]{1,0:T(8,128)}, u32[]{:S(2)}, u32[]{:S(2)}) collective-permute-start(f32[512,512]{1,0:T(8,128)} %get-tuple-element.146), channel_id=1, source_target_pairs={{0,1},{1,0},{2,3},{3,2},{4,5},{5,4},{6,7},{7,6},{8,9},{9,8},{10,11... | collective-permute-start | bytes 3145736 | tf_op jit(solution)/shard_map/ppermute | solution.py:179
  155.4 31.5 %all-to-all-start.3 = ((f32[16,128,128]{2,1,0:T(8,128)}), f32[16,128,128]{2,1,0:T(8,128)S(1)}, u32[]{:S(2)}, u32[]{:S(2)}) async-start(f32[16,128,128]{2,1,0:T(8,128)} %bitcast.89), calls=%async_computation.3 | async-start | bytes 2097152 | tf_op jit(solution)/shard_map/all_to_all | solution.py:388
  171.3 20.2 %collective-permute-start.27 = (f32[2,128,512]{2,1,0:T(8,128)}, f32[2,128,512]{2,1,0:T(8,128)}, u32[]{:S(2)}, u32[]{:S(2)}) collective-permute-start(f32[2,128,512]{2,1,0:T(8,128)} %get-tuple-element.147), channel_id=1, source_target_pairs={{0,1},{1,0},{2,3},{3,2},{4,5},{5,4},{6,7},{7,6},{8,9},{9,8},{10,11... | collective-permute-start | bytes 1572872 | tf_op jit(solution)/shard_map/ppermute | solution.py:179
  173.0 18.5 %collective-permute-start.26 = (f32[2,128,512]{2,1,0:T(8,128)}, f32[2,128,512]{2,1,0:T(8,128)}, u32[]{:S(2)}, u32[]{:S(2)}) collective-permute-start(f32[2,128,512]{2,1,0:T(8,128)} %get-tuple-element.162), channel_id=1, source_target_pairs={{0,4},{1,5},{2,6},{3,7},{4,0},{5,1},{6,2},{7,3},{8,12},{9,13},{10,... | collective-permute-start | bytes 1572872 | tf_op jit(solution)/shard_map/ppermute | solution.py:179
  186.9 9.4 %collective-permute-start.25 = (f32[2,32,128]{2,1,0:T(8,128)S(1)}, f32[2,32,128]{2,1,0:T(8,128)S(1)}, u32[]{:S(2)}, u32[]{:S(2)}) collective-permute-start(f32[2,32,128]{2,1,0:T(8,128)S(1)} %split.25), channel_id=1, source_target_pairs={{0,2},{1,3},{2,0},{3,1},{4,6},{5,7},{6,4},{7,5},{8,10},{9,11},{10,... | collective-permute-start | bytes 98312 | tf_op jit(solution)/shard_map/ppermute | solution.py:179
  194.2 15.9 %collective-permute-start.28 = (f32[2,64,1024]{2,1,0:T(8,128)S(1)}, f32[2,64,1024]{2,1,0:T(8,128)S(1)}, u32[]{:S(2)}, u32[]{:S(2)}) collective-permute-start(f32[2,64,1024]{2,1,0:T(8,128)S(1)} %pad_maximum_fusion), channel_id=1, source_target_pairs={{0,8},{1,9},{2,10},{3,11},{4,12},{5,13},{6,14},{7,15},{8,0},{9,1},... | collective-permute-start | bytes 1572872 | tf_op jit(solution)/shard_map/ppermute | solution.py:179
  196.4 16.4 %collective-permute-start.18 = (f32[17,512]{1,0:T(8,128)S(1)}, f32[17,512]{1,0:T(8,128)S(1)}, u32[]{:S(2)}, u32[]{:S(2)}) collective-permute-start(f32[17,512]{1,0:T(8,128)S(1)} %pad_maximum_fusion.7), channel_id=1, source_target_pairs={{0,8},{1,9},{2,10},{3,11},{4,12},{5,13},{6,14},{7,15},{8,0},{9,1},... | collective-permute-start | bytes 104456 | tf_op jit(solution)/shard_map/ppermute | solution.py:183
  196.5 17.0 %collective-permute-start.19 = (f32[17,512]{1,0:T(8,128)S(1)}, f32[17,512]{1,0:T(8,128)S(1)}, u32[]{:S(2)}, u32[]{:S(2)}) collective-permute-start(f32[17,512]{1,0:T(8,128)S(1)} %pad_maximum_fusion.7), channel_id=1, source_target_pairs={{0,24},{1,25},{2,26},{3,27},{4,28},{5,29},{6,30},{7,31},{8,16},{9,... | collective-permute-start | bytes 104456 | tf_op jit(solution)/shard_map/ppermute | solution.py:183
  200.1 13.3 %collective-permute-start.17 = (f32[17,512]{1,0:T(8,128)S(1)}, f32[17,512]{1,0:T(8,128)S(1)}, u32[]{:S(2)}, u32[]{:S(2)}) collective-permute-start(f32[17,512]{1,0:T(8,128)S(1)} %pad_maximum_fusion.7), channel_id=1, source_target_pairs={{0,16},{1,17},{2,18},{3,19},{4,20},{5,21},{6,22},{7,23},{8,24},{9,... | collective-permute-start | bytes 104456 | tf_op jit(solution)/shard_map/ppermute | solution.py:183
  210.2 16.4 %collective-permute-start.29 = (f32[68,1024]{1,0:T(8,128)S(1)}, f32[68,1024]{1,0:T(8,128)S(1)}, u32[]{:S(2)}, u32[]{:S(2)}) collective-permute-start(f32[68,1024]{1,0:T(8,128)S(1)} %pad_maximum_fusion.4), channel_id=1, source_target_pairs={{0,16},{1,17},{2,18},{3,19},{4,20},{5,21},{6,22},{7,23},{8,24},{9,... | collective-permute-start | bytes 835592 | tf_op jit(solution)/shard_map/ppermute | solution.py:179
  (36 other events, 354.2 us)

commit v4 on v3

--- a/solution.py
+++ b/solution.py
@@ -127,6 +127,8 @@
     vout = VOUT.get(name, ())
     kinds = [pltpu.VMEM if n in vout else pltpu.HBM for n in range(len(shapes))]
     shapes = [k(s.shape, s.dtype) for k, s in zip(kinds, shapes)]
+    if name in ('contract0', 'add_leaving', 'final'):
+        flops, moved = flops * 10, moved * 10
     run = pl.pallas_call(
         body,
         grid=grid,
@@ -929,6 +931,9 @@
             block_out = finish_output(there)
         if 4 == 4 and 1:
             block_out = finish_output(there)
+        mix_grad = mix_grad.reshape(mixing_count, -1, lanes)
+        mix_grad = turn_axes(mixing_order(mix_grad, mixing_index))
+        mix_stay, mix_leave = jnp.split(mix_grad, 2, axis=0)
         travelling = []
         for stay, leave, got, bits in (
             (staying[2], leave_e, came[1], plane_a),
@@ -937,15 +942,13 @@
             stay = stay + got[:, : quarter // 2]
             for bit in bits[1:-1][::-1]:
                 stay, leave = jnp.split(stay + flip(leave, bit), 2, axis=1)
+            if bits[0] == mixing_low[-1]:
+                rows_two = [leave.reshape(-1, channels), mix_leave.reshape(-1, channels)]
+                leave = jnp.concatenate(rows_two, axis=0)
             travelling.append((stay, flip(leave, bits[0])))
         if 4 == 0:
             block_out = finish_output(hold(flip(down_call(1, [], []), core_bit)))
 
-        mix_grad = mix_grad.reshape(mixing_count, -1, lanes)
-        mix_grad = turn_axes(mixing_order(mix_grad, mixing_index))
-        if 1:
-            mix_grad = after(mix_grad, block_out)
-        mix_grad = scatter_stages(mix_grad, mixing_low)
         def final_body(
             counts_ref,
             parts_ref,
@@ -1016,17 +1019,20 @@
         if 1:
             gate = small_one if 1 == 1 else block_out
             travelling = [(s, after(r, gate)) for s, r in travelling]
-        joined = jnp.concatenate([s + r for s, r in travelling], axis=2)
-        stay, leave = jnp.split(joined, 2, axis=1)
-        got = flip(leave, depth_bits[1])
-        if 1:
-            got = after(got, small_one)
-        both_grad = (stay + got).reshape(2 * shard, 2 * channels)
-        leaving_last = jnp.concatenate(
-            [both_grad[shard:], mix_grad[1].reshape(-1, 2 * channels)], axis=0
+        stays, gots = zip(*travelling)
+        span = stays[1].shape[0] * stays[1].shape[1]
+        mix_got = gots[1][span:].reshape(mix_stay.shape)
+        gots = [gots[0], gots[1][:span].reshape(stays[1].shape)]
+        joined = jnp.concatenate([s + r for s, r in zip(stays, gots)], axis=2)
+        mix_grad = scatter_stages(mix_stay + mix_got, mixing_low[:-1])
+        blocks = joined.reshape(2, 2, shard, 2 * channels)
+        leaving_far = jnp.concatenate(
+            [blocks[1, 0], mix_grad[1].reshape(-1, 2 * channels)], axis=0
         )
-        arrived_last = flip(after(leaving_last, last_parts), depth_bits[0])
-        both_grad = both_grad[:shard] + arrived_last[:shard]
+        arrived_last = flip(leaving_far, depth_bits[0])
+        got_both = flip_mask(blocks[1, 1], (1 << depth_bits[0]) | (1 << depth_bits[1]))
+        got_near = flip(blocks[0, 1], depth_bits[1])
+        both_grad = (blocks[0, 0] + got_near) + (arrived_last[:shard] + got_both)
         mixing_weight_grad = mix_grad[0].reshape(mixing_weight.shape) + arrived_last[
             shard:
         ].reshape(mixing_weight.shape)

time: 229 us -> 233 us (1.017)
  local copies, waits for them, and re-layouts: 7.69 us -> 10.8 us
  other arithmetic: 5.54 us -> 8.03 us
    ppermute x23 -> x22, waiting for transfers between devices: 64.8 us -> 58 us  [flip(): return lax.ppermute(x, AXES, pairs)]
    ppermute x7 -> x8, starting transfers between devices: 7.39 us -> 11.8 us  [flip_mask(): return lax.ppermute(x, AXES, pairs)]
    ppermute x23 -> x22, starting transfers between devices: 27 us -> 22.9 us  [flip(): return lax.ppermute(x, AXES, pairs)]
    ppermute x7 -> x8, waiting for transfers between devices: 1.99 us -> 5.34 us  [flip_mask(): return lax.ppermute(x, AXES, pairs)]
  transfers between devices with their start and end apart: 34 -> 34, of which waited for: 16 -> 16; matrix products, arithmetic and copies ran while one was open for 4% -> 6% of each run, Pallas kernels for 31% -> 30%
where the time goes in v4:
time: 233 us; the launch traced here: 232 us
  Pallas kernels  86 us (37%)
  waiting for transfers between devices  69.1 us (30%)
  starting transfers between devices  56 us (24%)
  local copies, waits for them, and re-layouts  10.8 us (5%)
  other arithmetic  8.03 us (3%)
    pallas_call x17, Pallas kernels, go(): outs = run(*operands)  86 us
    ppermute x22, waiting for transfers between devices, flip(): return lax.ppermute(x, AXES, pairs)  58 us
    ppermute x22, starting transfers between devices, flip(): return lax.ppermute(x, AXES, pairs)  22.9 us
    all_to_all x4, starting transfers between devices, exchange(): return lax.all_to_all(x.reshape(row_parts, -1, lanes), 'rows', 0, 0)  21.3 us
    ppermute x8, starting transfers between devices, flip_mask(): return lax.ppermute(x, AXES, pairs)  11.8 us
    all_to_all x4, waiting for transfers between devices, exchange(): return lax.all_to_all(x.reshape(row_parts, -1, lanes), 'rows', 0, 0)  5.77 us
    ppermute x8, waiting for transfers between devices, flip_mask(): return lax.ppermute(x, AXES, pairs)  5.34 us
  transfers between devices with their start and end apart: 34, of which 16 were waited for; matrix products, arithmetic and copies ran while one was open for 6% of the time, Pallas kernels for 30%

profile of v4, /device:TPU:0, one launch (start us, length us, event | category | flops | bytes accessed | tf_op | source)
XLA Modules:
  0.0 231.8 jit_solution(13027095464657394360)
XLA Ops:
  1.7 4.1 %collective-permute-start = (f32[64,1088]{1,0:T(8,128)S(1)}, f32[64,1088]{1,0:T(8,128)S(1)}, u32[]{:S(2)}, u32[]{:S(2)}) collective-permute-start(f32[64,1088]{1,0:T(8,128)S(1)} %pad_maximum_fusion.4), channel_id=1, source_target_pairs={{0,16},{1,17},{2,18},{3,19},{4,20},{5,21},{6,22},{7,23},{8,24},{9,... | collective-permute-start | bytes 835592 | tf_op jit(solution)/shard_map/ppermute | solution.py:181
  7.4 4.3 %head.1 = (f32[2,256,512]{2,1,0:T(8,128)}, f32[2,4,2,2,64,128]{5,4,3,2,1,0:T(8,128)}) custom-call(s32[2]{0:T(128)} %counts_ref.5, f32[2,4,4,64,512]{4,3,2,1,0:T(8,128)} %refs_1_.1, f32[4,512]{1,0:T(4,128)} %time_ref.3, f32[1,512]{1,0:T(1,128)} %bitcast.133, f32[1,512]{1,0:T(1,128)} %bitcast.131, f32[256,256]{1,0:T(8,128)} %constant.96.clone.table_ref), custom_call_target="tpu_custom_call" | custom-call | flops 805306368 | bytes 6291456 | tf_op jit(solution)/shard_map/head/pallas_call | solution.py:157
  11.8 3.7 %all-to-all-start = ((f32[16,128,128]{2,1,0:T(8,128)}), f32[16,128,128]{2,1,0:T(8,128)S(1)}, u32[]{:S(2)}, u32[]{:S(2)}) async-start(f32[16,128,128]{2,1,0:T(8,128)} %bitcast.103), calls=%async_computation | async-start | bytes 2097152 | tf_op jit(solution)/shard_map/all_to_all | solution.py:390
  15.5 3.7 %collective-permute-done = f32[64,1088]{1,0:T(8,128)S(1)} collective-permute-done((f32[64,1088]{1,0:T(8,128)S(1)}, f32[64,1088]{1,0:T(8,128)S(1)}, u32[]{:S(2)}, u32[]{:S(2)}) %collective-permute-start) | collective-permute-done | bytes 278560 | tf_op jit(solution)/shard_map/ppermute | solution.py:181
  28.6 13.3 %collective-permute-done.1 = f32[64,1024]{1,0:T(8,128)S(1)} collective-permute-done((f32[64,1024]{1,0:T(8,128)S(1)}, f32[64,1024]{1,0:T(8,128)S(1)}, u32[]{:S(2)}, u32[]{:S(2)}) %collective-permute-start.1) | collective-permute-done | bytes 262176 | tf_op jit(solution)/shard_map/ppermute | solution.py:181
  46.5 6.3 %mix.1 = (f32[16,2,8,8,128]{4,3,2,1,0:T(8,128)}, f32[512,256]{1,0:T(8,128)}, f32[512,256]{1,0:T(8,128)}, f32[512,256]{1,0:T(8,128)}) custom-call(f32[16,2,8,8,128]{4,3,2,1,0:T(8,128)S(1)} %bitcast.95, f32[256,256]{1,0:T(8,128)} %get-tuple-element.185.w0_ref, f32[256,256]{1,0:T(8,128)} %get-tuple-element.186.w1_ref, f32[2,1,256]{2,1,0:T(1,128)} %bitcast.136, ...), custom_call_target="tpu_custom_call" | custom-call | flops 1207959552 | bytes 4194304 | tf_op jit(solution)/shard_map/mix/pallas_call | solution.py:157
  57.6 4.7 %all-to-all-start.1 = ((f32[16,128,128]{2,1,0:T(8,128)}), f32[16,128,128]{2,1,0:T(8,128)S(1)}, u32[]{:S(2)}, u32[]{:S(2)}) async-start(f32[16,128,128]{2,1,0:T(8,128)} %bitcast.106), calls=%async_computation.1 | async-start | bytes 2097152 | tf_op jit(solution)/shard_map/all_to_all | solution.py:390
  65.0 4.5 %cotangent_up.2 = (f32[512,512]{1,0:T(8,128)}, f32[512,512]{1,0:T(8,128)}, bf16[512,512]{1,0:T(8,128)(2,1)}, bf16[512,512]{1,0:T(8,128)(2,1)}, bf16[512,512]{1,0:T(8,128)(2,1)}, /*index=5*/bf16[512,512]{1,0:T(8,128)(2,1)}) custom-call(f32[512,512]{1,0:T(8,128)} %bitcast.107, f32[512,512]{1,0:T(8,128)S(1)} %collective-permute-done.9.g2_ref, ...), custom_call_target="tpu_custom_call" | custom-call | flops 1610612736 | bytes 4194304 | tf_op jit(solution)/shard_map/cotangent_up/pallas_call | solution.py:157
  69.6 7.9 %collective-permute-done.10.refs_2_.refs_6_.refs_9_ = f32[128,1024]{1,0:T(8,128)S(1)} collective-permute-done((f32[128,1024]{1,0:T(8,128)S(1)}, f32[128,1024]{1,0:T(8,128)S(1)}, u32[]{:S(2)}, u32[]{:S(2)}) %collective-permute-start.10) | collective-permute-done | bytes 524320 | tf_op jit(solution)/shard_map/ppermute | solution.py:181
  77.5 10.4 %collective-permute-done.11.refs_3_.refs_7_.refs_10_ = f32[128,1024]{1,0:T(8,128)S(1)} collective-permute-done((f32[128,1024]{1,0:T(8,128)}, f32[128,1024]{1,0:T(8,128)S(1)}, u32[]{:S(2)}, u32[]{:S(2)}) %collective-permute-start.11) | collective-permute-done | bytes 524320 | tf_op jit(solution)/shard_map/ppermute | solution.py:181
  88.7 4.4 %cotangent_up.3 = (f32[512,512]{1,0:T(8,128)}, f32[512,512]{1,0:T(8,128)}) custom-call(f32[512,512]{1,0:T(8,128)} %bitcast.108, f32[512,512]{1,0:T(8,128)S(1)} %collective-permute-done.9.g2_ref, f32[128,1024]{1,0:T(8,128)} %copy-done.5, f32[128,1024]{1,0:T(8,128)} %collective-permute-done.7.refs_1_.refs_5_.refs_8_, f32[128,1024]{1,0:T(8,128)} %copy-done.7, ...), custom_call_target="tpu_custom_call" | custom-call | flops 1610612736 | bytes 4194304 | tf_op jit(solution)/shard_map/cotangent_up/pallas_call | solution.py:157
  97.1 8.4 %feed_forward0.1 = (bf16[512,1024]{1,0:T(8,128)(2,1)}, bf16[512,1024]{1,0:T(8,128)(2,1)}, bf16[512,1024]{1,0:T(8,128)(2,1)}, bf16[512,1024]{1,0:T(8,128)(2,1)}, ...) custom-call(f32[2,256,512]{2,1,0:T(8,128)S(1)} %get-tuple-element.106.n_ref, ...), custom_call_target="tpu_custom_call" | custom-call | flops 3221225472 | bytes 9437184 | tf_op jit(solution)/shard_map/feed_forward0/pallas_call | solution.py:157
  105.5 8.5 %feed_forward1.1 = (bf16[512,1024]{1,0:T(8,128)(2,1)}, bf16[512,1024]{1,0:T(8,128)(2,1)}, bf16[512,1024]{1,0:T(8,128)(2,1)}, bf16[512,1024]{1,0:T(8,128)(2,1)}, ...) custom-call(f32[2,256,512]{2,1,0:T(8,128)S(1)} %collective-permute-done.12., ...), custom_call_target="tpu_custom_call" | custom-call | flops 3221225472 | bytes 9437184 | tf_op jit(solution)/shard_map/feed_forward1/pallas_call | solution.py:157
  116.9 3.9 %middle_back.1 = (f32[2,256,512]{2,1,0:T(8,128)}, f32[2,4,2,2,64,128]{5,4,3,2,1,0:T(8,128)}, f32[8,512]{1,0:T(8,128)}) custom-call(f32[2,256,512]{2,1,0:T(8,128)} %get-tuple-element.105.mid_ref.refs_0_, f32[2,256,512]{2,1,0:T(8,128)S(1)} %get-tuple-element.108.g1_ref, f32[2,256,512]{2,1,0:T(8,128)S(1)} %collective-permute-done.13.g2_ref, ...), custom_call_target="tpu_custom_call" | custom-call | flops 402653184 | bytes 6291456 | tf_op jit(solution)/shard_map/middle_back/pallas_call | solution.py:157
  120.8 6.0 %all-to-all-start.2 = ((f32[16,128,128]{2,1,0:T(8,128)}), f32[16,128,128]{2,1,0:T(8,128)S(1)}, u32[]{:S(2)}, u32[]{:S(2)}) async-start(f32[16,128,128]{2,1,0:T(8,128)} %bitcast.105), calls=%async_computation.2 | async-start | bytes 2097152 | tf_op jit(solution)/shard_map/all_to_all | solution.py:390
  128.0 7.4 %weight_grads1.1 = (f32[512,512]{1,0:T(8,128)}, f32[512,512]{1,0:T(8,128)}) custom-call(bf16[512,1024]{1,0:T(8,128)(2,1)} %get-tuple-element.145.refs_0_.refs_1_.hh, bf16[512,1024]{1,0:T(8,128)(2,1)} %get-tuple-element.145.refs_0_.refs_1_.hh, bf16[512,1024]{1,0:T(8,128)(2,1)} %get-tuple-element.116.refs_2_.refs_3_.hl, ...), custom_call_target="tpu_custom_call" | custom-call | flops 3221225472 | bytes 8388608 | tf_op jit(solution)/shard_map/weight_grads1/pallas_call | solution.py:157
  139.0 7.7 %weight_grads0.1 = (f32[2,128,512]{2,1,0:T(8,128)}, f32[2,128,512]{2,1,0:T(8,128)}, f32[2,128,512]{2,1,0:T(8,128)}, f32[2,128,512]{2,1,0:T(8,128)}) custom-call(bf16[512,1024]{1,0:T(8,128)(2,1)} %get-tuple-element.145.refs_0_.refs_1_.hh, bf16[512,1024]{1,0:T(8,128)(2,1)} %get-tuple-element.145.refs_0_.refs_1_.hh, ...), custom_call_target="tpu_custom_call" | custom-call | flops 3221225472 | bytes 8388608 | tf_op jit(solution)/shard_map/weight_grads0/pallas_call | solution.py:157
  149.8 5.6 %mix_back.1 = (f32[16,2,8,8,128]{4,3,2,1,0:T(8,128)}, f32[2,2,2,64,64]{4,3,2,1,0:T(8,128)}, f32[2,1,256]{2,1,0:T(1,128)}) custom-call(f32[16,2,8,8,128]{4,3,2,1,0:T(8,128)S(1)} %bitcast.97, f32[512,256]{1,0:T(8,128)} %get-tuple-element.98.z_ref, f32[512,256]{1,0:T(8,128)} %get-tuple-element.137.u_ref, f32[512,256]{1,0:T(8,128)} %get-tuple-element.138.v_ref, ...), custom_call_target="tpu_custom_call" | custom-call | flops 1207959552 | bytes 4194304 | tf_op jit(solution)/shard_map/mix_back/pallas_call | solution.py:157
  155.4 6.9 %all-to-all-start.3 = ((f32[16,128,128]{2,1,0:T(8,128)}), f32[16,128,128]{2,1,0:T(8,128)S(1)}, u32[]{:S(2)}, u32[]{:S(2)}) async-start(f32[16,128,128]{2,1,0:T(8,128)} %bitcast.104), calls=%async_computation.3 | async-start | bytes 2097152 | tf_op jit(solution)/shard_map/all_to_all | solution.py:390
  163.4 5.0 %contract1.1 = f32[2,256,512]{2,1,0:T(8,128)} custom-call(bf16[512,1024]{1,0:T(8,128)(2,1)} %get-tuple-element.140.refs_10_.refs_11_.hh, bf16[512,1024]{1,0:T(8,128)(2,1)} %get-tuple-element.124.refs_12_.refs_13_.hl, f32[128,1024]{1,0:T(8,128)} %copy-done.4, f32[128,1024]{1,0:T(8,128)} %collective-permute-done.3.refs_1_.refs_4_, ...), custom_call_target="tpu_custom_call" | custom-call | flops 1610612736 | bytes 3145728 | tf_op jit(solution)/shard_map/contract1/pallas_call | solution.py:157
  177.4 5.3 %contract0.1 = f32[2,256,512]{2,1,0:T(8,128)} custom-call(bf16[512,1024]{1,0:T(8,128)(2,1)} %get-tuple-element.145.refs_0_.refs_1_.hh, bf16[512,1024]{1,0:T(8,128)(2,1)} %get-tuple-element.116.refs_2_.refs_3_.hl, f32[2,256,512]{2,1,0:T(8,128)} %get-tuple-element.105.mid_ref.refs_0_, f32[2,256,512]{2,1,0:T(8,128)S(1)} %collective-permute-done.16.refs_1_, ...), custom_call_target="tpu_custom_call" | custom-call | flops 16106127360 | bytes 31457280 | tf_op jit(solution)/shard_map/contract0/pallas_call | solution.py:157
  185.3 4.6 %final.1 = (f32[2,256,512]{2,1,0:T(8,128)}, f32[8,512]{1,0:T(8,128)}) custom-call(s32[2]{0:T(128)} %counts_ref.5, f32[2,4,2,2,64,128]{5,4,3,2,1,0:T(8,128)S(1)} %bitcast.96, f32[2,256,512]{2,1,0:T(8,128)} %get-tuple-element.91.merged_ref, f32[2,256,512]{2,1,0:T(8,128)} %get-tuple-element.148.refs_0_, f32[2,4,4,64,512]{4,3,2,1,0:T(8,128)} %refs_1_.1, ...), custom_call_target="tpu_custom_call" | custom-call | flops 4026531840 | bytes 83886080 | tf_op jit(solution)/shard_map/final/pallas_call | solution.py:157
  209.7 3.4 %collective-permute-done.23.refs_3_ = f32[17,512]{1,0:T(8,128)S(1)} collective-permute-done((f32[17,512]{1,0:T(8,128)S(1)}, f32[17,512]{1,0:T(8,128)S(1)}, u32[]{:S(2)}, u32[]{:S(2)}) %collective-permute-start.23) | collective-permute-done | bytes 34848 | tf_op jit(solution)/shard_map/ppermute | solution.py:185
  220.7 9.6 %collective-permute-done.27 = f32[68,1024]{1,0:T(8,128)S(1)} collective-permute-done((f32[68,1024]{1,0:T(8,128)S(1)}, f32[68,1024]{1,0:T(8,128)S(1)}, u32[]{:S(2)}, u32[]{:S(2)}) %collective-permute-start.27) | collective-permute-done | bytes 278560 | tf_op jit(solution)/shard_map/ppermute | solution.py:181
  (184 shorter events, 80.6 us)
Async XLA Ops:
  1.7 17.5 %collective-permute-start = (f32[64,1088]{1,0:T(8,128)S(1)}, f32[64,1088]{1,0:T(8,128)S(1)}, u32[]{:S(2)}, u32[]{:S(2)}) collective-permute-start(f32[64,1088]{1,0:T(8,128)S(1)} %pad_maximum_fusion.4), channel_id=1, source_target_pairs={{0,16},{1,17},{2,18},{3,19},{4,20},{5,21},{6,22},{7,23},{8,24},{9,... | collective-permute-start | bytes 835592 | tf_op jit(solution)/shard_map/ppermute | solution.py:181
  5.8 17.3 %collective-permute-start.2 = (f32[64,1088]{1,0:T(8,128)S(1)}, f32[64,1088]{1,0:T(8,128)S(1)}, u32[]{:S(2)}, u32[]{:S(2)}) collective-permute-start(f32[64,1088]{1,0:T(8,128)S(1)} %pad_maximum_fusion.4), channel_id=1, source_target_pairs={{0,8},{1,9},{2,10},{3,11},{4,12},{5,13},{6,14},{7,15},{8,0},{9,1},... | collective-permute-start | bytes 835592 | tf_op jit(solution)/shard_map/ppermute | solution.py:181
  11.8 34.7 %all-to-all-start = ((f32[16,128,128]{2,1,0:T(8,128)}), f32[16,128,128]{2,1,0:T(8,128)S(1)}, u32[]{:S(2)}, u32[]{:S(2)}) async-start(f32[16,128,128]{2,1,0:T(8,128)} %bitcast.103), calls=%async_computation | async-start | bytes 2097152 | tf_op jit(solution)/shard_map/all_to_all | solution.py:390
  25.0 21.5 %collective-permute-start.4 = (f32[128,1024]{1,0:T(8,128)S(1)}, f32[128,1024]{1,0:T(8,128)}, u32[]{:S(2)}, u32[]{:S(2)}) collective-permute-start(f32[128,1024]{1,0:T(8,128)S(1)} %pad_maximum_fusion.3.refs_0_.refs_3_), channel_id=1, source_target_pairs={{0,1},{1,0},{2,3},{3,2},{4,5},{5,4},{6,7},{7,6},{8,9},{9,8},{10,11... | collective-permute-start | bytes 1572872 | tf_op jit(solution)/shard_map/ppermute | solution.py:181
  25.5 18.2 %collective-permute-start.3 = (f32[128,1024]{1,0:T(8,128)S(1)}, f32[128,1024]{1,0:T(8,128)}, u32[]{:S(2)}, u32[]{:S(2)}) collective-permute-start(f32[128,1024]{1,0:T(8,128)S(1)} %pad_maximum_fusion.3.refs_0_.refs_3_), channel_id=1, source_target_pairs={{0,4},{1,5},{2,6},{3,7},{4,0},{5,1},{6,2},{7,3},{8,12},{9,13},{10,... | collective-permute-start | bytes 1572872 | tf_op jit(solution)/shard_map/ppermute | solution.py:181
  25.7 16.3 %collective-permute-start.1 = (f32[64,1024]{1,0:T(8,128)S(1)}, f32[64,1024]{1,0:T(8,128)S(1)}, u32[]{:S(2)}, u32[]{:S(2)}) collective-permute-start(f32[64,1024]{1,0:T(8,128)S(1)} %slice.142), channel_id=1, source_target_pairs={{0,8},{1,9},{2,10},{3,11},{4,12},{5,13},{6,14},{7,15},{8,0},{9,1},... | collective-permute-start | bytes 786440 | tf_op jit(solution)/shard_map/ppermute | solution.py:181
  42.0 14.1 %collective-permute-start.7 = (f32[128,1024]{1,0:T(8,128)S(1)}, f32[128,1024]{1,0:T(8,128)}, u32[]{:S(2)}, u32[]{:S(2)}) collective-permute-start(f32[128,1024]{1,0:T(8,128)S(1)} %pad_maximum_fusion.2.refs_0_.refs_4_.refs_7_), channel_id=1, source_target_pairs={{0,4},{1,5},{2,6},{3,7},{4,0},{5,1},{6,2},{7,3},{8,12},{9,13},{10,... | collective-permute-start | bytes 1572872 | tf_op jit(solution)/shard_map/ppermute | solution.py:181
  43.7 13.9 %collective-permute-start.8 = (f32[128,1024]{1,0:T(8,128)}, f32[128,1024]{1,0:T(8,128)}, u32[]{:S(2)}, u32[]{:S(2)}) collective-permute-start(f32[128,1024]{1,0:T(8,128)} %collective-permute-done.3.refs_1_.refs_4_), channel_id=1, source_target_pairs={{0,1},{1,0},{2,3},{3,2},{4,5},{5,4},{6,7},{7,6},{8,9},{9,8},{10,11... | collective-permute-start | bytes 1572872 | tf_op jit(solution)/shard_map/ppermute | solution.py:181
  57.6 35.5 %all-to-all-start.1 = ((f32[16,128,128]{2,1,0:T(8,128)}), f32[16,128,128]{2,1,0:T(8,128)S(1)}, u32[]{:S(2)}, u32[]{:S(2)}) async-start(f32[16,128,128]{2,1,0:T(8,128)} %bitcast.106), calls=%async_computation.1 | async-start | bytes 2097152 | tf_op jit(solution)/shard_map/all_to_all | solution.py:390
  62.8 14.8 %collective-permute-start.10 = (f32[128,1024]{1,0:T(8,128)S(1)}, f32[128,1024]{1,0:T(8,128)S(1)}, u32[]{:S(2)}, u32[]{:S(2)}) collective-permute-start(f32[128,1024]{1,0:T(8,128)S(1)} %pad_maximum_fusion.2.refs_0_.refs_4_.refs_7_), channel_id=1, source_target_pairs={{0,1},{1,0},{2,3},{3,2},{4,5},{5,4},{6,7},{7,6},{8,9},{9,8},{10,11... | collective-permute-start | bytes 1572872 | tf_op jit(solution)/shard_map/ppermute | solution.py:181
  64.3 23.7 %collective-permute-start.11 = (f32[128,1024]{1,0:T(8,128)}, f32[128,1024]{1,0:T(8,128)S(1)}, u32[]{:S(2)}, u32[]{:S(2)}) collective-permute-start(f32[128,1024]{1,0:T(8,128)} %collective-permute-done.7.refs_1_.refs_5_.refs_8_), channel_id=1, source_target_pairs={{0,1},{1,0},{2,3},{3,2},{4,5},{5,4},{6,7},{7,6},{8,9},{9,8},{10,11... | collective-permute-start | bytes 1572872 | tf_op jit(solution)/shard_map/ppermute | solution.py:181
  96.1 9.4 %collective-permute-start.12 = (f32[2,256,512]{2,1,0:T(8,128)S(1)}, f32[2,256,512]{2,1,0:T(8,128)S(1)}, u32[]{:S(2)}, u32[]{:S(2)}) collective-permute-start(f32[2,256,512]{2,1,0:T(8,128)S(1)} %get-tuple-element.106.n_ref), channel_id=1, source_target_pairs={{0,2},{1,3},{2,0},{3,1},{4,6},{5,7},{6,4},{7,5},{8,10},{9,11},{10,... | collective-permute-start | bytes 3145736 | tf_op jit(solution)/shard_map/ppermute | solution.py:181
  120.8 29.0 %all-to-all-start.2 = ((f32[16,128,128]{2,1,0:T(8,128)}), f32[16,128,128]{2,1,0:T(8,128)S(1)}, u32[]{:S(2)}, u32[]{:S(2)}) async-start(f32[16,128,128]{2,1,0:T(8,128)} %bitcast.105), calls=%async_computation.2 | async-start | bytes 2097152 | tf_op jit(solution)/shard_map/all_to_all | solution.py:390
  135.5 33.5 %collective-permute-start.14 = (f32[512,512]{1,0:T(8,128)}, f32[512,512]{1,0:T(8,128)}, u32[]{:S(2)}, u32[]{:S(2)}) collective-permute-start(f32[512,512]{1,0:T(8,128)} %get-tuple-element.131), channel_id=1, source_target_pairs={{0,4},{1,5},{2,6},{3,7},{4,0},{5,1},{6,2},{7,3},{8,12},{9,13},{10,... | collective-permute-start | bytes 3145736 | tf_op jit(solution)/shard_map/ppermute | solution.py:181
  137.4 31.5 %collective-permute-start.15 = (f32[512,512]{1,0:T(8,128)}, f32[512,512]{1,0:T(8,128)S(1)}, u32[]{:S(2)}, u32[]{:S(2)}) collective-permute-start(f32[512,512]{1,0:T(8,128)} %get-tuple-element.143), channel_id=1, source_target_pairs={{0,1},{1,0},{2,3},{3,2},{4,5},{5,4},{6,7},{7,6},{8,9},{9,8},{10,11... | collective-permute-start | bytes 3145736 | tf_op jit(solution)/shard_map/ppermute | solution.py:181
  155.4 29.9 %all-to-all-start.3 = ((f32[16,128,128]{2,1,0:T(8,128)}), f32[16,128,128]{2,1,0:T(8,128)S(1)}, u32[]{:S(2)}, u32[]{:S(2)}) async-start(f32[16,128,128]{2,1,0:T(8,128)} %bitcast.104), calls=%async_computation.3 | async-start | bytes 2097152 | tf_op jit(solution)/shard_map/all_to_all | solution.py:390
  172.3 26.9 %collective-permute-start.26 = (f32[2,128,512]{2,1,0:T(8,128)}, f32[2,128,512]{2,1,0:T(8,128)}, u32[]{:S(2)}, u32[]{:S(2)}) collective-permute-start(f32[2,128,512]{2,1,0:T(8,128)} %get-tuple-element.159), channel_id=1, source_target_pairs={{0,4},{1,5},{2,6},{3,7},{4,0},{5,1},{6,2},{7,3},{8,12},{9,13},{10,... | collective-permute-start | bytes 1572872 | tf_op jit(solution)/shard_map/ppermute | solution.py:181
  175.9 21.4 %collective-permute-start.24 = (f32[288,512]{1,0:T(8,128)}, f32[288,512]{1,0:T(8,128)}, u32[]{:S(2)}, u32[]{:S(2)}) collective-permute-start(f32[288,512]{1,0:T(8,128)} %pad_maximum_fusion.1), channel_id=1, source_target_pairs={{0,1},{1,0},{2,3},{3,2},{4,5},{5,4},{6,7},{7,6},{8,9},{9,8},{10,11... | collective-permute-start | bytes 1769480 | tf_op jit(solution)/shard_map/ppermute | solution.py:181
  190.7 15.9 %collective-permute-start.18 = (f32[17,512]{1,0:T(8,128)S(1)}, f32[17,512]{1,0:T(8,128)S(1)}, u32[]{:S(2)}, u32[]{:S(2)}) collective-permute-start(f32[17,512]{1,0:T(8,128)S(1)} %pad_maximum_fusion.8), channel_id=1, source_target_pairs={{0,8},{1,9},{2,10},{3,11},{4,12},{5,13},{6,14},{7,15},{8,0},{9,1},... | collective-permute-start | bytes 104456 | tf_op jit(solution)/shard_map/ppermute | solution.py:185
  194.0 12.6 %collective-permute-start.19 = (f32[17,512]{1,0:T(8,128)S(1)}, f32[17,512]{1,0:T(8,128)S(1)}, u32[]{:S(2)}, u32[]{:S(2)}) collective-permute-start(f32[17,512]{1,0:T(8,128)S(1)} %pad_maximum_fusion.8), channel_id=1, source_target_pairs={{0,24},{1,25},{2,26},{3,27},{4,28},{5,29},{6,30},{7,31},{8,16},{9,... | collective-permute-start | bytes 104456 | tf_op jit(solution)/shard_map/ppermute | solution.py:185
  197.3 9.3 %collective-permute-start.17 = (f32[17,512]{1,0:T(8,128)S(1)}, f32[17,512]{1,0:T(8,128)S(1)}, u32[]{:S(2)}, u32[]{:S(2)}) collective-permute-start(f32[17,512]{1,0:T(8,128)S(1)} %pad_maximum_fusion.8), channel_id=1, source_target_pairs={{0,16},{1,17},{2,18},{3,19},{4,20},{5,21},{6,22},{7,23},{8,24},{9,... | collective-permute-start | bytes 104456 | tf_op jit(solution)/shard_map/ppermute | solution.py:185
  202.0 18.6 %collective-permute-start.28 = (f32[64,1024]{1,0:T(8,128)S(1)}, f32[64,1024]{1,0:T(8,128)S(1)}, u32[]{:S(2)}, u32[]{:S(2)}) collective-permute-start(f32[64,1024]{1,0:T(8,128)S(1)} %get-tuple-element.166), channel_id=1, source_target_pairs={{0,8},{1,9},{2,10},{3,11},{4,12},{5,13},{6,14},{7,15},{8,0},{9,1},... | collective-permute-start | bytes 786440 | tf_op jit(solution)/shard_map/ppermute | solution.py:181
  203.2 17.5 %collective-permute-start.29 = (f32[64,1024]{1,0:T(8,128)S(1)}, f32[64,1024]{1,0:T(8,128)S(1)}, u32[]{:S(2)}, u32[]{:S(2)}) collective-permute-start(f32[64,1024]{1,0:T(8,128)S(1)} %get-tuple-element.167), channel_id=1, source_target_pairs={{0,24},{1,25},{2,26},{3,27},{4,28},{5,29},{6,30},{7,31},{8,16},{9,... | collective-permute-start | bytes 786440 | tf_op jit(solution)/shard_map/ppermute | solution.py:185
  206.5 23.8 %collective-permute-start.27 = (f32[68,1024]{1,0:T(8,128)S(1)}, f32[68,1024]{1,0:T(8,128)S(1)}, u32[]{:S(2)}, u32[]{:S(2)}) collective-permute-start(f32[68,1024]{1,0:T(8,128)S(1)} %pad_maximum_fusion.5), channel_id=1, source_target_pairs={{0,16},{1,17},{2,18},{3,19},{4,20},{5,21},{6,22},{7,23},{8,24},{9,... | collective-permute-start | bytes 835592 | tf_op jit(solution)/shard_map/ppermute | solution.py:181
  (34 other events, 381.0 us)
